TPU v7x, 256 devices: a whole 4x4x8 slice. The times are simulated.
256 devices in a mesh: seq: 32 (over x, y, z_lo), dp: 8 (over z_hi, core).
Axes of the slice: x: 4, y: 4, z: 8 (z_hi: 4, z_lo: 2; z = z_hi * 2 + z_lo), core: 2. Of those that a mesh axis runs over, the one named last changes fastest.
Arguments:
- queries: bfloat16 [16, 2048, 4096], P('dp', 'seq'), may hold values from -300 to 300
- key_states: bfloat16 [16, 2048, 4096], P('dp', 'seq'), may hold values from -4.5 to 4.5
- value_states: bfloat16 [16, 2048, 4096], P('dp', 'seq'), may hold values from -6 to 6
- grad_output: bfloat16 [16, 2048, 4096], P('dp', 'seq'), may hold values from -6 to 6
- query_bias: bfloat16 [4096], P(('seq', 'dp')), may hold values from -5 to 5
Outputs:
- grad_queries: bfloat16 [16, 2048, 4096], P('dp', 'seq')
- grad_keys: bfloat16 [16, 2048, 4096], P('dp', 'seq')
- grad_values: bfloat16 [16, 2048, 4096], P('dp', 'seq')
- grad_bias: float32 [4096], P(('seq', 'dp'))
All inputs are finite; a program needn't handle non-finite values.
Results may differ from a plain program's by a relative error of at most 0.007.
Values may be sent and summed in bfloat16 or wider, within the bound.
No kernel may reach another device: no remote copies, remote signals or barrier semaphores. Data moves between devices by JAX's collectives and lax.ppermute only.
A program may use at most 128 MiB of HBM per device.

v0:
```python
import math

import jax
import jax.numpy as jnp
from jax import lax
from jax.sharding import PartitionSpec as P

HDIM = 128
QBLOCKS = 4


masked_value = -1e30


def attend(query_full, key_rows, value_rows, grad_rows):
    item_count, seq_length, total_cols = query_full.shape
    head_count = total_cols // HDIM

    def heads_view(values):
        return values.reshape(item_count, seq_length, head_count, HDIM)

    query_heads = heads_view(query_full)
    key_heads = heads_view(key_rows)
    value_heads = heads_view(value_rows)
    grad_heads = heads_view(grad_rows)
    factor = 1.0 / math.sqrt(HDIM)
    block_rows = seq_length // QBLOCKS
    grad_keys = jnp.zeros((item_count, seq_length, head_count, HDIM), jnp.float32)
    grad_values = jnp.zeros((item_count, seq_length, head_count, HDIM), jnp.float32)
    query_parts = []
    for block_idx in range(QBLOCKS):
        row_start = block_idx * block_rows
        key_end = row_start + block_rows
        block_query = query_heads[:, row_start:key_end]
        seen_keys = key_heads[:, :key_end]
        seen_values = value_heads[:, :key_end]
        block_grad = grad_heads[:, row_start:key_end]
        scores = (
            jnp.einsum(
                "nqhd,nkhd->nhqk", block_query, seen_keys, preferred_element_type=jnp.float32
            )
            * factor
        )
        row_ids = row_start + jnp.arange(block_rows)[:, None]
        key_ids = jnp.arange(key_end)[None, :]
        scores = jnp.where(key_ids <= row_ids, scores, masked_value)
        highest = jnp.max(scores, axis=-1, keepdims=True)
        shifted = jnp.exp(scores - highest)
        weights = shifted / jnp.sum(shifted, axis=-1, keepdims=True)
        grad_probs = jnp.einsum(
            "nqhd,nkhd->nhqk", block_grad, seen_values, preferred_element_type=jnp.float32
        )
        row_dot = jnp.sum(weights * grad_probs, axis=-1, keepdims=True)
        grad_scores = (weights * (grad_probs - row_dot) * factor).astype(jnp.bfloat16)
        weights_low = weights.astype(jnp.bfloat16)
        grad_values = grad_values.at[:, :key_end].add(
            jnp.einsum(
                "nhqk,nqhd->nkhd", weights_low, block_grad, preferred_element_type=jnp.float32
            )
        )
        grad_keys = grad_keys.at[:, :key_end].add(
            jnp.einsum(
                "nhqk,nqhd->nkhd", grad_scores, block_query, preferred_element_type=jnp.float32
            )
        )
        query_parts.append(
            jnp.einsum(
                "nhqk,nkhd->nqhd", grad_scores, seen_keys, preferred_element_type=jnp.float32
            )
        )
    grad_queries = jnp.concatenate(query_parts, axis=1)
    shape_out = (item_count, seq_length, total_cols)
    return (
        grad_queries.reshape(shape_out),
        grad_keys.reshape(shape_out),
        grad_values.reshape(shape_out),
    )


def head_gradients(pieces, bias_cols):
    query_rows, key_rows, value_rows, grad_rows = pieces
    query_full = (
        query_rows.astype(jnp.float32) + bias_cols.astype(jnp.float32)[None, None, :]
    ).astype(jnp.bfloat16)
    grad_q, grad_k, grad_v = attend(query_full, key_rows, value_rows, grad_rows)
    column_sums = jnp.sum(grad_q, axis=1)
    return (
        grad_q.astype(jnp.bfloat16),
        grad_k.astype(jnp.bfloat16),
        grad_v.astype(jnp.bfloat16),
        column_sums,
    )


def body(queries, key_states, value_states, grad_output, query_bias):
    bias_cols = lax.all_gather(query_bias, "dp", axis=0, tiled=True)
    regrouped = (
        lax.all_to_all(queries, "seq", split_axis=2, concat_axis=1, tiled=True),
        lax.all_to_all(key_states, "seq", split_axis=2, concat_axis=1, tiled=True),
        lax.all_to_all(value_states, "seq", split_axis=2, concat_axis=1, tiled=True),
        lax.all_to_all(grad_output, "seq", split_axis=2, concat_axis=1, tiled=True),
    )
    grad_q, grad_k, grad_v, column_sums = head_gradients(regrouped, bias_cols)
    returned = (
        lax.all_to_all(grad_q, "seq", split_axis=1, concat_axis=2, tiled=True),
        lax.all_to_all(grad_k, "seq", split_axis=1, concat_axis=2, tiled=True),
        lax.all_to_all(grad_v, "seq", split_axis=1, concat_axis=2, tiled=True),
    )
    grad_queries, grad_keys, grad_values = returned
    bias_total = jnp.sum(column_sums, axis=0)
    grad_bias = lax.psum_scatter(bias_total, "dp", scatter_dimension=0, tiled=True)
    return (grad_queries, grad_keys, grad_values, grad_bias)


def solution(mesh):
    in_specs = (
        P("dp", "seq", None),
        P("dp", "seq", None),
        P("dp", "seq", None),
        P("dp", "seq", None),
        P(("seq", "dp")),
    )
    out_specs = (P("dp", "seq", None), P("dp", "seq", None), P("dp", "seq", None), P(("seq", "dp")))
    return jax.shard_map(body, mesh=mesh, in_specs=in_specs, out_specs=out_specs, check_vma=False)
```

profile of v0, /device:TPU:32, one launch (start us, length us, event | category | flops | bytes accessed | tf_op | source)
XLA Modules:
  0.0 370.2 jit_solution(15202894478364725666)
XLA Ops:
  7.9 8.5 %all-to-all-start = ((bf16[32,2,8192]{2,1,0:T(2,128)(2,1)}), bf16[32,2,8192]{2,1,0:T(2,128)(2,1)S(1)}, u32[]{:S(2)}, u32[]{:S(2)}) async-start(bf16[32,2,8192]{2,1,0:T(2,128)(2,1)} %reshape.615), calls=%async_computation | async-start | bytes 2097152 | tf_op jit(solution)/shard_map/all_to_all | solution.py:98
  23.8 9.5 %all-to-all-done = bf16[32,2,8192]{2,1,0:T(2,128)(2,1)S(1)} async-done(((bf16[32,2,8192]{2,1,0:T(2,128)(2,1)}), bf16[32,2,8192]{2,1,0:T(2,128)(2,1)S(1)}, u32[]{:S(2)}, u32[]{:S(2)}) %all-to-all-start) | async-done | bytes 1048608 | tf_op jit(solution)/shard_map/all_to_all | solution.py:98
  46.2 8.2 %all-to-all-done.1 = bf16[32,2,8192]{2,1,0:T(2,128)(2,1)} async-done(((bf16[32,2,8192]{2,1,0:T(2,128)(2,1)}), bf16[32,2,8192]{2,1,0:T(2,128)(2,1)}, u32[]{:S(2)}, u32[]{:S(2)}) %all-to-all-start.1) | async-done | bytes 1048608 | tf_op jit(solution)/shard_map/all_to_all | solution.py:99
  54.4 5.8 %all-to-all-start.3 = ((bf16[32,2,8192]{2,1,0:T(2,128)(2,1)}), bf16[32,2,8192]{2,1,0:T(2,128)(2,1)}, u32[]{:S(2)}, u32[]{:S(2)}) async-start(bf16[32,2,8192]{2,1,0:T(2,128)(2,1)} %reshape.611), calls=%async_computation.3 | async-start | bytes 2097152 | tf_op jit(solution)/shard_map/all_to_all | solution.py:100
  61.7 19.5 %all-reduce.2 = bf16[128]{0:T(256)(128)(2,1)S(1)} all-reduce(bf16[128]{0:T(256)(128)(2,1)S(1)} %dynamic-update-slice.22), channel_id=1, replica_groups=mesh['seq'=32,'dp'=8] {'dp'}, use_global_device_ids=true, to_apply=%add.2 | all-reduce | flops 128 | bytes 512
  89.8 8.9 %all-to-all-start.2 = ((bf16[32,2,8192]{2,1,0:T(2,128)(2,1)}), bf16[32,2,8192]{2,1,0:T(2,128)(2,1)}, u32[]{:S(2)}, u32[]{:S(2)}) async-start(bf16[32,2,8192]{2,1,0:T(2,128)(2,1)} %reshape.613), calls=%async_computation.2 | async-start | bytes 2097152 | tf_op jit(solution)/shard_map/all_to_all | solution.py:101
  155.4 6.0 %fusion.177 = (f32[2,512]{1,0:T(2,128)S(1)}, f32[2,512,1536]{2,1,0:T(8,128)}) fusion(pred[512,1536]{1,0:T(8,128)(4,1)S(1)} %copy-done.6, bf16[2,2048,1,128]{3,1,0,2:T(8,128)(2,1)S(1)} %bitcast.278, bf16[2,2048,1,128]{3,1,0,2:T(8,128)(2,1)} %copy-done.5), kind=kOutput, calls=%fused_computation.159 | convolution fusion | flops 408946176 | bytes 8130560 | tf_op jit(solution)/shard_map/sub | solution.py:48
  161.4 5.7 %fusion.178 = (f32[2,512]{1,0:T(2,128)S(1)}, f32[2,512,1024]{2,1,0:T(8,128)S(1)}) fusion(f32[2,512,1024]{2,1,0:T(8,128)} %fusion.142, pred[512,1024]{1,0:T(8,128)(4,1)} %iota_compare_fusion.2), kind=kOutput, calls=%fused_computation.160 | output fusion | flops 6292479 | bytes 8916992 | tf_op jit(solution)/shard_map/sub | solution.py:48
  171.2 6.6 %fusion.57 = f32[2,2048,1,128]{3,1,0,2:T(8,128)} fusion(f32[2,2048,1,128]{3,1,0,2:T(8,128)} %fusion.123, bf16[2,2048,1,128]{3,1,0,2:T(8,128)(2,1)S(1)} %bitcast.268, f32[2,512]{1,0:T(2,128)S(1)} %get-tuple-element.128, pred[512,1536]{1,0:T(8,128)(4,1)} %iota_compare_fusion.1, bf16[2,2048,1,128]{3,1,0,2:T(8,128)(2,1)S(1)} %bitcast.279, ...), kind=kOutput, calls=%fused_computation.49 | convolution fusion | flops 813566464 | bytes 5246976 | tf_op jit(solution)/shard_map/nhqk,nqhd->nkhd/dot_general | solution.py:57
  177.8 7.9 %fusion.176 = (f32[2,512]{1,0:T(2,128)S(1)}, f32[2,512,2048]{2,1,0:T(8,128)}) fusion(pred[512,2048]{1,0:T(8,128)(4,1)} %iota_compare_fusion, bf16[2,2048,128]{2,1,0:T(8,128)(2,1)S(1)} %bitcast.280, bf16[2,2048,1,128]{3,1,0,2:T(8,128)(2,1)} %copy-done.5), kind=kOutput, calls=%fused_computation.158 | convolution fusion | flops 545261568 | bytes 10752000 | tf_op jit(solution)/shard_map/sub | solution.py:48
  185.7 5.8 %fusion.87 = bf16[2,2048,128]{2,1,0:T(8,128)(2,1)S(1)} fusion(f32[2,2048,1,128]{3,1,0,2:T(8,128)} %fusion.57, bf16[2,2048,1,128]{3,1,0,2:T(8,128)(2,1)S(1)} %bitcast.269, f32[2,512,2048]{2,1,0:T(8,128)} %get-tuple-element.127, f32[2,512]{1,0:T(2,128)S(1)} %get-tuple-element.126), kind=kOutput, calls=%fused_computation.59 | convolution fusion | flops 542113792 | bytes 11800576 | tf_op jit(solution)/shard_map/nhqk,nqhd->nkhd/dot_general | solution.py:57
  191.4 9.5 %copy.80 = bf16[2,2048,128]{2,0,1:T(2,128)(2,1)} copy(bf16[2,2048,128]{2,1,0:T(8,128)(2,1)S(1)} %fusion.87) | data formatting | bytes 2097152 | tf_op jit(solution)/shard_map/convert_element_type | solution.py:90
  200.9 8.6 %all-to-all-start.6 = ((bf16[2,2048,128]{2,0,1:T(2,128)(2,1)}), bf16[2,2048,128]{2,0,1:T(2,128)(2,1)S(1)}, u32[]{:S(2)}, u32[]{:S(2)}) async-start(bf16[2,2048,128]{2,0,1:T(2,128)(2,1)} %copy.80), calls=%async_computation.6 | async-start | bytes 2097152 | tf_op jit(solution)/shard_map/all_to_all | solution.py:107
  212.2 13.1 %fusion.117 = f32[2,2048,1,128]{1,3,0,2:T(8,128)} fusion(f32[2,2048,1,128]{1,3,0,2:T(8,128)} %scatter-add.20, f32[2,512,1024]{2,1,0:T(8,128)} %fusion.141, bf16[2,2048,1,128]{3,1,0,2:T(8,128)(2,1)} %copy-done.5, f32[2,512,1024]{2,1,0:T(8,128)} %copy-done.9, f32[2,512]{1,0:T(2,128)S(1)} %get-tuple-element.130), kind=kOutput, calls=%fused_computation.82 | convolution fusion | flops 276039680 | bytes 19144704 | tf_op jit(solution)/shard_map/nhqk,nqhd->nkhd/dot_general | solution.py:62
  229.0 15.9 %fusion.63 = f32[2,2048,1,128]{1,3,0,2:T(8,128)} fusion(f32[2,2048,1,128]{1,3,0,2:T(8,128)} %fusion.117, f32[2,512,1536]{2,1,0:T(8,128)} %fusion.139, bf16[2,2048,1,128]{3,1,0,2:T(8,128)(2,1)} %copy-done.5, f32[2,512,1536]{2,1,0:T(8,128)} %get-tuple-element.129, f32[2,512]{1,0:T(2,128)S(1)} %get-tuple-element.128), kind=kOutput, calls=%fused_computation.51 | convolution fusion | flops 414059008 | bytes 28581888 | tf_op jit(solution)/shard_map/nhqk,nqhd->nkhd/dot_general | solution.py:62
  249.3 17.6 %fusion.84 = bf16[2,2048,128]{1,2,0:T(8,128)(2,1)S(1)} fusion(f32[2,2048,1,128]{1,3,0,2:T(8,128)} %fusion.63, f32[2,512,2048]{2,1,0:T(8,128)} %fusion.145, bf16[2,2048,1,128]{3,1,0,2:T(8,128)(2,1)} %copy-done.5, f32[2,512,2048]{2,1,0:T(8,128)} %get-tuple-element.127, f32[2,512]{1,0:T(2,128)S(1)} %get-tuple-element.126), kind=kOutput, calls=%fused_computation.58 | convolution fusion | flops 552602624 | bytes 36970496 | tf_op jit(solution)/shard_map/nhqk,nqhd->nkhd/dot_general | solution.py:62
  268.9 8.7 %all-to-all-start.5 = ((bf16[2,2048,128]{2,0,1:T(2,128)(2,1)}), bf16[2,2048,128]{2,0,1:T(2,128)(2,1)S(1)}, u32[]{:S(2)}, u32[]{:S(2)}) async-start(bf16[2,2048,128]{2,0,1:T(2,128)(2,1)} %copy.74), calls=%async_computation.5 | async-start | bytes 2097152 | tf_op jit(solution)/shard_map/all_to_all | solution.py:106
  277.6 11.8 %fusion.82 = f32[2,512,128]{2,1,0:T(8,128)} fusion(f32[2,512,1024]{2,1,0:T(8,128)} %fusion.141, bf16[2,2048,1,128]{3,1,0,2:T(8,128)(2,1)S(1)} %bitcast.281, f32[2,512,1024]{2,1,0:T(8,128)} %copy-done.9, f32[2,512]{1,0:T(2,128)S(1)} %get-tuple-element.130), kind=kOutput, calls=%fused_computation.57 | convolution fusion | flops 275777536 | bytes 17833984 | tf_op jit(solution)/shard_map/nhqk,nkhd->nqhd/dot_general | solution.py:67
  289.4 5.6 %fusion.171 = (f32[128]{0:T(128)S(1)}, bf16[2,512,1,128]{3,1,0,2:T(8,128)(2,1)S(1)}, bf16[2,512,1,128]{3,1,0,2:T(8,128)(2,1)}, f32[128]{0:T(128)S(1)}) fusion(f32[2,512,128]{2,1,0:T(8,128)} %fusion.82, bf16[2,2048,1,128]{3,1,0,2:T(8,128)(2,1)S(1)} %bitcast.282, f32[2,512,512]{1,2,0:T(8,128)} %copy-done.4, f32[2,512,512]{1,2,0:T(8,128)} %get-tuple-element.133, ...), kind=kOutput, calls=%fused_computation.153 | convolution fusion | flops 138413312 | bytes 9708544 | tf_op jit(solution)/shard_map/nhqk,nkhd->nqhd/dot_general | solution.py:67
  295.0 13.2 %fusion.173 = (f32[128]{0:T(128)S(1)}, bf16[2,512,1,128]{3,1,0,2:T(8,128)(2,1)}) fusion(bf16[2,2048,1,128]{3,1,0,2:T(8,128)(2,1)S(1)} %bitcast.283, f32[2,512,1536]{2,1,0:T(8,128)} %fusion.139, f32[2,512,1536]{2,1,0:T(8,128)} %get-tuple-element.129, f32[2,512]{1,0:T(2,128)S(1)} %get-tuple-element.128), kind=kOutput, calls=%fused_computation.155 | convolution fusion | flops 413927808 | bytes 26223104 | tf_op jit(solution)/shard_map/nhqk,nkhd->nqhd/dot_general | solution.py:67
  308.2 15.2 %fusion.174 = (f32[128]{0:T(128)S(1)}, bf16[2,512,1,128]{3,1,0,2:T(8,128)(2,1)}) fusion(bf16[2,2048,128]{2,1,0:T(8,128)(2,1)S(1)} %bitcast.284, f32[2,512,2048]{2,1,0:T(8,128)} %fusion.145, f32[2,512,2048]{2,1,0:T(8,128)} %get-tuple-element.127, f32[2,512]{1,0:T(2,128)S(1)} %get-tuple-element.126), kind=kOutput, calls=%fused_computation.156 | convolution fusion | flops 551816064 | bytes 18092544 | tf_op jit(solution)/shard_map/nhqk,nkhd->nqhd/dot_general | solution.py:67
  324.6 9.5 %copy.67 = bf16[2,2048,128]{2,0,1:T(2,128)(2,1)} copy(bf16[2,2048,128]{2,1,0:T(8,128)(2,1)S(1)} %maximum_bitcast_fusion) | data formatting | bytes 2097152 | tf_op jit(solution)/shard_map/convert_element_type | solution.py:88
  334.0 8.3 %all-to-all-start.4 = ((bf16[2,2048,128]{2,0,1:T(2,128)(2,1)}), bf16[2,2048,128]{2,0,1:T(2,128)(2,1)S(1)}, u32[]{:S(2)}, u32[]{:S(2)}) async-start(bf16[2,2048,128]{2,0,1:T(2,128)(2,1)} %copy.67), calls=%async_computation.4 | async-start | bytes 2097152 | tf_op jit(solution)/shard_map/all_to_all | solution.py:105
  343.0 18.9 %all-reduce.3 = f32[128]{0:T(128)S(1)} all-reduce(f32[128]{0:T(128)S(1)} %add_add_fusion), channel_id=2, replica_groups=mesh['seq'=32,'dp'=8] {'dp'}, use_global_device_ids=true, to_apply=%region_16.17.clone | all-reduce | flops 128 | bytes 1024
  (75 shorter events, 119.5 us)
Async XLA Ops:
  7.9 25.4 %all-to-all-start = ((bf16[32,2,8192]{2,1,0:T(2,128)(2,1)}), bf16[32,2,8192]{2,1,0:T(2,128)(2,1)S(1)}, u32[]{:S(2)}, u32[]{:S(2)}) async-start(bf16[32,2,8192]{2,1,0:T(2,128)(2,1)} %reshape.615), calls=%async_computation | async-start | bytes 2097152 | tf_op jit(solution)/shard_map/all_to_all | solution.py:98
  33.3 21.0 %all-to-all-start.1 = ((bf16[32,2,8192]{2,1,0:T(2,128)(2,1)}), bf16[32,2,8192]{2,1,0:T(2,128)(2,1)}, u32[]{:S(2)}, u32[]{:S(2)}) async-start(bf16[32,2,8192]{2,1,0:T(2,128)(2,1)} %reshape.609), calls=%async_computation.1 | async-start | bytes 2097152 | tf_op jit(solution)/shard_map/all_to_all | solution.py:99
  38.9 21.4 %copy-start.7 = (u32[256]{0:T(256)S(1)}, u32[256]{0:T(256)}, u32[]{:S(2)}) copy-start(u32[256]{0:T(256)} %constant.226) | copy-start | bytes 3076
  38.9 22.6 %copy-start.8 = (bf16[16]{0:T(256)(128)(2,1)S(1)}, bf16[16]{0:T(256)(128)(2,1)}, u32[]{:S(2)}) copy-start(bf16[16]{0:T(256)(128)(2,1)} %param.29) | copy-start | bytes 100
  54.4 35.4 %all-to-all-start.3 = ((bf16[32,2,8192]{2,1,0:T(2,128)(2,1)}), bf16[32,2,8192]{2,1,0:T(2,128)(2,1)}, u32[]{:S(2)}, u32[]{:S(2)}) async-start(bf16[32,2,8192]{2,1,0:T(2,128)(2,1)} %reshape.611), calls=%async_computation.3 | async-start | bytes 2097152 | tf_op jit(solution)/shard_map/all_to_all | solution.py:100
  89.8 41.9 %all-to-all-start.2 = ((bf16[32,2,8192]{2,1,0:T(2,128)(2,1)}), bf16[32,2,8192]{2,1,0:T(2,128)(2,1)}, u32[]{:S(2)}, u32[]{:S(2)}) async-start(bf16[32,2,8192]{2,1,0:T(2,128)(2,1)} %reshape.613), calls=%async_computation.2 | async-start | bytes 2097152 | tf_op jit(solution)/shard_map/all_to_all | solution.py:101
  123.8 5.2 %copy-start.1 = (bf16[2,64,32,128]{3,1,2,0:T(8,128)(2,1)S(1)}, bf16[2,64,32,128]{3,1,2,0:T(8,128)(2,1)}, u32[]{:S(2)}) copy-start(bf16[2,64,32,128]{3,1,2,0:T(8,128)(2,1)} %copy.61) | copy-start | bytes 3145732
  125.7 6.0 %copy-start.5 = (bf16[2,2048,1,128]{3,1,0,2:T(8,128)(2,1)}, bf16[2,2048,1,128]{3,1,0,2:T(8,128)(2,1)S(1)}, u32[]{:S(2)}) copy-start(bf16[2,2048,1,128]{3,1,0,2:T(8,128)(2,1)S(1)} %fusion.90) | copy-start | bytes 3145732
  142.4 3.6 copy-start.4
  150.2 5.3 %copy-start.2 = (bf16[2,64,32,128]{3,1,2,0:T(8,128)(2,1)S(1)}, bf16[2,64,32,128]{3,1,2,0:T(8,128)(2,1)}, u32[]{:S(2)}) copy-start(bf16[2,64,32,128]{3,1,2,0:T(8,128)(2,1)} %copy.61) | copy-start | bytes 3145732
  150.2 5.3 %copy-start.6 = (pred[512,1536]{1,0:T(8,128)(4,1)S(1)}, pred[512,1536]{1,0:T(8,128)(4,1)}, u32[]{:S(2)}) copy-start(pred[512,1536]{1,0:T(8,128)(4,1)} %iota_compare_fusion.1) | copy-start | bytes 2359300
  161.4 5.7 %copy-start = (bf16[2,64,32,128]{3,1,2,0:T(8,128)(2,1)S(1)}, bf16[2,64,32,128]{3,1,2,0:T(8,128)(2,1)}, u32[]{:S(2)}) copy-start(bf16[2,64,32,128]{3,1,2,0:T(8,128)(2,1)} %copy.63) | copy-start | bytes 3145732
  167.1 4.1 %copy-start.9 = (f32[2,512,1024]{2,1,0:T(8,128)}, f32[2,512,1024]{2,1,0:T(8,128)S(1)}, u32[]{:S(2)}) copy-start(f32[2,512,1024]{2,1,0:T(8,128)S(1)} %get-tuple-element.131) | copy-start | bytes 12582916
  200.9 68.1 %all-to-all-start.6 = ((bf16[2,2048,128]{2,0,1:T(2,128)(2,1)}), bf16[2,2048,128]{2,0,1:T(2,128)(2,1)S(1)}, u32[]{:S(2)}, u32[]{:S(2)}) async-start(bf16[2,2048,128]{2,0,1:T(2,128)(2,1)} %copy.80), calls=%async_computation.6 | async-start | bytes 2097152 | tf_op jit(solution)/shard_map/all_to_all | solution.py:107
  266.9 10.7 %copy-start.3 = (bf16[2,64,32,128]{3,1,2,0:T(8,128)(2,1)S(1)}, bf16[2,64,32,128]{3,1,2,0:T(8,128)(2,1)}, u32[]{:S(2)}) copy-start(bf16[2,64,32,128]{3,1,2,0:T(8,128)(2,1)} %copy.61) | copy-start | bytes 3145732
  268.9 65.1 %all-to-all-start.5 = ((bf16[2,2048,128]{2,0,1:T(2,128)(2,1)}), bf16[2,2048,128]{2,0,1:T(2,128)(2,1)S(1)}, u32[]{:S(2)}, u32[]{:S(2)}) async-start(bf16[2,2048,128]{2,0,1:T(2,128)(2,1)} %copy.74), calls=%async_computation.5 | async-start | bytes 2097152 | tf_op jit(solution)/shard_map/all_to_all | solution.py:106
  334.0 33.8 %all-to-all-start.4 = ((bf16[2,2048,128]{2,0,1:T(2,128)(2,1)}), bf16[2,2048,128]{2,0,1:T(2,128)(2,1)S(1)}, u32[]{:S(2)}, u32[]{:S(2)}) async-start(bf16[2,2048,128]{2,0,1:T(2,128)(2,1)} %copy.67), calls=%async_computation.4 | async-start | bytes 2097152 | tf_op jit(solution)/shard_map/all_to_all | solution.py:105
where the time goes:
time: 377 us; the launch traced here: 370 us
  matrix products  149 us (40%)
  local copies, waits for them, and re-layouts  95.4 us (25%)
  starting transfers between devices  54.3 us (14%)
  blocking collectives  38.4 us (10%)
  waiting for transfers between devices  17.8 us (5%)
  other arithmetic  13 us (3%)
    dot_general x4, matrix products, attend(): jnp.einsum('nhqk,nqhd->nkhd', grad_scores, block_query, preferred_element...  50.8 us
    unnamed x36, local copies, waits for them, and re-layouts  47 us
    dot_general x4, matrix products, attend(): jnp.einsum('nhqk,nkhd->nqhd', grad_scores, seen_keys, preferred_element_t...  45.8 us
    unnamed x2, blocking collectives  38.4 us
    dot_general x4, matrix products, attend(): jnp.einsum('nhqk,nqhd->nkhd', weights_low, block_grad, preferred_element_...  20 us
    sub x3, matrix products, attend(): shifted = jnp.exp(scores - highest)  17.2 us
    dot_general x4, matrix products, attend(): jnp.einsum('nqhd,nkhd->nhqk', block_grad, seen_values, preferred_element_...  12.2 us
    all_to_all x1, waiting for transfers between devices, body(): lax.all_to_all(queries, 'seq', split_axis=2, concat_axis=1, tiled=True)  9.55 us
  transfers between devices with their start and end apart: 7, of which 2 were waited for; matrix products, arithmetic and copies ran while one was open for 48% of the time, Pallas kernels for 0%

commit v1 on v0

v1 whole, which is shorter than its diff:
```python
import functools
import math

import jax
import jax.numpy as jnp
from jax import lax
from jax.experimental import pallas as pl
from jax.experimental.pallas import tpu as pltpu
from jax.sharding import PartitionSpec as P

HDIM = 128
TILE = 256
MASKED = -1e30


def _pack_kernel(*refs):
    out_ref = refs[-1]
    heads = out_ref.shape[0]
    for t, ref in enumerate(refs[:-1]):
        for h in range(heads):
            out_ref[h, t] = ref[0, :, h * HDIM : (h + 1) * HDIM]


def pack(arrays, item, step_heads):
    _, rows, width = arrays[0].shape
    heads = width // HDIM
    count = len(arrays)
    return pl.pallas_call(
        _pack_kernel,
        grid=(heads // step_heads,),
        in_specs=[
            pl.BlockSpec((1, rows, step_heads * HDIM), lambda c: (item, 0, c))
        ] * count,
        out_specs=pl.BlockSpec((step_heads, count, rows, HDIM), lambda c: (c, 0, 0, 0)),
        out_shape=jax.ShapeDtypeStruct((heads, count, rows, HDIM), arrays[0].dtype),
        cost_estimate=pl.CostEstimate(
            flops=0, bytes_accessed=4 * count * rows * width, transcendentals=0
        ),
        name="pack",
    )(*arrays)


def _unpack_kernel(count, in_ref, *refs):
    outs = refs[-count:]
    heads = in_ref.shape[0]
    for t, ref in enumerate(outs):
        for h in range(heads):
            ref[0, :, h * HDIM : (h + 1) * HDIM] = in_ref[h, t]


def unpack(packed, item, items, step_heads, into=None):
    heads, count, rows, _ = packed.shape
    width = heads * HDIM
    kwargs = {}
    operands = [packed]
    in_specs = [pl.BlockSpec((step_heads, count, rows, HDIM), lambda c: (c, 0, 0, 0))]
    if into is not None:
        operands += list(into)
        in_specs += [pl.BlockSpec(memory_space=pl.ANY)] * count
        kwargs["input_output_aliases"] = {1 + t: t for t in range(count)}
    return pl.pallas_call(
        functools.partial(_unpack_kernel, count),
        grid=(heads // step_heads,),
        in_specs=in_specs,
        out_specs=[
            pl.BlockSpec((1, rows, step_heads * HDIM), lambda c: (item, 0, c))
        ] * count,
        out_shape=[jax.ShapeDtypeStruct((items, rows, width), packed.dtype)] * count,
        cost_estimate=pl.CostEstimate(
            flops=0, bytes_accessed=4 * count * rows * width, transcendentals=0
        ),
        name="unpack",
        **kwargs,
    )(*operands)


def _dot_nt(a, b):
    return lax.dot_general(a, b, (((1,), (1,)), ((), ())), preferred_element_type=jnp.float32)


def _dot(a, b):
    return jnp.dot(a, b, preferred_element_type=jnp.float32)


def _fold(x, op):
    parts = [x[r : r + 8] for r in range(0, x.shape[0], 8)]
    while len(parts) > 1:
        parts = [op(a, b) for a, b in zip(parts[::2], parts[1::2])]
    return parts[0]


def _attend_kernel(x_ref, bias_ref, y_ref, sums_ref, q_s, kt_s, s_s, dp_s, dk_s, dv_s):
    peers, _, rows, _ = x_ref.shape
    blocks = peers * rows // TILE
    per = TILE // rows
    factor = 1.0 / math.sqrt(HDIM)

    def piece(t, i):
        return x_ref[i * per : (i + 1) * per, t].reshape(TILE, HDIM)

    for i in range(blocks):
        q_s[i] = (piece(0, i).astype(jnp.float32) + bias_ref[...]).astype(jnp.bfloat16)
        kt_s[i] = piece(1, i).T

    key_id = lax.broadcasted_iota(jnp.int32, (TILE, TILE), 0)
    query_id = lax.broadcasted_iota(jnp.int32, (TILE, TILE), 1)
    sums = jnp.zeros((8, HDIM), jnp.float32)
    for i in range(blocks):
        q_i = q_s[i]
        g_i = piece(3, i)
        top = None
        for j in range(i + 1):
            s = _dot_nt(piece(1, j), q_i) * factor
            if j == i:
                s = jnp.where(key_id <= query_id, s, MASKED)
            s_s[j] = s
            part = _fold(s, jnp.maximum)
            top = part if top is None else jnp.maximum(top, part)
        top = jnp.max(top, axis=0, keepdims=True)
        total = jnp.zeros((8, TILE), jnp.float32)
        row_dot = jnp.zeros((8, TILE), jnp.float32)
        for j in range(i + 1):
            e = jnp.exp(s_s[j] - top)
            dp = _dot_nt(piece(2, j), g_i)
            s_s[j] = e
            dp_s[j] = dp
            total = total + _fold(e, jnp.add)
            row_dot = row_dot + _fold(e * dp, jnp.add)
        inv = 1.0 / jnp.sum(total, axis=0, keepdims=True)
        row_dot = jnp.sum(row_dot, axis=0, keepdims=True) * inv
        dqt = None
        for j in range(i + 1):
            p = s_s[j] * inv
            ds = (p * (dp_s[j] - row_dot) * factor).astype(jnp.bfloat16)
            dv = _dot(p.astype(jnp.bfloat16), g_i)
            dk = _dot(ds, q_i)
            term = _dot(kt_s[j], ds)
            dqt = term if dqt is None else dqt + term
            if j == i:
                dv_s[j] = dv
                dk_s[j] = dk
            else:
                dv_s[j] += dv
                dk_s[j] += dk
        dq = dqt.T
        sums = sums + _fold(dq, jnp.add)
        y_ref[i * per : (i + 1) * per, 0] = dq.astype(jnp.bfloat16).reshape(per, rows, HDIM)
    for j in range(blocks):
        y_ref[j * per : (j + 1) * per, 1] = dk_s[j].astype(jnp.bfloat16).reshape(per, rows, HDIM)
        y_ref[j * per : (j + 1) * per, 2] = dv_s[j].astype(jnp.bfloat16).reshape(per, rows, HDIM)
    sums_ref[...] = jnp.sum(sums, axis=0, keepdims=True)


def attend(x, bias):
    peers, _, rows, _ = x.shape
    seq = peers * rows
    blocks = seq // TILE
    area = seq * (seq + TILE) // 2
    return pl.pallas_call(
        _attend_kernel,
        in_specs=[pl.BlockSpec(memory_space=pltpu.VMEM)] * 2,
        out_specs=[pl.BlockSpec(memory_space=pltpu.VMEM)] * 2,
        out_shape=[
            jax.ShapeDtypeStruct((peers, 3, rows, HDIM), jnp.bfloat16),
            jax.ShapeDtypeStruct((1, HDIM), jnp.float32),
        ],
        scratch_shapes=[
            pltpu.VMEM((blocks, TILE, HDIM), jnp.bfloat16),
            pltpu.VMEM((blocks, HDIM, TILE), jnp.bfloat16),
            pltpu.VMEM((blocks, TILE, TILE), jnp.float32),
            pltpu.VMEM((blocks, TILE, TILE), jnp.float32),
            pltpu.VMEM((blocks, TILE, HDIM), jnp.float32),
            pltpu.VMEM((blocks, TILE, HDIM), jnp.float32),
        ],
        compiler_params=pltpu.CompilerParams(vmem_limit_bytes=32 * 1024 * 1024),
        cost_estimate=pl.CostEstimate(
            flops=10 * area * HDIM * 2, bytes_accessed=14 * seq * HDIM, transcendentals=area
        ),
        name="attend",
    )(x, bias)


def spread_sum(x, size):
    step = 1
    while step < size:
        x = x + lax.ppermute(x, "dp", [(d, d ^ step) for d in range(size)])
        step *= 2
    return x


def body(queries, key_states, value_states, grad_output, query_bias, *, dp_size):
    items, rows, width = queries.shape
    inputs = (queries, key_states, value_states, grad_output)
    me = lax.axis_index("dp")
    share = query_bias.shape[0]

    own = lax.broadcasted_iota(jnp.int32, (dp_size, share), 0) == me
    slots = jnp.where(own, query_bias[None, :], jnp.zeros((), query_bias.dtype))
    bias = spread_sum(slots, dp_size).astype(jnp.float32).reshape(1, dp_size * share)

    sums = None
    results = []
    for item in range(items):
        packed = pack(inputs, item, 8)
        moved = lax.all_to_all(packed, "seq", split_axis=0, concat_axis=0, tiled=True)
        grads, part = attend(moved, bias)
        sums = part if sums is None else sums + part
        results.append(lax.all_to_all(grads, "seq", split_axis=0, concat_axis=0, tiled=True))
    outs = None
    for item, packed in enumerate(results):
        outs = unpack(packed, item, items, 8, into=outs)
    total = spread_sum(sums.reshape(dp_size, share), dp_size)
    grad_bias = lax.dynamic_index_in_dim(total, me, 0, keepdims=False)
    return (*outs, grad_bias)


def solution(mesh):
    rows = P("dp", "seq", None)
    cols = P(("seq", "dp"))
    return jax.shard_map(
        functools.partial(body, dp_size=mesh.shape["dp"]),
        mesh=mesh,
        in_specs=(rows, rows, rows, rows, cols),
        out_specs=(rows, rows, rows, cols),
        check_vma=False,
    )
```

time: 377 us -> 162 us (0.43)
  the two profiles are of different devices: /device:TPU:32 before, /device:TPU:8 now
where the time goes in v1:
time: 162 us; the launch traced here: 161 us
  waiting for transfers between devices  69.6 us (43%)
  starting transfers between devices  48.8 us (30%)
  Pallas kernels  34.4 us (21%)
  local copies, waits for them, and re-layouts  7.04 us (4%)
    ppermute x6, waiting for transfers between devices, spread_sum(): x = x + lax.ppermute(x, 'dp', [(d, d ^ step) for d in range(size)])  37.1 us
    all_to_all x2, waiting for transfers between devices, body(): lax.all_to_all(packed, 'seq', split_axis=0, concat_axis=0, tiled=True)  25 us
    pallas_call x2, Pallas kernels, attend(): pl.pallas_call(_attend_kernel, in_specs=[pl.BlockSpec(memory_space=pltpu....  19.1 us
    all_to_all x2, starting transfers between devices, body(): lax.all_to_all(grads, 'seq', split_axis=0, concat_axis=0, tiled=True)  18.2 us
    all_to_all x2, starting transfers between devices, body(): lax.all_to_all(packed, 'seq', split_axis=0, concat_axis=0, tiled=True)  15.9 us
    ppermute x6, starting transfers between devices, spread_sum(): x = x + lax.ppermute(x, 'dp', [(d, d ^ step) for d in range(size)])  14.7 us
    pallas_call x2, Pallas kernels, pack(): pl.pallas_call(_pack_kernel, grid=(heads // step_heads,), in_specs=[pl.Bl...  7.93 us
    all_to_all x2, waiting for transfers between devices, body(): lax.all_to_all(grads, 'seq', split_axis=0, concat_axis=0, tiled=True)  7.44 us
  transfers between devices with their start and end apart: 10, of which 8 were waited for; matrix products, arithmetic and copies ran while one was open for 1% of the time, Pallas kernels for 17%

profile of v1, /device:TPU:8, one launch (start us, length us, event | category | flops | bytes accessed | tf_op | source)
XLA Modules:
  0.0 160.8 jit_solution(2976413821694977297)
XLA Ops:
  0.6 3.9 %pack.3 = bf16[32,4,64,128]{3,2,1,0:T(8,128)(2,1)} custom-call(bf16[2,64,4096]{2,1,0:T(8,128)(2,1)} %refs_0_.3, bf16[2,64,4096]{2,1,0:T(8,128)(2,1)} %refs_1_.3, bf16[2,64,4096]{2,1,0:T(8,128)(2,1)} %refs_2_.3, bf16[2,64,4096]{2,1,0:T(8,128)(2,1)} %refs_3_.3), custom_call_target="tpu_custom_call" | custom-call | bytes 4194304 | tf_op jit(solution)/shard_map/pack/pallas_call | solution.py:28
  4.6 8.9 %all-to-all-start.2 = ((bf16[32,4,64,128]{3,2,1,0:T(8,128)(2,1)}), bf16[32,4,64,128]{3,2,1,0:T(8,128)(2,1)S(1)}, u32[]{:S(2)}, u32[]{:S(2)}) async-start(bf16[32,4,64,128]{3,2,1,0:T(8,128)(2,1)} %pack.3), calls=%async_computation.2 | async-start | bytes 4194304 | tf_op jit(solution)/shard_map/all_to_all | solution.py:205
  13.5 4.0 %pack.2 = bf16[32,4,64,128]{3,2,1,0:T(8,128)(2,1)} custom-call(bf16[2,64,4096]{2,1,0:T(8,128)(2,1)} %refs_0_.3, bf16[2,64,4096]{2,1,0:T(8,128)(2,1)} %refs_1_.3, bf16[2,64,4096]{2,1,0:T(8,128)(2,1)} %refs_2_.3, bf16[2,64,4096]{2,1,0:T(8,128)(2,1)} %refs_3_.3), custom_call_target="tpu_custom_call" | custom-call | bytes 4194304 | tf_op jit(solution)/shard_map/pack/pallas_call | solution.py:28
  17.5 25.0 %all-to-all-done.2.x_ref = bf16[32,4,64,128]{3,2,1,0:T(8,128)(2,1)S(1)} async-done(((bf16[32,4,64,128]{3,2,1,0:T(8,128)(2,1)}), bf16[32,4,64,128]{3,2,1,0:T(8,128)(2,1)S(1)}, u32[]{:S(2)}, u32[]{:S(2)}) %all-to-all-start.2) | async-done | bytes 2097184 | tf_op jit(solution)/shard_map/all_to_all | solution.py:205
  42.4 1.3 copy-done
  43.8 7.0 %all-to-all-start = ((bf16[32,4,64,128]{3,2,1,0:T(8,128)(2,1)}), bf16[32,4,64,128]{3,2,1,0:T(8,128)(2,1)S(1)}, u32[]{:S(2)}, u32[]{:S(2)}) async-start(bf16[32,4,64,128]{3,2,1,0:T(8,128)(2,1)} %pack.2), calls=%async_computation | async-start | bytes 4194304 | tf_op jit(solution)/shard_map/all_to_all | solution.py:205
  52.1 3.3 %collective-permute-start.1 = (bf16[8,16]{1,0:T(8,128)(2,1)S(1)}, bf16[8,16]{1,0:T(8,128)(2,1)S(1)}, u32[]{:S(2)}, u32[]{:S(2)}) collective-permute-start(bf16[8,16]{1,0:T(8,128)(2,1)S(1)} %fusion), channel_id=1, source_target_pairs={{0,2},{1,3},{2,0},{3,1},{4,6},{5,7},{6,4},{7,5},{8,10},{9,11},{10,... | collective-permute-start | bytes 776 | tf_op jit(solution)/shard_map/ppermute | solution.py:186
  55.4 17.8 %collective-permute-done.1 = bf16[8,16]{1,0:T(8,128)(2,1)S(1)} collective-permute-done((bf16[8,16]{1,0:T(8,128)(2,1)S(1)}, bf16[8,16]{1,0:T(8,128)(2,1)S(1)}, u32[]{:S(2)}, u32[]{:S(2)}) %collective-permute-start.1) | collective-permute-done | bytes 288 | tf_op jit(solution)/shard_map/ppermute | solution.py:186
  73.3 6.3 %collective-permute-start.2 = (bf16[8,16]{1,0:T(8,128)(2,1)S(1)}, bf16[8,16]{1,0:T(8,128)(2,1)S(1)}, u32[]{:S(2)}, u32[]{:S(2)}) collective-permute-start(bf16[8,16]{1,0:T(8,128)(2,1)S(1)} %fusion.1), channel_id=1, source_target_pairs={{0,4},{1,5},{2,6},{3,7},{4,0},{5,1},{6,2},{7,3},{8,12},{9,13},{10,... | collective-permute-start | bytes 776 | tf_op jit(solution)/shard_map/ppermute | solution.py:186
  79.6 1.6 collective-permute-done.2
  81.3 1.6 copy-done.1
  82.8 9.6 %attend.3 = (bf16[32,3,64,128]{3,2,1,0:T(8,128)(2,1)S(1)}, f32[1,128]{1,0:T(1,128)S(1)}) custom-call(bf16[32,4,64,128]{3,2,1,0:T(8,128)(2,1)S(1)} %copy-done.1, f32[1,128]{1,0:T(1,128)S(1)} %reshape.21.bias_ref), custom_call_target="tpu_custom_call" | custom-call | flops 6039797760 | bytes 3670016 | tf_op jit(solution)/shard_map/attend/pallas_call | solution.py:159
  93.6 12.7 %all-to-all-start.3 = ((bf16[32,3,64,128]{3,2,1,0:T(8,128)(2,1)}), bf16[32,3,64,128]{3,2,1,0:T(8,128)(2,1)}, u32[]{:S(2)}, u32[]{:S(2)}) async-start(bf16[32,3,64,128]{3,2,1,0:T(8,128)(2,1)} %copy-done.3), calls=%async_computation.3 | async-start | bytes 3145728 | tf_op jit(solution)/shard_map/all_to_all | solution.py:208
  106.3 9.6 %attend.2 = (bf16[32,3,64,128]{3,2,1,0:T(8,128)(2,1)S(1)}, f32[1,128]{1,0:T(1,128)S(1)}) custom-call(bf16[32,4,64,128]{3,2,1,0:T(8,128)(2,1)S(1)} %all-to-all-done.x_ref, f32[1,128]{1,0:T(1,128)S(1)} %reshape.21.bias_ref), custom_call_target="tpu_custom_call" | custom-call | flops 6039797760 | bytes 3670016 | tf_op jit(solution)/shard_map/attend/pallas_call | solution.py:159
  115.9 1.2 copy-done.2
  117.0 7.4 %all-to-all-done.3.in_ref = bf16[32,3,64,128]{3,2,1,0:T(8,128)(2,1)} async-done(((bf16[32,3,64,128]{3,2,1,0:T(8,128)(2,1)}), bf16[32,3,64,128]{3,2,1,0:T(8,128)(2,1)}, u32[]{:S(2)}, u32[]{:S(2)}) %all-to-all-start.3) | async-done | bytes 1572896 | tf_op jit(solution)/shard_map/all_to_all | solution.py:208
  124.4 5.5 %all-to-all-start.1 = ((bf16[32,3,64,128]{3,2,1,0:T(8,128)(2,1)}), bf16[32,3,64,128]{3,2,1,0:T(8,128)(2,1)S(1)}, u32[]{:S(2)}, u32[]{:S(2)}) async-start(bf16[32,3,64,128]{3,2,1,0:T(8,128)(2,1)} %copy-done.2), calls=%async_computation.1 | async-start | bytes 3145728 | tf_op jit(solution)/shard_map/all_to_all | solution.py:208
  130.1 1.2 collective-permute-done.3
  131.2 13.0 %collective-permute-done.4 = f32[8,16]{1,0:T(8,128)S(1)} collective-permute-done((f32[8,16]{1,0:T(8,128)S(1)}, f32[8,16]{1,0:T(8,128)S(1)}, u32[]{:S(2)}, u32[]{:S(2)}) %collective-permute-start.4) | collective-permute-done | bytes 544 | tf_op jit(solution)/shard_map/ppermute | solution.py:186
  144.3 5.1 %collective-permute-start.5 = (f32[8,16]{1,0:T(8,128)S(1)}, f32[8,16]{1,0:T(8,128)S(1)}, u32[]{:S(2)}, u32[]{:S(2)}) collective-permute-start(f32[8,16]{1,0:T(8,128)S(1)} %add.30), channel_id=1, source_target_pairs={{0,4},{1,5},{2,6},{3,7},{4,0},{5,1},{6,2},{7,3},{8,12},{9,13},{10,... | collective-permute-start | bytes 1544 | tf_op jit(solution)/shard_map/ppermute | solution.py:186
  149.3 2.4 %collective-permute-done.5 = f32[8,16]{1,0:T(8,128)S(1)} collective-permute-done((f32[8,16]{1,0:T(8,128)S(1)}, f32[8,16]{1,0:T(8,128)S(1)}, u32[]{:S(2)}, u32[]{:S(2)}) %collective-permute-start.5) | collective-permute-done | bytes 544 | tf_op jit(solution)/shard_map/ppermute | solution.py:186
  152.3 3.6 %unpack.2 = (bf16[2,64,4096]{2,1,0:T(8,128)(2,1)}, bf16[2,64,4096]{2,1,0:T(8,128)(2,1)}, bf16[2,64,4096]{2,1,0:T(8,128)(2,1)}) custom-call(bf16[32,3,64,128]{3,2,1,0:T(8,128)(2,1)} %all-to-all-done.3.in_ref), custom_call_target="tpu_custom_call" | custom-call | bytes 3145728 | tf_op jit(solution)/shard_map/unpack/pallas_call | solution.py:61
  155.9 1.2 copy-done.4
  157.1 3.6 %unpack.3 = (bf16[2,64,4096]{2,1,0:T(8,128)(2,1)}, bf16[2,64,4096]{2,1,0:T(8,128)(2,1)}, bf16[2,64,4096]{2,1,0:T(8,128)(2,1)}) custom-call(bf16[32,3,64,128]{3,2,1,0:T(8,128)(2,1)} %copy-done.4, bf16[2,64,4096]{2,1,0:T(8,128)(2,1)} %get-tuple-element.16.refs_0_, ...), custom_call_target="tpu_custom_call", output_to_operand_aliasing={{0}: (1, {}), {1}: (2, {}), {2}: (3, {})} | custom-call | bytes 3145728 | tf_op jit(solution)/shard_map/unpack/pallas_call | solution.py:61
  (26 shorter events, 3.3 us)
Async XLA Ops:
  4.6 37.9 %all-to-all-start.2 = ((bf16[32,4,64,128]{3,2,1,0:T(8,128)(2,1)}), bf16[32,4,64,128]{3,2,1,0:T(8,128)(2,1)S(1)}, u32[]{:S(2)}, u32[]{:S(2)}) async-start(bf16[32,4,64,128]{3,2,1,0:T(8,128)(2,1)} %pack.3), calls=%async_computation.2 | async-start | bytes 4194304 | tf_op jit(solution)/shard_map/all_to_all | solution.py:205
  17.5 33.3 %copy-start.5 = (bf16[16]{0:T(256)(128)(2,1)S(1)}, bf16[16]{0:T(256)(128)(2,1)}, u32[]{:S(2)}) copy-start(bf16[16]{0:T(256)(128)(2,1)} %param.9) | copy-start | bytes 100
  42.4 1.3 copy-start
  43.8 49.8 %all-to-all-start = ((bf16[32,4,64,128]{3,2,1,0:T(8,128)(2,1)}), bf16[32,4,64,128]{3,2,1,0:T(8,128)(2,1)S(1)}, u32[]{:S(2)}, u32[]{:S(2)}) async-start(bf16[32,4,64,128]{3,2,1,0:T(8,128)(2,1)} %pack.2), calls=%async_computation | async-start | bytes 4194304 | tf_op jit(solution)/shard_map/all_to_all | solution.py:205
  50.9 1.2 collective-permute-start
  52.1 21.1 %collective-permute-start.1 = (bf16[8,16]{1,0:T(8,128)(2,1)S(1)}, bf16[8,16]{1,0:T(8,128)(2,1)S(1)}, u32[]{:S(2)}, u32[]{:S(2)}) collective-permute-start(bf16[8,16]{1,0:T(8,128)(2,1)S(1)} %fusion), channel_id=1, source_target_pairs={{0,2},{1,3},{2,0},{3,1},{4,6},{5,7},{6,4},{7,5},{8,10},{9,11},{10,... | collective-permute-start | bytes 776 | tf_op jit(solution)/shard_map/ppermute | solution.py:186
  73.3 7.9 %collective-permute-start.2 = (bf16[8,16]{1,0:T(8,128)(2,1)S(1)}, bf16[8,16]{1,0:T(8,128)(2,1)S(1)}, u32[]{:S(2)}, u32[]{:S(2)}) collective-permute-start(bf16[8,16]{1,0:T(8,128)(2,1)S(1)} %fusion.1), channel_id=1, source_target_pairs={{0,4},{1,5},{2,6},{3,7},{4,0},{5,1},{6,2},{7,3},{8,12},{9,13},{10,... | collective-permute-start | bytes 776 | tf_op jit(solution)/shard_map/ppermute | solution.py:186
  81.3 1.6 copy-start.1
  92.4 1.1 copy-start.3
  93.6 30.9 %all-to-all-start.3 = ((bf16[32,3,64,128]{3,2,1,0:T(8,128)(2,1)}), bf16[32,3,64,128]{3,2,1,0:T(8,128)(2,1)}, u32[]{:S(2)}, u32[]{:S(2)}) async-start(bf16[32,3,64,128]{3,2,1,0:T(8,128)(2,1)} %copy-done.3), calls=%async_computation.3 | async-start | bytes 3145728 | tf_op jit(solution)/shard_map/all_to_all | solution.py:208
  115.8 1.2 copy-start.2
  124.4 31.5 %all-to-all-start.1 = ((bf16[32,3,64,128]{3,2,1,0:T(8,128)(2,1)}), bf16[32,3,64,128]{3,2,1,0:T(8,128)(2,1)S(1)}, u32[]{:S(2)}, u32[]{:S(2)}) async-start(bf16[32,3,64,128]{3,2,1,0:T(8,128)(2,1)} %copy-done.2), calls=%async_computation.1 | async-start | bytes 3145728 | tf_op jit(solution)/shard_map/all_to_all | solution.py:208
  130.0 1.2 collective-permute-start.3
  131.2 13.0 %collective-permute-start.4 = (f32[8,16]{1,0:T(8,128)S(1)}, f32[8,16]{1,0:T(8,128)S(1)}, u32[]{:S(2)}, u32[]{:S(2)}) collective-permute-start(f32[8,16]{1,0:T(8,128)S(1)} %add.29), channel_id=1, source_target_pairs={{0,2},{1,3},{2,0},{3,1},{4,6},{5,7},{6,4},{7,5},{8,10},{9,11},{10,... | collective-permute-start | bytes 1544 | tf_op jit(solution)/shard_map/ppermute | solution.py:186
  144.3 7.5 %collective-permute-start.5 = (f32[8,16]{1,0:T(8,128)S(1)}, f32[8,16]{1,0:T(8,128)S(1)}, u32[]{:S(2)}, u32[]{:S(2)}) collective-permute-start(f32[8,16]{1,0:T(8,128)S(1)} %add.30), channel_id=1, source_target_pairs={{0,4},{1,5},{2,6},{3,7},{4,0},{5,1},{6,2},{7,3},{8,12},{9,13},{10,... | collective-permute-start | bytes 1544 | tf_op jit(solution)/shard_map/ppermute | solution.py:186
  155.9 1.2 copy-start.4

commit v2 on v1

--- a/solution.py
+++ b/solution.py
@@ -13,62 +13,101 @@
 MASKED = -1e30
 
 
-def _pack_kernel(*refs):
-    out_ref = refs[-1]
-    heads = out_ref.shape[0]
-    for t, ref in enumerate(refs[:-1]):
-        for h in range(heads):
-            out_ref[h, t] = ref[0, :, h * HDIM : (h + 1) * HDIM]
-
-
-def pack(arrays, item, step_heads):
+def _pack_kernel(item, count, groups, *refs):
+    srcs, out_ref = refs[:count], refs[count]
+    in_s, out_s, in_sem, out_sem = refs[-4:]
+    heads = out_ref.shape[0] // groups
+
+    def load(c, t):
+        cols = pl.ds(c * heads * HDIM, heads * HDIM)
+        return pltpu.make_async_copy(
+            srcs[t].at[item, :, cols], in_s.at[t, :, cols], in_sem.at[c, t]
+        )
+
+    def store(c):
+        span = pl.ds(c * heads, heads)
+        return pltpu.make_async_copy(out_s.at[span], out_ref.at[span], out_sem.at[c])
+
+    for c in range(groups):
+        for t in range(count):
+            load(c, t).start()
+    for c in range(groups):
+        for t in range(count):
+            load(c, t).wait()
+            for h in range(c * heads, (c + 1) * heads):
+                out_s[h, t] = in_s[t, :, h * HDIM : (h + 1) * HDIM]
+        store(c).start()
+    for c in range(groups):
+        store(c).wait()
+
+
+def pack(arrays, item, groups):
     _, rows, width = arrays[0].shape
     heads = width // HDIM
     count = len(arrays)
+    dtype = arrays[0].dtype
     return pl.pallas_call(
-        _pack_kernel,
-        grid=(heads // step_heads,),
-        in_specs=[
-            pl.BlockSpec((1, rows, step_heads * HDIM), lambda c: (item, 0, c))
-        ] * count,
-        out_specs=pl.BlockSpec((step_heads, count, rows, HDIM), lambda c: (c, 0, 0, 0)),
-        out_shape=jax.ShapeDtypeStruct((heads, count, rows, HDIM), arrays[0].dtype),
+        functools.partial(_pack_kernel, item, count, groups),
+        in_specs=[pl.BlockSpec(memory_space=pl.ANY)] * count,
+        out_specs=pl.BlockSpec(memory_space=pl.ANY),
+        out_shape=jax.ShapeDtypeStruct((heads, count, rows, HDIM), dtype),
+        scratch_shapes=[
+            pltpu.VMEM((count, rows, width), dtype),
+            pltpu.VMEM((heads, count, rows, HDIM), dtype),
+            pltpu.SemaphoreType.DMA((groups, count)),
+            pltpu.SemaphoreType.DMA((groups,)),
+        ],
         cost_estimate=pl.CostEstimate(
             flops=0, bytes_accessed=4 * count * rows * width, transcendentals=0
         ),
+        compiler_params=pltpu.CompilerParams(vmem_limit_bytes=56 * 1024 * 1024),
         name="pack",
     )(*arrays)
 
 
-def _unpack_kernel(count, in_ref, *refs):
-    outs = refs[-count:]
-    heads = in_ref.shape[0]
-    for t, ref in enumerate(outs):
-        for h in range(heads):
-            ref[0, :, h * HDIM : (h + 1) * HDIM] = in_ref[h, t]
-
-
-def unpack(packed, item, items, step_heads, into=None):
+def _unpack_kernel(item, count, groups, *refs):
+    in_ref, outs = refs[0], refs[-count - 2 : -2]
+    out_s, out_sem = refs[-2:]
+    heads = in_ref.shape[0] // groups
+
+    def store(c, t):
+        cols = pl.ds(c * heads * HDIM, heads * HDIM)
+        return pltpu.make_async_copy(
+            out_s.at[t, :, cols], outs[t].at[item, :, cols], out_sem.at[c, t]
+        )
+
+    for c in range(groups):
+        for t in range(count):
+            for h in range(c * heads, (c + 1) * heads):
+                out_s[t, :, h * HDIM : (h + 1) * HDIM] = in_ref[h, t]
+            store(c, t).start()
+    for c in range(groups):
+        for t in range(count):
+            store(c, t).wait()
+
+
+def unpack(packed, item, items, groups, into=None):
     heads, count, rows, _ = packed.shape
     width = heads * HDIM
     kwargs = {}
     operands = [packed]
-    in_specs = [pl.BlockSpec((step_heads, count, rows, HDIM), lambda c: (c, 0, 0, 0))]
     if into is not None:
         operands += list(into)
-        in_specs += [pl.BlockSpec(memory_space=pl.ANY)] * count
         kwargs["input_output_aliases"] = {1 + t: t for t in range(count)}
     return pl.pallas_call(
-        functools.partial(_unpack_kernel, count),
-        grid=(heads // step_heads,),
-        in_specs=in_specs,
-        out_specs=[
-            pl.BlockSpec((1, rows, step_heads * HDIM), lambda c: (item, 0, c))
-        ] * count,
+        functools.partial(_unpack_kernel, item, count, groups),
+        in_specs=[pl.BlockSpec(memory_space=pltpu.VMEM)]
+        + [pl.BlockSpec(memory_space=pl.ANY)] * (len(operands) - 1),
+        out_specs=[pl.BlockSpec(memory_space=pl.ANY)] * count,
         out_shape=[jax.ShapeDtypeStruct((items, rows, width), packed.dtype)] * count,
+        scratch_shapes=[
+            pltpu.VMEM((count, rows, width), packed.dtype),
+            pltpu.SemaphoreType.DMA((groups, count)),
+        ],
         cost_estimate=pl.CostEstimate(
             flops=0, bytes_accessed=4 * count * rows * width, transcendentals=0
         ),
+        compiler_params=pltpu.CompilerParams(vmem_limit_bytes=8 * 1024 * 1024),
         name="unpack",
         **kwargs,
     )(*operands)
@@ -89,7 +128,7 @@
     return parts[0]
 
 
-def _attend_kernel(x_ref, bias_ref, y_ref, sums_ref, q_s, kt_s, s_s, dp_s, dk_s, dv_s):
+def _attend_kernel(x_ref, bias_ref, prior_ref, y_ref, sums_ref, q_s, kt_s, s_s, dp_s, dk_s, dv_s):
     peers, _, rows, _ = x_ref.shape
     blocks = peers * rows // TILE
     per = TILE // rows
@@ -104,7 +143,7 @@
 
     key_id = lax.broadcasted_iota(jnp.int32, (TILE, TILE), 0)
     query_id = lax.broadcasted_iota(jnp.int32, (TILE, TILE), 1)
-    sums = jnp.zeros((8, HDIM), jnp.float32)
+    sums = prior_ref[...]
     for i in range(blocks):
         q_i = q_s[i]
         g_i = piece(3, i)
@@ -148,21 +187,21 @@
     for j in range(blocks):
         y_ref[j * per : (j + 1) * per, 1] = dk_s[j].astype(jnp.bfloat16).reshape(per, rows, HDIM)
         y_ref[j * per : (j + 1) * per, 2] = dv_s[j].astype(jnp.bfloat16).reshape(per, rows, HDIM)
-    sums_ref[...] = jnp.sum(sums, axis=0, keepdims=True)
-
-
-def attend(x, bias):
+    sums_ref[...] = sums
+
+
+def attend(x, bias, prior):
     peers, _, rows, _ = x.shape
     seq = peers * rows
     blocks = seq // TILE
     area = seq * (seq + TILE) // 2
     return pl.pallas_call(
         _attend_kernel,
-        in_specs=[pl.BlockSpec(memory_space=pltpu.VMEM)] * 2,
+        in_specs=[pl.BlockSpec(memory_space=pltpu.VMEM)] * 3,
         out_specs=[pl.BlockSpec(memory_space=pltpu.VMEM)] * 2,
         out_shape=[
             jax.ShapeDtypeStruct((peers, 3, rows, HDIM), jnp.bfloat16),
-            jax.ShapeDtypeStruct((1, HDIM), jnp.float32),
+            jax.ShapeDtypeStruct((8, HDIM), jnp.float32),
         ],
         scratch_shapes=[
             pltpu.VMEM((blocks, TILE, HDIM), jnp.bfloat16),
@@ -177,39 +216,42 @@
             flops=10 * area * HDIM * 2, bytes_accessed=14 * seq * HDIM, transcendentals=area
         ),
         name="attend",
-    )(x, bias)
+    )(x, bias, prior)
 
 
 def spread_sum(x, size):
-    step = 1
-    while step < size:
-        x = x + lax.ppermute(x, "dp", [(d, d ^ step) for d in range(size)])
-        step *= 2
-    return x
+    pair = x + lax.ppermute(x, "dp", [(d, d ^ 1) for d in range(size)])
+    parts = [pair]
+    for step in range(2, size, 2):
+        parts.append(lax.ppermute(pair, "dp", [(d, d ^ step) for d in range(size)]))
+    return sum(parts[1:], parts[0])
 
 
 def body(queries, key_states, value_states, grad_output, query_bias, *, dp_size):
     items, rows, width = queries.shape
     inputs = (queries, key_states, value_states, grad_output)
+    share = query_bias.shape[0]
     me = lax.axis_index("dp")
-    share = query_bias.shape[0]
 
     own = lax.broadcasted_iota(jnp.int32, (dp_size, share), 0) == me
     slots = jnp.where(own, query_bias[None, :], jnp.zeros((), query_bias.dtype))
     bias = spread_sum(slots, dp_size).astype(jnp.float32).reshape(1, dp_size * share)
 
-    sums = None
+    sums = jnp.zeros((8, HDIM), jnp.float32)
     results = []
     for item in range(items):
-        packed = pack(inputs, item, 8)
+        packed = pack(inputs, item, 4)
+        if item == 1:
+            packed, bias = lax.optimization_barrier((packed, bias))
         moved = lax.all_to_all(packed, "seq", split_axis=0, concat_axis=0, tiled=True)
-        grads, part = attend(moved, bias)
-        sums = part if sums is None else sums + part
+        grads, sums = attend(moved, bias, sums)
         results.append(lax.all_to_all(grads, "seq", split_axis=0, concat_axis=0, tiled=True))
     outs = None
     for item, packed in enumerate(results):
-        outs = unpack(packed, item, items, 8, into=outs)
-    total = spread_sum(sums.reshape(dp_size, share), dp_size)
+        outs = unpack(packed, item, items, 4, into=outs)
+        if item == 0:
+            outs, sums = lax.optimization_barrier((outs, sums))
+    total = spread_sum(jnp.sum(sums, axis=0).reshape(dp_size, share), dp_size)
     grad_bias = lax.dynamic_index_in_dim(total, me, 0, keepdims=False)
     return (*outs, grad_bias)
 

time: 162 us -> 134 us (0.83)
  waiting for transfers between devices: 69.6 us -> 59.2 us
  starting transfers between devices: 48.8 us -> 41.5 us
  Pallas kernels: 34.4 us -> 28.6 us
  local copies, waits for them, and re-layouts: 7.04 us -> 3.05 us
    ppermute x6 -> x8, waiting for transfers between devices: 37.1 us -> 21.7 us  [the longest x6 19.4 us: spread_sum(): parts.append(lax.ppermute(pair, 'dp', [(d, d ^ step) for d in range(size)]))]
    all_to_all x2, waiting for transfers between devices: 7.44 us -> 18.8 us  [body(): lax.all_to_all(grads, 'seq', split_axis=0, concat_axis=0, tiled=True)]
    all_to_all x2, starting transfers between devices: 18.2 us -> 9.85 us  [body(): lax.all_to_all(grads, 'seq', split_axis=0, concat_axis=0, tiled=True)]
    pallas_call x4, Pallas kernels: 15.2 us -> 7.81 us  [the longest x2 5.29 us: pack(): pl.pallas_call(functools.partial(_pack_kernel, item, count, groups), in_s...]
    all_to_all x2, waiting for transfers between devices: 25 us -> 18.7 us  [body(): lax.all_to_all(packed, 'seq', split_axis=0, concat_axis=0, tiled=True)]
    unnamed x12 -> x6, local copies, waits for them, and re-layouts: 6.36 us -> 2.36 us
    ppermute x6 -> x8, starting transfers between devices: 14.7 us -> 14.3 us  [the longest x6 14.3 us: spread_sum(): parts.append(lax.ppermute(pair, 'dp', [(d, d ^ step) for d in range(size)]))]
  transfers between devices with their start and end apart: 10 -> 12, of which waited for: 8 -> 7; matrix products, arithmetic and copies ran while one was open for 1% -> 0% of each run, Pallas kernels for 17% -> 19%
where the time goes in v2:
time: 134 us; the launch traced here: 133 us
  waiting for transfers between devices  59.2 us (44%)
  starting transfers between devices  41.5 us (31%)
  Pallas kernels  28.6 us (21%)
  local copies, waits for them, and re-layouts  3.05 us (2%)
    pallas_call x2, Pallas kernels, attend(): pl.pallas_call(_attend_kernel, in_specs=[pl.BlockSpec(memory_space=pltpu....  20.8 us
    ppermute x6, waiting for transfers between devices, spread_sum(): parts.append(lax.ppermute(pair, 'dp', [(d, d ^ step) for d in range(size)]))  19.4 us
    all_to_all x2, waiting for transfers between devices, body(): lax.all_to_all(grads, 'seq', split_axis=0, concat_axis=0, tiled=True)  18.8 us
    all_to_all x2, waiting for transfers between devices, body(): lax.all_to_all(packed, 'seq', split_axis=0, concat_axis=0, tiled=True)  18.7 us
    all_to_all x2, starting transfers between devices, body(): lax.all_to_all(packed, 'seq', split_axis=0, concat_axis=0, tiled=True)  17.3 us
    ppermute x6, starting transfers between devices, spread_sum(): parts.append(lax.ppermute(pair, 'dp', [(d, d ^ step) for d in range(size)]))  14.3 us
    all_to_all x2, starting transfers between devices, body(): lax.all_to_all(grads, 'seq', split_axis=0, concat_axis=0, tiled=True)  9.85 us
    pallas_call x2, Pallas kernels, pack(): pl.pallas_call(functools.partial(_pack_kernel, item, count, groups), in_s...  5.29 us
  transfers between devices with their start and end apart: 12, of which 7 were waited for; matrix products, arithmetic and copies ran while one was open for 0% of the time, Pallas kernels for 19%

profile of v2, /device:TPU:8, one launch (start us, length us, event | category | flops | bytes accessed | tf_op | source)
XLA Modules:
  0.0 133.3 jit_solution(5954949549968147150)
XLA Ops:
  0.6 2.6 %pack.3 = bf16[32,4,64,128]{3,2,1,0:T(8,128)(2,1)} custom-call(bf16[2,64,4096]{2,1,0:T(8,128)(2,1)} %refs_0_.3, bf16[2,64,4096]{2,1,0:T(8,128)(2,1)} %refs_1_.3, bf16[2,64,4096]{2,1,0:T(8,128)(2,1)} %refs_2_.3, bf16[2,64,4096]{2,1,0:T(8,128)(2,1)} %refs_3_.3), custom_call_target="tpu_custom_call" | custom-call | bytes 4194304 | tf_op jit(solution)/shard_map/pack/pallas_call | solution.py:49
  3.3 8.9 %all-to-all-start.1 = ((bf16[32,4,64,128]{3,2,1,0:T(8,128)(2,1)}), bf16[32,4,64,128]{3,2,1,0:T(8,128)(2,1)S(1)}, u32[]{:S(2)}, u32[]{:S(2)}) async-start(bf16[32,4,64,128]{3,2,1,0:T(8,128)(2,1)} %pack.3), calls=%async_computation.1 | async-start | bytes 4194304 | tf_op jit(solution)/shard_map/all_to_all | solution.py:246
  12.3 1.1 collective-permute-done
  13.6 3.3 %collective-permute-start.1 = (bf16[8,16]{1,0:T(8,128)(2,1)S(1)}, bf16[8,16]{1,0:T(8,128)(2,1)S(1)}, u32[]{:S(2)}, u32[]{:S(2)}) collective-permute-start(bf16[8,16]{1,0:T(8,128)(2,1)S(1)} %fusion), channel_id=1, source_target_pairs={{0,2},{1,3},{2,0},{3,1},{4,6},{5,7},{6,4},{7,5},{8,10},{9,11},{10,... | collective-permute-start | bytes 776 | tf_op jit(solution)/shard_map/ppermute | solution.py:226
  16.8 4.5 %collective-permute-start.2 = (bf16[8,16]{1,0:T(8,128)(2,1)S(1)}, bf16[8,16]{1,0:T(8,128)(2,1)S(1)}, u32[]{:S(2)}, u32[]{:S(2)}) collective-permute-start(bf16[8,16]{1,0:T(8,128)(2,1)S(1)} %fusion), channel_id=1, source_target_pairs={{0,4},{1,5},{2,6},{3,7},{4,0},{5,1},{6,2},{7,3},{8,12},{9,13},{10,... | collective-permute-start | bytes 776 | tf_op jit(solution)/shard_map/ppermute | solution.py:226
  21.3 2.7 %pack.2 = bf16[32,4,64,128]{3,2,1,0:T(8,128)(2,1)} custom-call(bf16[2,64,4096]{2,1,0:T(8,128)(2,1)} %refs_0_.3, bf16[2,64,4096]{2,1,0:T(8,128)(2,1)} %refs_1_.3, bf16[2,64,4096]{2,1,0:T(8,128)(2,1)} %refs_2_.3, bf16[2,64,4096]{2,1,0:T(8,128)(2,1)} %refs_3_.3), custom_call_target="tpu_custom_call" | custom-call | bytes 4194304 | tf_op jit(solution)/shard_map/pack/pallas_call | solution.py:49
  24.0 12.7 %collective-permute-done.1 = bf16[8,16]{1,0:T(8,128)(2,1)S(1)} collective-permute-done((bf16[8,16]{1,0:T(8,128)(2,1)S(1)}, bf16[8,16]{1,0:T(8,128)(2,1)S(1)}, u32[]{:S(2)}, u32[]{:S(2)}) %collective-permute-start.1) | collective-permute-done | bytes 288 | tf_op jit(solution)/shard_map/ppermute | solution.py:226
  36.7 6.7 %collective-permute-done.2 = bf16[8,16]{1,0:T(8,128)(2,1)S(1)} collective-permute-done((bf16[8,16]{1,0:T(8,128)(2,1)S(1)}, bf16[8,16]{1,0:T(8,128)(2,1)S(1)}, u32[]{:S(2)}, u32[]{:S(2)}) %collective-permute-start.2) | collective-permute-done | bytes 288 | tf_op jit(solution)/shard_map/ppermute | solution.py:226
  43.6 8.4 %all-to-all-start = ((bf16[32,4,64,128]{3,2,1,0:T(8,128)(2,1)}), bf16[32,4,64,128]{3,2,1,0:T(8,128)(2,1)}, u32[]{:S(2)}, u32[]{:S(2)}) async-start(bf16[32,4,64,128]{3,2,1,0:T(8,128)(2,1)} %pack.2), calls=%async_computation | async-start | bytes 4194304 | tf_op jit(solution)/shard_map/all_to_all | solution.py:246
  52.0 9.6 %attend.2 = (bf16[32,3,64,128]{3,2,1,0:T(8,128)(2,1)S(1)}, f32[8,128]{1,0:T(8,128)S(1)}) custom-call(bf16[32,4,64,128]{3,2,1,0:T(8,128)(2,1)S(1)} %all-to-all-done.1.x_ref, f32[1,128]{1,0:T(1,128)S(1)} %reshape.21.bias_ref, f32[8,128]{1,0:T(8,128)S(1)} %broadcast_in_dim.18.prior_ref), custom_call_target="tpu_custom_call" | custom-call | flops 6039797760 | bytes 3670016 | tf_op jit(solution)/shard_map/attend/pallas_call | solution.py:198
  61.6 1.2 copy-done.1
  62.7 18.6 %all-to-all-done.x_ref = bf16[32,4,64,128]{3,2,1,0:T(8,128)(2,1)} async-done(((bf16[32,4,64,128]{3,2,1,0:T(8,128)(2,1)}), bf16[32,4,64,128]{3,2,1,0:T(8,128)(2,1)}, u32[]{:S(2)}, u32[]{:S(2)}) %all-to-all-start) | async-done | bytes 2097184 | tf_op jit(solution)/shard_map/all_to_all | solution.py:246
  81.4 4.8 %all-to-all-start.3 = ((bf16[32,3,64,128]{3,2,1,0:T(8,128)(2,1)}), bf16[32,3,64,128]{3,2,1,0:T(8,128)(2,1)S(1)}, u32[]{:S(2)}, u32[]{:S(2)}) async-start(bf16[32,3,64,128]{3,2,1,0:T(8,128)(2,1)} %copy-done.1), calls=%async_computation.3 | async-start | bytes 3145728 | tf_op jit(solution)/shard_map/all_to_all | solution.py:248
  86.2 11.2 %attend.3 = (bf16[32,3,64,128]{3,2,1,0:T(8,128)(2,1)S(1)}, f32[8,128]{1,0:T(8,128)S(1)}) custom-call(bf16[32,4,64,128]{3,2,1,0:T(8,128)(2,1)} %all-to-all-done.x_ref, f32[1,128]{1,0:T(1,128)S(1)} %reshape.21.bias_ref, f32[8,128]{1,0:T(8,128)S(1)} %get-tuple-element.22.prior_ref), custom_call_target="tpu_custom_call" | custom-call | flops 6039797760 | bytes 3670016 | tf_op jit(solution)/shard_map/attend/pallas_call | solution.py:198
  97.4 1.2 copy-done
  98.5 7.7 %all-to-all-done.3.refs_0_ = bf16[32,3,64,128]{3,2,1,0:T(8,128)(2,1)S(1)} async-done(((bf16[32,3,64,128]{3,2,1,0:T(8,128)(2,1)}), bf16[32,3,64,128]{3,2,1,0:T(8,128)(2,1)S(1)}, u32[]{:S(2)}, u32[]{:S(2)}) %all-to-all-start.3) | async-done | bytes 1572896 | tf_op jit(solution)/shard_map/all_to_all | solution.py:248
  106.2 5.1 %all-to-all-start.2 = ((bf16[32,3,64,128]{3,2,1,0:T(8,128)(2,1)}), bf16[32,3,64,128]{3,2,1,0:T(8,128)(2,1)S(1)}, u32[]{:S(2)}, u32[]{:S(2)}) async-start(bf16[32,3,64,128]{3,2,1,0:T(8,128)(2,1)} %copy-done), calls=%async_computation.2 | async-start | bytes 3145728 | tf_op jit(solution)/shard_map/all_to_all | solution.py:248
  111.3 1.3 unpack.2
  112.7 1.2 collective-permute-done.4
  113.9 2.8 %collective-permute-start.5 = (f32[8,16]{1,0:T(8,128)S(1)}, f32[8,16]{1,0:T(8,128)S(1)}, u32[]{:S(2)}, u32[]{:S(2)}) collective-permute-start(f32[8,16]{1,0:T(8,128)S(1)} %add.32), channel_id=1, source_target_pairs={{0,2},{1,3},{2,0},{3,1},{4,6},{5,7},{6,4},{7,5},{8,10},{9,11},{10,... | collective-permute-start | bytes 1544 | tf_op jit(solution)/shard_map/ppermute | solution.py:226
  116.7 1.1 collective-permute-start.6
  117.8 2.6 %collective-permute-start.7 = (f32[8,16]{1,0:T(8,128)S(1)}, f32[8,16]{1,0:T(8,128)S(1)}, u32[]{:S(2)}, u32[]{:S(2)}) collective-permute-start(f32[8,16]{1,0:T(8,128)S(1)} %add.32), channel_id=1, source_target_pairs={{0,6},{1,7},{2,4},{3,5},{4,2},{5,3},{6,0},{7,1},{8,14},{9,15},{10,... | collective-permute-start | bytes 1544 | tf_op jit(solution)/shard_map/ppermute | solution.py:226
  120.3 11.1 %all-to-all-done.2.refs_0_ = bf16[32,3,64,128]{3,2,1,0:T(8,128)(2,1)S(1)} async-done(((bf16[32,3,64,128]{3,2,1,0:T(8,128)(2,1)}), bf16[32,3,64,128]{3,2,1,0:T(8,128)(2,1)S(1)}, u32[]{:S(2)}, u32[]{:S(2)}) %all-to-all-start.2) | async-done | bytes 1572896 | tf_op jit(solution)/shard_map/all_to_all | solution.py:248
  131.5 1.3 unpack.3
  (23 shorter events, 1.0 us)
Async XLA Ops:
  3.3 8.9 %copy-start.2 = (bf16[16]{0:T(256)(128)(2,1)S(1)}, bf16[16]{0:T(256)(128)(2,1)}, u32[]{:S(2)}) copy-start(bf16[16]{0:T(256)(128)(2,1)} %param.9) | copy-start | bytes 100
  3.3 40.3 %all-to-all-start.1 = ((bf16[32,4,64,128]{3,2,1,0:T(8,128)(2,1)}), bf16[32,4,64,128]{3,2,1,0:T(8,128)(2,1)S(1)}, u32[]{:S(2)}, u32[]{:S(2)}) async-start(bf16[32,4,64,128]{3,2,1,0:T(8,128)(2,1)} %pack.3), calls=%async_computation.1 | async-start | bytes 4194304 | tf_op jit(solution)/shard_map/all_to_all | solution.py:246
  12.3 1.2 collective-permute-start
  13.6 23.1 %collective-permute-start.1 = (bf16[8,16]{1,0:T(8,128)(2,1)S(1)}, bf16[8,16]{1,0:T(8,128)(2,1)S(1)}, u32[]{:S(2)}, u32[]{:S(2)}) collective-permute-start(bf16[8,16]{1,0:T(8,128)(2,1)S(1)} %fusion), channel_id=1, source_target_pairs={{0,2},{1,3},{2,0},{3,1},{4,6},{5,7},{6,4},{7,5},{8,10},{9,11},{10,... | collective-permute-start | bytes 776 | tf_op jit(solution)/shard_map/ppermute | solution.py:226
  16.8 26.6 %collective-permute-start.2 = (bf16[8,16]{1,0:T(8,128)(2,1)S(1)}, bf16[8,16]{1,0:T(8,128)(2,1)S(1)}, u32[]{:S(2)}, u32[]{:S(2)}) collective-permute-start(bf16[8,16]{1,0:T(8,128)(2,1)S(1)} %fusion), channel_id=1, source_target_pairs={{0,4},{1,5},{2,6},{3,7},{4,0},{5,1},{6,2},{7,3},{8,12},{9,13},{10,... | collective-permute-start | bytes 776 | tf_op jit(solution)/shard_map/ppermute | solution.py:226
  21.3 22.1 %collective-permute-start.3 = (bf16[8,16]{1,0:T(8,128)(2,1)S(1)}, bf16[8,16]{1,0:T(8,128)(2,1)S(1)}, u32[]{:S(2)}, u32[]{:S(2)}) collective-permute-start(bf16[8,16]{1,0:T(8,128)(2,1)S(1)} %fusion), channel_id=1, source_target_pairs={{0,6},{1,7},{2,4},{3,5},{4,2},{5,3},{6,0},{7,1},{8,14},{9,15},{10,... | collective-permute-start | bytes 776 | tf_op jit(solution)/shard_map/ppermute | solution.py:226
  43.6 37.8 %all-to-all-start = ((bf16[32,4,64,128]{3,2,1,0:T(8,128)(2,1)}), bf16[32,4,64,128]{3,2,1,0:T(8,128)(2,1)}, u32[]{:S(2)}, u32[]{:S(2)}) async-start(bf16[32,4,64,128]{3,2,1,0:T(8,128)(2,1)} %pack.2), calls=%async_computation | async-start | bytes 4194304 | tf_op jit(solution)/shard_map/all_to_all | solution.py:246
  61.5 1.2 copy-start.1
  81.4 24.8 %all-to-all-start.3 = ((bf16[32,3,64,128]{3,2,1,0:T(8,128)(2,1)}), bf16[32,3,64,128]{3,2,1,0:T(8,128)(2,1)S(1)}, u32[]{:S(2)}, u32[]{:S(2)}) async-start(bf16[32,3,64,128]{3,2,1,0:T(8,128)(2,1)} %copy-done.1), calls=%async_computation.3 | async-start | bytes 3145728 | tf_op jit(solution)/shard_map/all_to_all | solution.py:248
  97.4 1.2 copy-start
  106.2 25.3 %all-to-all-start.2 = ((bf16[32,3,64,128]{3,2,1,0:T(8,128)(2,1)}), bf16[32,3,64,128]{3,2,1,0:T(8,128)(2,1)S(1)}, u32[]{:S(2)}, u32[]{:S(2)}) async-start(bf16[32,3,64,128]{3,2,1,0:T(8,128)(2,1)} %copy-done), calls=%async_computation.2 | async-start | bytes 3145728 | tf_op jit(solution)/shard_map/all_to_all | solution.py:248
  112.7 1.2 collective-permute-start.4
  113.9 18.9 %collective-permute-start.5 = (f32[8,16]{1,0:T(8,128)S(1)}, f32[8,16]{1,0:T(8,128)S(1)}, u32[]{:S(2)}, u32[]{:S(2)}) collective-permute-start(f32[8,16]{1,0:T(8,128)S(1)} %add.32), channel_id=1, source_target_pairs={{0,2},{1,3},{2,0},{3,1},{4,6},{5,7},{6,4},{7,5},{8,10},{9,11},{10,... | collective-permute-start | bytes 1544 | tf_op jit(solution)/shard_map/ppermute | solution.py:226
  116.7 16.1 %collective-permute-start.6 = (f32[8,16]{1,0:T(8,128)S(1)}, f32[8,16]{1,0:T(8,128)S(1)}, u32[]{:S(2)}, u32[]{:S(2)}) collective-permute-start(f32[8,16]{1,0:T(8,128)S(1)} %add.32), channel_id=1, source_target_pairs={{0,4},{1,5},{2,6},{3,7},{4,0},{5,1},{6,2},{7,3},{8,12},{9,13},{10,... | collective-permute-start | bytes 1544 | tf_op jit(solution)/shard_map/ppermute | solution.py:226
  117.8 15.0 %collective-permute-start.7 = (f32[8,16]{1,0:T(8,128)S(1)}, f32[8,16]{1,0:T(8,128)S(1)}, u32[]{:S(2)}, u32[]{:S(2)}) collective-permute-start(f32[8,16]{1,0:T(8,128)S(1)} %add.32), channel_id=1, source_target_pairs={{0,6},{1,7},{2,4},{3,5},{4,2},{5,3},{6,0},{7,1},{8,14},{9,15},{10,... | collective-permute-start | bytes 1544 | tf_op jit(solution)/shard_map/ppermute | solution.py:226

commit v3 on v2

v3 whole, which is shorter than its diff:
```python
import functools
import math

import jax
import jax.numpy as jnp
from jax import lax
from jax.experimental import pallas as pl
from jax.experimental.pallas import tpu as pltpu
from jax.sharding import PartitionSpec as P

HDIM = 128
TILE = 256
MASKED = -1e30
IN_CHUNKS = ((0, 1),)
OUT_CHUNKS = ((0, 1),)
GATE = -1


def _pack_kernel(items, count, groups, *refs):
    srcs, out_ref = refs[:count], refs[count]
    in_s, out_s, in_sem, out_sem = refs[count + 1 :]
    heads = out_ref.shape[0] // groups

    def load(c, n, t):
        cols = pl.ds(c * heads * HDIM, heads * HDIM)
        return pltpu.make_async_copy(
            srcs[t].at[items[n], :, cols], in_s.at[n * count + t, :, cols], in_sem.at[c, n, t]
        )

    def store(c):
        span = pl.ds(c * heads, heads)
        return pltpu.make_async_copy(out_s.at[span], out_ref.at[span], out_sem.at[c])

    places = [(n, t) for n in range(len(items)) for t in range(count)]
    for c in range(groups):
        for n, t in places:
            load(c, n, t).start()
    for c in range(groups):
        for n, t in places:
            load(c, n, t).wait()
            for h in range(c * heads, (c + 1) * heads):
                out_s[h, n * count + t] = in_s[n * count + t, :, h * HDIM : (h + 1) * HDIM]
        store(c).start()
    for c in range(groups):
        store(c).wait()


def pack(arrays, items, groups):
    _, rows, width = arrays[0].shape
    heads = width // HDIM
    count = len(arrays)
    total = count * len(items)
    dtype = arrays[0].dtype
    return pl.pallas_call(
        functools.partial(_pack_kernel, items, count, groups),
        in_specs=[pl.BlockSpec(memory_space=pl.ANY)] * count,
        out_specs=pl.BlockSpec(memory_space=pl.ANY),
        out_shape=jax.ShapeDtypeStruct((heads, total, rows, HDIM), dtype),
        scratch_shapes=[
            pltpu.VMEM((total, rows, width), dtype),
            pltpu.VMEM((heads, total, rows, HDIM), dtype),
            pltpu.SemaphoreType.DMA((groups, len(items), count)),
            pltpu.SemaphoreType.DMA((groups,)),
        ],
        cost_estimate=pl.CostEstimate(
            flops=0, bytes_accessed=4 * total * rows * width, transcendentals=0
        ),
        compiler_params=pltpu.CompilerParams(vmem_limit_bytes=56 * 1024 * 1024),
        name="pack",
    )(*arrays)


def _unpack_kernel(items, count, groups, *refs):
    in_ref, outs = refs[0], refs[-count - 2 : -2]
    out_s, out_sem = refs[-2:]
    heads = in_ref.shape[0] // groups

    def store(c, n, t):
        cols = pl.ds(c * heads * HDIM, heads * HDIM)
        return pltpu.make_async_copy(
            out_s.at[n * count + t, :, cols], outs[t].at[items[n], :, cols], out_sem.at[c, n, t]
        )

    places = [(n, t) for n in range(len(items)) for t in range(count)]
    for c in range(groups):
        for n, t in places:
            for h in range(c * heads, (c + 1) * heads):
                out_s[n * count + t, :, h * HDIM : (h + 1) * HDIM] = in_ref[h, n * count + t]
            store(c, n, t).start()
    for c in range(groups):
        for n, t in places:
            store(c, n, t).wait()


def unpack(packed, items, count, all_items, groups, into=None):
    heads, total, rows, _ = packed.shape
    width = heads * HDIM
    kwargs = {}
    operands = [packed]
    if into is not None:
        operands += list(into)
        kwargs["input_output_aliases"] = {1 + t: t for t in range(count)}
    return pl.pallas_call(
        functools.partial(_unpack_kernel, items, count, groups),
        in_specs=[pl.BlockSpec(memory_space=pltpu.VMEM)]
        + [pl.BlockSpec(memory_space=pl.ANY)] * (len(operands) - 1),
        out_specs=[pl.BlockSpec(memory_space=pl.ANY)] * count,
        out_shape=[jax.ShapeDtypeStruct((all_items, rows, width), packed.dtype)] * count,
        scratch_shapes=[
            pltpu.VMEM((total, rows, width), packed.dtype),
            pltpu.SemaphoreType.DMA((groups, len(items), count)),
        ],
        cost_estimate=pl.CostEstimate(
            flops=0, bytes_accessed=4 * total * rows * width, transcendentals=0
        ),
        compiler_params=pltpu.CompilerParams(vmem_limit_bytes=8 * 1024 * 1024),
        name="unpack",
        **kwargs,
    )(*operands)


def _dot_nt(a, b):
    return lax.dot_general(a, b, (((1,), (1,)), ((), ())), preferred_element_type=jnp.float32)


def _dot(a, b):
    return jnp.dot(a, b, preferred_element_type=jnp.float32)


def _fold(x, op):
    parts = [x[r : r + 8] for r in range(0, x.shape[0], 8)]
    out = parts[0]
    for part in parts[1:]:
        out = op(out, part)
    return out


def _attend_kernel(
    items,
    x_hbm,
    bias_ref,
    prior_ref,
    y_hbm,
    sums_ref,
    x_ref,
    y_ref,
    q_s,
    kt_s,
    qt_s,
    gt_s,
    s_s,
    dp_s,
    dk_s,
    dv_s,
    in_sem,
    out_sem,
):
    peers, _, rows, _ = x_ref.shape
    blocks = peers * rows // TILE
    per = TILE // rows
    factor = 1.0 / math.sqrt(HDIM)
    scale = factor * math.log2(math.e)
    key_id = lax.broadcasted_iota(jnp.int32, (TILE, TILE), 0)
    query_id = lax.broadcasted_iota(jnp.int32, (TILE, TILE), 1)
    state = {}
    total_sums = [prior_ref[...]]

    def load(n, i):
        place = (pl.ds(i * per, per), pl.ds(4 * n, 4))
        return pltpu.make_async_copy(x_hbm.at[place], x_ref.at[place], in_sem.at[n, i])

    def store(n, i):
        place = (pl.ds(i * per, per), pl.ds(3 * n, 3))
        return pltpu.make_async_copy(y_ref.at[place], y_hbm.at[place], out_sem.at[n, i])

    def piece(n, t, i):
        return x_ref[i * per : (i + 1) * per, 4 * n + t].reshape(TILE, HDIM)

    def score(step, n, i, j):
        if j == 0:
            load(n, i).wait()
            q_s[n, i] = (piece(n, 0, i).astype(jnp.float32) + bias_ref[...]).astype(jnp.bfloat16)
            kt_s[n, i] = piece(n, 1, i).T
            qt_s[step % 3] = q_s[n, i].T
            gt_s[step % 3] = piece(n, 3, i).T
        s = _dot(piece(n, 1, j), qt_s[step % 3])
        if j == i:
            s = jnp.where(key_id <= query_id, s, MASKED)
        s_s[step % 3, j] = s
        part = _fold(s, jnp.maximum)
        top = part if j == 0 else jnp.maximum(state[step, "top"], part)
        if j == i:
            top = jnp.max(top, axis=0, keepdims=True) * scale
        state[step, "top"] = top

    def weigh(step, n, i, j):
        e = jnp.exp2(s_s[step % 3, j] * scale - state[step, "top"])
        dp = _dot(piece(n, 2, j), gt_s[step % 3])
        s_s[step % 3, j] = e
        dp_s[step % 2, j] = dp
        total, row_dot = _fold(e, jnp.add), _fold(e * dp, jnp.add)
        if j > 0:
            total, row_dot = total + state[step, "total"], row_dot + state[step, "dot"]
        if j == i:
            total = 1.0 / jnp.sum(total, axis=0, keepdims=True)
            row_dot = jnp.sum(row_dot, axis=0, keepdims=True) * total
        state[step, "total"], state[step, "dot"] = total, row_dot

    def spread(step, n, i, j):
        p = s_s[step % 3, j] * state[step, "total"]
        ds = (p * (dp_s[step % 2, j] - state[step, "dot"]) * factor).astype(jnp.bfloat16)
        dv = _dot_nt(gt_s[step % 3], p.astype(jnp.bfloat16))
        dk = _dot_nt(qt_s[step % 3], ds)
        dq = _dot(kt_s[n, j], ds)
        if j > 0:
            dq = state[step, "dq"] + dq
        state[step, "dq"] = dq
        if i < blocks - 1:
            if j == i:
                dv_s[n, j] = dv
                dk_s[n, j] = dk
            else:
                dv_s[n, j] += dv
                dk_s[n, j] += dk
        else:
            if j < i:
                dv = dv_s[n, j] + dv
                dk = dk_s[n, j] + dk
            span = slice(j * per, (j + 1) * per)
            y_ref[span, 3 * n + 1] = dk.T.astype(jnp.bfloat16).reshape(per, rows, HDIM)
            y_ref[span, 3 * n + 2] = dv.T.astype(jnp.bfloat16).reshape(per, rows, HDIM)
        if j == i:
            dq = dq.T
            total_sums[0] = total_sums[0] + _fold(dq, jnp.add)
            span = slice(i * per, (i + 1) * per)
            y_ref[span, 3 * n] = dq.astype(jnp.bfloat16).reshape(per, rows, HDIM)
        if i == blocks - 1:
            store(n, j).start()

    order = [(n, i) for n in range(items) for i in range(blocks)]
    for n, i in order:
        load(n, i).start()
    for step in range(len(order) + 2):
        stages = []
        for lag, fn in ((2, spread), (1, weigh), (0, score)):
            if 0 <= step - lag < len(order):
                stages.append((fn, step - lag, *order[step - lag]))
        for j in range(blocks):
            for fn, at, n, i in stages:
                if j <= i:
                    fn(at, n, i, j)
    sums_ref[...] = total_sums[0]
    for n, i in order:
        store(n, i).wait()


def attend(x, bias, prior, items):
    peers, _, rows, _ = x.shape
    seq = peers * rows
    blocks = seq // TILE
    area = items * seq * (seq + TILE) // 2
    return pl.pallas_call(
        functools.partial(_attend_kernel, items),
        in_specs=[pl.BlockSpec(memory_space=pl.ANY)] + [pl.BlockSpec(memory_space=pltpu.VMEM)] * 2,
        out_specs=[pl.BlockSpec(memory_space=pl.ANY), pl.BlockSpec(memory_space=pltpu.VMEM)],
        out_shape=[
            jax.ShapeDtypeStruct((peers, 3 * items, rows, HDIM), jnp.bfloat16),
            jax.ShapeDtypeStruct((8, HDIM), jnp.float32),
        ],
        scratch_shapes=[
            pltpu.VMEM(x.shape, x.dtype),
            pltpu.VMEM((peers, 3 * items, rows, HDIM), jnp.bfloat16),
            pltpu.VMEM((items, blocks, TILE, HDIM), jnp.bfloat16),
            pltpu.VMEM((items, blocks, HDIM, TILE), jnp.bfloat16),
            pltpu.VMEM((3, HDIM, TILE), jnp.bfloat16),
            pltpu.VMEM((3, HDIM, TILE), jnp.bfloat16),
            pltpu.VMEM((3, blocks, TILE, TILE), jnp.float32),
            pltpu.VMEM((2, blocks, TILE, TILE), jnp.float32),
            pltpu.VMEM((items, blocks, HDIM, TILE), jnp.float32),
            pltpu.VMEM((items, blocks, HDIM, TILE), jnp.float32),
            pltpu.SemaphoreType.DMA((items, blocks)),
            pltpu.SemaphoreType.DMA((items, blocks)),
        ],
        compiler_params=pltpu.CompilerParams(vmem_limit_bytes=56 * 1024 * 1024),
        cost_estimate=pl.CostEstimate(
            flops=10 * area * HDIM, bytes_accessed=14 * items * seq * HDIM, transcendentals=area
        ),
        name="attend",
    )(x, bias, prior)


def spread_sum(x, size):
    pair = x + lax.ppermute(x, "dp", [(d, d ^ 1) for d in range(size)])
    parts = [pair]
    for step in range(2, size, 2):
        parts.append(lax.ppermute(pair, "dp", [(d, d ^ step) for d in range(size)]))
    return sum(parts[1:], parts[0])


def body(queries, key_states, value_states, grad_output, query_bias, *, dp_size):
    items, rows, width = queries.shape
    inputs = (queries, key_states, value_states, grad_output)
    share = query_bias.shape[0]
    me = lax.axis_index("dp")

    own = lax.broadcasted_iota(jnp.int32, (dp_size, share), 0) == me
    slots = jnp.where(own, query_bias[None, :], jnp.zeros((), query_bias.dtype))
    bias = spread_sum(slots, dp_size).astype(jnp.float32).reshape(1, dp_size * share)

    sums = jnp.zeros((8, HDIM), jnp.float32)
    received = {}
    for first, chunk in enumerate(IN_CHUNKS):
        packed = pack(inputs, chunk, 4)
        if GATE == first:
            packed, bias = lax.optimization_barrier((packed, bias))
        moved = lax.all_to_all(packed, "seq", split_axis=0, concat_axis=0, tiled=True)
        for n, item in enumerate(chunk):
            received[item] = moved[:, 4 * n : 4 * n + 4]
    outs = None
    for chunk in OUT_CHUNKS:
        x = jnp.concatenate([received[item] for item in chunk], axis=1)
        grads, sums = attend(x, bias, sums, len(chunk))
        packed = lax.all_to_all(grads, "seq", split_axis=0, concat_axis=0, tiled=True)
        outs = unpack(packed, chunk, 3, items, 4, into=outs)
        if chunk[0] == 0 and len(OUT_CHUNKS) > 1:
            outs, sums = lax.optimization_barrier((outs, sums))
    total = spread_sum(jnp.sum(sums, axis=0).reshape(dp_size, share), dp_size)
    grad_bias = lax.dynamic_index_in_dim(total, me, 0, keepdims=False)
    return (*outs, grad_bias)


def solution(mesh):
    rows = P("dp", "seq", None)
    cols = P(("seq", "dp"))
    return jax.shard_map(
        functools.partial(body, dp_size=mesh.shape["dp"]),
        mesh=mesh,
        in_specs=(rows, rows, rows, rows, cols),
        out_specs=(rows, rows, rows, cols),
        check_vma=False,
    )
```

time: 134 us -> 156 us (1.16)
  waiting for transfers between devices: 59.2 us -> 92.1 us
  starting transfers between devices: 41.5 us -> 34.1 us
  Pallas kernels: 28.6 us -> 25.3 us
    ppermute x6, waiting for transfers between devices: 19.4 us -> 79.5 us  [spread_sum(): parts.append(lax.ppermute(pair, 'dp', [(d, d ^ step) for d in range(size)]))]
    all_to_all x2 -> x1, waiting for transfers between devices: 18.8 us -> 4.47 us  [body(): lax.all_to_all(grads, 'seq', split_axis=0, concat_axis=0, tiled=True)]
    all_to_all x2 -> x1, waiting for transfers between devices: 18.7 us -> 5.83 us  [body(): lax.all_to_all(packed, 'seq', split_axis=0, concat_axis=0, tiled=True)]
    all_to_all x2 -> x1, starting transfers between devices: 17.3 us -> 8.95 us  [body(): lax.all_to_all(packed, 'seq', split_axis=0, concat_axis=0, tiled=True)]
    pallas_call x6 -> x3, Pallas kernels: 28.6 us -> 25.3 us  [the longest x1 19.8 us: attend(): pl.pallas_call(functools.partial(_attend_kernel, items), in_specs=[pl.Blo...]
    unnamed x6 -> x4, local copies, waits for them, and re-layouts: 2.36 us -> 0.01 us
    all_to_all x2 -> x1, starting transfers between devices: 9.85 us -> 10.8 us  [body(): lax.all_to_all(grads, 'seq', split_axis=0, concat_axis=0, tiled=True)]
  transfers between devices with their start and end apart: 12 -> 10, of which waited for: 7 -> 8; matrix products, arithmetic and copies ran while one was open for 0% -> 1% of each run, Pallas kernels for 19% -> 0%
where the time goes in v3:
time: 156 us; the launch traced here: 155 us
  waiting for transfers between devices  92.1 us (59%)
  starting transfers between devices  34.1 us (22%)
  Pallas kernels  25.3 us (16%)
  local copies, waits for them, and re-layouts  1.8 us (1%)
    ppermute x6, waiting for transfers between devices, spread_sum(): parts.append(lax.ppermute(pair, 'dp', [(d, d ^ step) for d in range(size)]))  79.5 us
    pallas_call x1, Pallas kernels, attend(): pl.pallas_call(functools.partial(_attend_kernel, items), in_specs=[pl.Blo...  19.8 us
    ppermute x6, starting transfers between devices, spread_sum(): parts.append(lax.ppermute(pair, 'dp', [(d, d ^ step) for d in range(size)]))  14.3 us
    all_to_all x1, starting transfers between devices, body(): lax.all_to_all(grads, 'seq', split_axis=0, concat_axis=0, tiled=True)  10.8 us
    all_to_all x1, starting transfers between devices, body(): lax.all_to_all(packed, 'seq', split_axis=0, concat_axis=0, tiled=True)  8.95 us
    all_to_all x1, waiting for transfers between devices, body(): lax.all_to_all(packed, 'seq', split_axis=0, concat_axis=0, tiled=True)  5.83 us
    all_to_all x1, waiting for transfers between devices, body(): lax.all_to_all(grads, 'seq', split_axis=0, concat_axis=0, tiled=True)  4.47 us
    pallas_call x1, Pallas kernels, pack(): pl.pallas_call(functools.partial(_pack_kernel, items, count, groups), in_...  3.69 us
  transfers between devices with their start and end apart: 10, of which 8 were waited for; matrix products, arithmetic and copies ran while one was open for 1% of the time, Pallas kernels for 0%

profile of v3, /device:TPU:8, one launch (start us, length us, event | category | flops | bytes accessed | tf_op | source)
XLA Modules:
  0.0 154.5 jit_solution(11671856107777988143)
XLA Ops:
  0.6 3.7 %pack.1 = bf16[32,8,64,128]{3,2,1,0:T(8,128)(2,1)} custom-call(bf16[2,64,4096]{2,1,0:T(8,128)(2,1)} %refs_0_.1, bf16[2,64,4096]{2,1,0:T(8,128)(2,1)} %refs_1_.1, bf16[2,64,4096]{2,1,0:T(8,128)(2,1)} %refs_2_.1, bf16[2,64,4096]{2,1,0:T(8,128)(2,1)} %refs_3_.1), custom_call_target="tpu_custom_call" | custom-call | bytes 8388608 | tf_op jit(solution)/shard_map/pack/pallas_call | solution.py:54
  4.3 9.0 %all-to-all-start = ((bf16[32,8,64,128]{3,2,1,0:T(8,128)(2,1)}), bf16[32,8,64,128]{3,2,1,0:T(8,128)(2,1)}, u32[]{:S(2)}, u32[]{:S(2)}) async-start(bf16[32,8,64,128]{3,2,1,0:T(8,128)(2,1)} %pack.1), calls=%async_computation | async-start | bytes 8388608 | tf_op jit(solution)/shard_map/all_to_all | solution.py:316
  13.4 1.1 collective-permute-done
  14.7 5.4 %collective-permute-start.3 = (bf16[8,16]{1,0:T(8,128)(2,1)S(1)}, bf16[8,16]{1,0:T(8,128)(2,1)S(1)}, u32[]{:S(2)}, u32[]{:S(2)}) collective-permute-start(bf16[8,16]{1,0:T(8,128)(2,1)S(1)} %fusion), channel_id=1, source_target_pairs={{0,6},{1,7},{2,4},{3,5},{4,2},{5,3},{6,0},{7,1},{8,14},{9,15},{10,... | collective-permute-start | bytes 776 | tf_op jit(solution)/shard_map/ppermute | solution.py:296
  20.1 1.4 collective-permute-start.2
  21.5 0.9 collective-permute-start.1
  22.5 47.9 %collective-permute-done.3 = bf16[8,16]{1,0:T(8,128)(2,1)S(1)} collective-permute-done((bf16[8,16]{1,0:T(8,128)(2,1)S(1)}, bf16[8,16]{1,0:T(8,128)(2,1)S(1)}, u32[]{:S(2)}, u32[]{:S(2)}) %collective-permute-start.3) | collective-permute-done | bytes 288 | tf_op jit(solution)/shard_map/ppermute | solution.py:296
  70.3 0.9 collective-permute-done.2
  71.3 0.1 add_convert_fusion
  71.3 0.6 reshape.21.bias_ref
  71.9 5.8 %all-to-all-done.x_hbm = bf16[32,8,64,128]{3,2,1,0:T(8,128)(2,1)} async-done(((bf16[32,8,64,128]{3,2,1,0:T(8,128)(2,1)}), bf16[32,8,64,128]{3,2,1,0:T(8,128)(2,1)}, u32[]{:S(2)}, u32[]{:S(2)}) %all-to-all-start) | async-done | bytes 4194336 | tf_op jit(solution)/shard_map/all_to_all | solution.py:316
  77.8 0.6 broadcast_in_dim.18.prior_ref
  78.3 19.8 %attend.1 = (bf16[32,6,64,128]{3,2,1,0:T(8,128)(2,1)}, f32[8,128]{1,0:T(8,128)}) custom-call(bf16[32,8,64,128]{3,2,1,0:T(8,128)(2,1)} %all-to-all-done.x_hbm, f32[1,128]{1,0:T(1,128)} %reshape.21.bias_ref, f32[8,128]{1,0:T(8,128)} %broadcast_in_dim.18.prior_ref), custom_call_target="tpu_custom_call" | custom-call | flops 6039797760 | bytes 7340032 | tf_op jit(solution)/shard_map/attend/pallas_call | solution.py:262
  98.1 10.8 %all-to-all-start.1 = ((bf16[32,6,64,128]{3,2,1,0:T(8,128)(2,1)}), bf16[32,6,64,128]{3,2,1,0:T(8,128)(2,1)S(1)}, u32[]{:S(2)}, u32[]{:S(2)}) async-start(bf16[32,6,64,128]{3,2,1,0:T(8,128)(2,1)} %get-tuple-element.9), calls=%async_computation.1 | async-start | bytes 6291456 | tf_op jit(solution)/shard_map/all_to_all | solution.py:323
  108.9 0.1 reshape.19
  109.1 1.2 collective-permute-done.4
  110.2 0.5 collective-permute-start.7
  110.7 4.5 %collective-permute-start.6 = (f32[8,16]{1,0:T(8,128)S(1)}, f32[8,16]{1,0:T(8,128)S(1)}, u32[]{:S(2)}, u32[]{:S(2)}) collective-permute-start(f32[8,16]{1,0:T(8,128)S(1)} %add.32), channel_id=1, source_target_pairs={{0,4},{1,5},{2,6},{3,7},{4,0},{5,1},{6,2},{7,3},{8,12},{9,13},{10,... | collective-permute-start | bytes 1544 | tf_op jit(solution)/shard_map/ppermute | solution.py:296
  115.2 1.5 collective-permute-start.5
  116.7 30.0 %collective-permute-done.7 = f32[8,16]{1,0:T(8,128)S(1)} collective-permute-done((f32[8,16]{1,0:T(8,128)S(1)}, f32[8,16]{1,0:T(8,128)S(1)}, u32[]{:S(2)}, u32[]{:S(2)}) %collective-permute-start.7) | collective-permute-done | bytes 544 | tf_op jit(solution)/shard_map/ppermute | solution.py:296
  146.7 0.8 collective-permute-done.6
  147.5 0.5 dynamic-slice_bitcast_fusion
  148.0 4.5 %all-to-all-done.1.refs_0_ = bf16[32,6,64,128]{3,2,1,0:T(8,128)(2,1)S(1)} async-done(((bf16[32,6,64,128]{3,2,1,0:T(8,128)(2,1)}), bf16[32,6,64,128]{3,2,1,0:T(8,128)(2,1)S(1)}, u32[]{:S(2)}, u32[]{:S(2)}) %all-to-all-start.1) | async-done | bytes 3145760 | tf_op jit(solution)/shard_map/all_to_all | solution.py:323
  152.5 1.9 %unpack.1 = (bf16[2,64,4096]{2,1,0:T(8,128)(2,1)}, bf16[2,64,4096]{2,1,0:T(8,128)(2,1)}, bf16[2,64,4096]{2,1,0:T(8,128)(2,1)}) custom-call(bf16[32,6,64,128]{3,2,1,0:T(8,128)(2,1)S(1)} %all-to-all-done.1.refs_0_), custom_call_target="tpu_custom_call" | custom-call | bytes 6291456 | tf_op jit(solution)/shard_map/unpack/pallas_call | solution.py:103
  (14 shorter events, 0.3 us)
Async XLA Ops:
  4.3 9.0 %copy-start = (bf16[16]{0:T(256)(128)(2,1)S(1)}, bf16[16]{0:T(256)(128)(2,1)}, u32[]{:S(2)}) copy-start(bf16[16]{0:T(256)(128)(2,1)} %param.9) | copy-start | bytes 100
  4.3 73.4 %all-to-all-start = ((bf16[32,8,64,128]{3,2,1,0:T(8,128)(2,1)}), bf16[32,8,64,128]{3,2,1,0:T(8,128)(2,1)}, u32[]{:S(2)}, u32[]{:S(2)}) async-start(bf16[32,8,64,128]{3,2,1,0:T(8,128)(2,1)} %pack.1), calls=%async_computation | async-start | bytes 8388608 | tf_op jit(solution)/shard_map/all_to_all | solution.py:316
  13.4 1.2 collective-permute-start
  14.7 55.7 %collective-permute-start.3 = (bf16[8,16]{1,0:T(8,128)(2,1)S(1)}, bf16[8,16]{1,0:T(8,128)(2,1)S(1)}, u32[]{:S(2)}, u32[]{:S(2)}) collective-permute-start(bf16[8,16]{1,0:T(8,128)(2,1)S(1)} %fusion), channel_id=1, source_target_pairs={{0,6},{1,7},{2,4},{3,5},{4,2},{5,3},{6,0},{7,1},{8,14},{9,15},{10,... | collective-permute-start | bytes 776 | tf_op jit(solution)/shard_map/ppermute | solution.py:296
  20.1 51.2 %collective-permute-start.2 = (bf16[8,16]{1,0:T(8,128)(2,1)S(1)}, bf16[8,16]{1,0:T(8,128)(2,1)S(1)}, u32[]{:S(2)}, u32[]{:S(2)}) collective-permute-start(bf16[8,16]{1,0:T(8,128)(2,1)S(1)} %fusion), channel_id=1, source_target_pairs={{0,4},{1,5},{2,6},{3,7},{4,0},{5,1},{6,2},{7,3},{8,12},{9,13},{10,... | collective-permute-start | bytes 776 | tf_op jit(solution)/shard_map/ppermute | solution.py:296
  21.5 49.8 %collective-permute-start.1 = (bf16[8,16]{1,0:T(8,128)(2,1)S(1)}, bf16[8,16]{1,0:T(8,128)(2,1)S(1)}, u32[]{:S(2)}, u32[]{:S(2)}) collective-permute-start(bf16[8,16]{1,0:T(8,128)(2,1)S(1)} %fusion), channel_id=1, source_target_pairs={{0,2},{1,3},{2,0},{3,1},{4,6},{5,7},{6,4},{7,5},{8,10},{9,11},{10,... | collective-permute-start | bytes 776 | tf_op jit(solution)/shard_map/ppermute | solution.py:296
  98.1 10.8 %copy-start.1 = (f32[8,128]{1,0:T(8,128)S(1)}, f32[8,128]{1,0:T(8,128)}, u32[]{:S(2)}) copy-start(f32[8,128]{1,0:T(8,128)} %get-tuple-element.13) | copy-start | bytes 12292
  98.1 54.3 %all-to-all-start.1 = ((bf16[32,6,64,128]{3,2,1,0:T(8,128)(2,1)}), bf16[32,6,64,128]{3,2,1,0:T(8,128)(2,1)S(1)}, u32[]{:S(2)}, u32[]{:S(2)}) async-start(bf16[32,6,64,128]{3,2,1,0:T(8,128)(2,1)} %get-tuple-element.9), calls=%async_computation.1 | async-start | bytes 6291456 | tf_op jit(solution)/shard_map/all_to_all | solution.py:323
  109.0 1.2 collective-permute-start.4
  110.2 36.5 %collective-permute-start.7 = (f32[8,16]{1,0:T(8,128)S(1)}, f32[8,16]{1,0:T(8,128)S(1)}, u32[]{:S(2)}, u32[]{:S(2)}) collective-permute-start(f32[8,16]{1,0:T(8,128)S(1)} %add.32), channel_id=1, source_target_pairs={{0,6},{1,7},{2,4},{3,5},{4,2},{5,3},{6,0},{7,1},{8,14},{9,15},{10,... | collective-permute-start | bytes 1544 | tf_op jit(solution)/shard_map/ppermute | solution.py:296
  110.7 36.8 %collective-permute-start.6 = (f32[8,16]{1,0:T(8,128)S(1)}, f32[8,16]{1,0:T(8,128)S(1)}, u32[]{:S(2)}, u32[]{:S(2)}) collective-permute-start(f32[8,16]{1,0:T(8,128)S(1)} %add.32), channel_id=1, source_target_pairs={{0,4},{1,5},{2,6},{3,7},{4,0},{5,1},{6,2},{7,3},{8,12},{9,13},{10,... | collective-permute-start | bytes 1544 | tf_op jit(solution)/shard_map/ppermute | solution.py:296
  115.2 32.3 %collective-permute-start.5 = (f32[8,16]{1,0:T(8,128)S(1)}, f32[8,16]{1,0:T(8,128)S(1)}, u32[]{:S(2)}, u32[]{:S(2)}) collective-permute-start(f32[8,16]{1,0:T(8,128)S(1)} %add.32), channel_id=1, source_target_pairs={{0,2},{1,3},{2,0},{3,1},{4,6},{5,7},{6,4},{7,5},{8,10},{9,11},{10,... | collective-permute-start | bytes 1544 | tf_op jit(solution)/shard_map/ppermute | solution.py:296

commit v4 on v2

--- a/solution.py
+++ b/solution.py
@@ -211,7 +211,7 @@
             pltpu.VMEM((blocks, TILE, HDIM), jnp.float32),
             pltpu.VMEM((blocks, TILE, HDIM), jnp.float32),
         ],
-        compiler_params=pltpu.CompilerParams(vmem_limit_bytes=32 * 1024 * 1024),
+        compiler_params=pltpu.CompilerParams(vmem_limit_bytes=62 * 1024 * 1024),
         cost_estimate=pl.CostEstimate(
             flops=10 * area * HDIM * 2, bytes_accessed=14 * seq * HDIM, transcendentals=area
         ),
@@ -241,7 +241,7 @@
     results = []
     for item in range(items):
         packed = pack(inputs, item, 4)
-        if item == 1:
+        if item == 0:
             packed, bias = lax.optimization_barrier((packed, bias))
         moved = lax.all_to_all(packed, "seq", split_axis=0, concat_axis=0, tiled=True)
         grads, sums = attend(moved, bias, sums)

time: 134 us -> 146 us (1.090)
  Pallas kernels: 28.6 us -> 34 us
  waiting for transfers between devices: 59.2 us -> 64.6 us
    all_to_all x2, waiting for transfers between devices: 18.7 us -> 40.7 us  [body(): lax.all_to_all(packed, 'seq', split_axis=0, concat_axis=0, tiled=True)]
    ppermute x6, waiting for transfers between devices: 19.4 us -> 3.02 us  [spread_sum(): parts.append(lax.ppermute(pair, 'dp', [(d, d ^ step) for d in range(size)]))]
    pallas_call x2, Pallas kernels: 20.8 us -> 24.7 us  [attend(): pl.pallas_call(_attend_kernel, in_specs=[pl.BlockSpec(memory_space=pltpu....]
    unnamed x6 -> x4, local copies, waits for them, and re-layouts: 2.36 us -> 0.01 us
    all_to_all x2, starting transfers between devices: 17.3 us -> 15 us  [body(): lax.all_to_all(packed, 'seq', split_axis=0, concat_axis=0, tiled=True)]
    all_to_all x2, starting transfers between devices: 9.85 us -> 12.1 us  [body(): lax.all_to_all(grads, 'seq', split_axis=0, concat_axis=0, tiled=True)]
  transfers between devices with their start and end apart: 12 -> 12, of which waited for: 7 -> 7; matrix products, arithmetic and copies ran while one was open for 0% -> 0% of each run, Pallas kernels for 19% -> 23%
where the time goes in v4:
time: 146 us; the launch traced here: 145 us
  waiting for transfers between devices  64.6 us (44%)
  starting transfers between devices  42.3 us (29%)
  Pallas kernels  34 us (23%)
  local copies, waits for them, and re-layouts  1.8 us (1%)
  other arithmetic  1.57 us (1%)
    all_to_all x2, waiting for transfers between devices, body(): lax.all_to_all(packed, 'seq', split_axis=0, concat_axis=0, tiled=True)  40.7 us
    pallas_call x2, Pallas kernels, attend(): pl.pallas_call(_attend_kernel, in_specs=[pl.BlockSpec(memory_space=pltpu....  24.7 us
    all_to_all x2, waiting for transfers between devices, body(): lax.all_to_all(grads, 'seq', split_axis=0, concat_axis=0, tiled=True)  18.6 us
    ppermute x6, starting transfers between devices, spread_sum(): parts.append(lax.ppermute(pair, 'dp', [(d, d ^ step) for d in range(size)]))  15.2 us
    all_to_all x2, starting transfers between devices, body(): lax.all_to_all(packed, 'seq', split_axis=0, concat_axis=0, tiled=True)  15 us
    all_to_all x2, starting transfers between devices, body(): lax.all_to_all(grads, 'seq', split_axis=0, concat_axis=0, tiled=True)  12.1 us
    pallas_call x2, Pallas kernels, pack(): pl.pallas_call(functools.partial(_pack_kernel, item, count, groups), in_s...  5.35 us
    pallas_call x2, Pallas kernels, unpack(): pl.pallas_call(functools.partial(_unpack_kernel, item, count, groups), in...  3.92 us
  transfers between devices with their start and end apart: 12, of which 7 were waited for; matrix products, arithmetic and copies ran while one was open for 0% of the time, Pallas kernels for 23%

profile of v4, /device:TPU:8, one launch (start us, length us, event | category | flops | bytes accessed | tf_op | source)
XLA Modules:
  0.0 145.0 jit_solution(15638030920102097080)
XLA Ops:
  0.6 0.7 broadcast_select_fusion
  1.4 1.2 collective-permute-done
  2.5 0.7 fusion
  3.3 3.3 %collective-permute-start.1 = (bf16[8,16]{1,0:T(8,128)(2,1)S(1)}, bf16[8,16]{1,0:T(8,128)(2,1)S(1)}, u32[]{:S(2)}, u32[]{:S(2)}) collective-permute-start(bf16[8,16]{1,0:T(8,128)(2,1)S(1)} %fusion), channel_id=1, source_target_pairs={{0,2},{1,3},{2,0},{3,1},{4,6},{5,7},{6,4},{7,5},{8,10},{9,11},{10,... | collective-permute-start | bytes 776 | tf_op jit(solution)/shard_map/ppermute | solution.py:226
  6.5 5.4 %collective-permute-start.2 = (bf16[8,16]{1,0:T(8,128)(2,1)S(1)}, bf16[8,16]{1,0:T(8,128)(2,1)S(1)}, u32[]{:S(2)}, u32[]{:S(2)}) collective-permute-start(bf16[8,16]{1,0:T(8,128)(2,1)S(1)} %fusion), channel_id=1, source_target_pairs={{0,4},{1,5},{2,6},{3,7},{4,0},{5,1},{6,2},{7,3},{8,12},{9,13},{10,... | collective-permute-start | bytes 776 | tf_op jit(solution)/shard_map/ppermute | solution.py:226
  11.9 2.7 %pack.3 = bf16[32,4,64,128]{3,2,1,0:T(8,128)(2,1)} custom-call(bf16[2,64,4096]{2,1,0:T(8,128)(2,1)} %refs_0_.3, bf16[2,64,4096]{2,1,0:T(8,128)(2,1)} %refs_1_.3, bf16[2,64,4096]{2,1,0:T(8,128)(2,1)} %refs_2_.3, bf16[2,64,4096]{2,1,0:T(8,128)(2,1)} %refs_3_.3), custom_call_target="tpu_custom_call" | custom-call | bytes 4194304 | tf_op jit(solution)/shard_map/pack/pallas_call | solution.py:49
  14.6 3.0 %collective-permute-done.3 = bf16[8,16]{1,0:T(8,128)(2,1)S(1)} collective-permute-done((bf16[8,16]{1,0:T(8,128)(2,1)S(1)}, bf16[8,16]{1,0:T(8,128)(2,1)S(1)}, u32[]{:S(2)}, u32[]{:S(2)}) %collective-permute-start.3) | collective-permute-done | bytes 288 | tf_op jit(solution)/shard_map/ppermute | solution.py:226
  18.3 8.0 %all-to-all-start.1 = ((bf16[32,4,64,128]{3,2,1,0:T(8,128)(2,1)}), bf16[32,4,64,128]{3,2,1,0:T(8,128)(2,1)}, u32[]{:S(2)}, u32[]{:S(2)}) async-start(bf16[32,4,64,128]{3,2,1,0:T(8,128)(2,1)} %pack.3), calls=%async_computation.1 | async-start | bytes 4194304 | tf_op jit(solution)/shard_map/all_to_all | solution.py:246
  26.3 2.7 %pack.2 = bf16[32,4,64,128]{3,2,1,0:T(8,128)(2,1)} custom-call(bf16[2,64,4096]{2,1,0:T(8,128)(2,1)} %refs_0_.3, bf16[2,64,4096]{2,1,0:T(8,128)(2,1)} %refs_1_.3, bf16[2,64,4096]{2,1,0:T(8,128)(2,1)} %refs_2_.3, bf16[2,64,4096]{2,1,0:T(8,128)(2,1)} %refs_3_.3), custom_call_target="tpu_custom_call" | custom-call | bytes 4194304 | tf_op jit(solution)/shard_map/pack/pallas_call | solution.py:49
  29.0 27.0 %all-to-all-done.1.x_ref = bf16[32,4,64,128]{3,2,1,0:T(8,128)(2,1)} async-done(((bf16[32,4,64,128]{3,2,1,0:T(8,128)(2,1)}), bf16[32,4,64,128]{3,2,1,0:T(8,128)(2,1)}, u32[]{:S(2)}, u32[]{:S(2)}) %all-to-all-start.1) | async-done | bytes 2097184 | tf_op jit(solution)/shard_map/all_to_all | solution.py:246
  56.1 6.9 %all-to-all-start = ((bf16[32,4,64,128]{3,2,1,0:T(8,128)(2,1)}), bf16[32,4,64,128]{3,2,1,0:T(8,128)(2,1)}, u32[]{:S(2)}, u32[]{:S(2)}) async-start(bf16[32,4,64,128]{3,2,1,0:T(8,128)(2,1)} %pack.2), calls=%async_computation | async-start | bytes 4194304 | tf_op jit(solution)/shard_map/all_to_all | solution.py:246
  63.6 12.3 %attend.2 = (bf16[32,3,64,128]{3,2,1,0:T(8,128)(2,1)}, f32[8,128]{1,0:T(8,128)}) custom-call(bf16[32,4,64,128]{3,2,1,0:T(8,128)(2,1)} %all-to-all-done.1.x_ref, f32[1,128]{1,0:T(1,128)} %reshape.22.bias_ref, f32[8,128]{1,0:T(8,128)} %broadcast_in_dim.18.prior_ref), custom_call_target="tpu_custom_call" | custom-call | flops 6039797760 | bytes 3670016 | tf_op jit(solution)/shard_map/attend/pallas_call | solution.py:198
  75.9 13.7 %all-to-all-done.x_ref = bf16[32,4,64,128]{3,2,1,0:T(8,128)(2,1)} async-done(((bf16[32,4,64,128]{3,2,1,0:T(8,128)(2,1)}), bf16[32,4,64,128]{3,2,1,0:T(8,128)(2,1)}, u32[]{:S(2)}, u32[]{:S(2)}) %all-to-all-start) | async-done | bytes 2097184 | tf_op jit(solution)/shard_map/all_to_all | solution.py:246
  89.6 6.2 %all-to-all-start.3 = ((bf16[32,3,64,128]{3,2,1,0:T(8,128)(2,1)}), bf16[32,3,64,128]{3,2,1,0:T(8,128)(2,1)S(1)}, u32[]{:S(2)}, u32[]{:S(2)}) async-start(bf16[32,3,64,128]{3,2,1,0:T(8,128)(2,1)} %get-tuple-element.24), calls=%async_computation.3 | async-start | bytes 3145728 | tf_op jit(solution)/shard_map/all_to_all | solution.py:248
  95.8 12.3 %attend.3 = (bf16[32,3,64,128]{3,2,1,0:T(8,128)(2,1)}, f32[8,128]{1,0:T(8,128)}) custom-call(bf16[32,4,64,128]{3,2,1,0:T(8,128)(2,1)} %all-to-all-done.x_ref, f32[1,128]{1,0:T(1,128)} %reshape.22.bias_ref, f32[8,128]{1,0:T(8,128)} %get-tuple-element.22.prior_ref), custom_call_target="tpu_custom_call" | custom-call | flops 6039797760 | bytes 3670016 | tf_op jit(solution)/shard_map/attend/pallas_call | solution.py:198
  108.1 7.5 %all-to-all-done.3.refs_0_ = bf16[32,3,64,128]{3,2,1,0:T(8,128)(2,1)S(1)} async-done(((bf16[32,3,64,128]{3,2,1,0:T(8,128)(2,1)}), bf16[32,3,64,128]{3,2,1,0:T(8,128)(2,1)S(1)}, u32[]{:S(2)}, u32[]{:S(2)}) %all-to-all-start.3) | async-done | bytes 1572896 | tf_op jit(solution)/shard_map/all_to_all | solution.py:248
  115.7 5.9 %all-to-all-start.2 = ((bf16[32,3,64,128]{3,2,1,0:T(8,128)(2,1)}), bf16[32,3,64,128]{3,2,1,0:T(8,128)(2,1)}, u32[]{:S(2)}, u32[]{:S(2)}) async-start(bf16[32,3,64,128]{3,2,1,0:T(8,128)(2,1)} %get-tuple-element.23), calls=%async_computation.2 | async-start | bytes 3145728 | tf_op jit(solution)/shard_map/all_to_all | solution.py:248
  121.6 1.3 unpack.2
  123.0 1.2 collective-permute-done.4
  124.2 1.5 %collective-permute-start.5 = (f32[8,16]{1,0:T(8,128)S(1)}, f32[8,16]{1,0:T(8,128)S(1)}, u32[]{:S(2)}, u32[]{:S(2)}) collective-permute-start(f32[8,16]{1,0:T(8,128)S(1)} %add.32), channel_id=1, source_target_pairs={{0,2},{1,3},{2,0},{3,1},{4,6},{5,7},{6,4},{7,5},{8,10},{9,11},{10,... | collective-permute-start | bytes 1544 | tf_op jit(solution)/shard_map/ppermute | solution.py:226
  125.6 2.7 %collective-permute-start.6 = (f32[8,16]{1,0:T(8,128)S(1)}, f32[8,16]{1,0:T(8,128)S(1)}, u32[]{:S(2)}, u32[]{:S(2)}) collective-permute-start(f32[8,16]{1,0:T(8,128)S(1)} %add.32), channel_id=1, source_target_pairs={{0,4},{1,5},{2,6},{3,7},{4,0},{5,1},{6,2},{7,3},{8,12},{9,13},{10,... | collective-permute-start | bytes 1544 | tf_op jit(solution)/shard_map/ppermute | solution.py:226
  128.3 2.4 %collective-permute-start.7 = (f32[8,16]{1,0:T(8,128)S(1)}, f32[8,16]{1,0:T(8,128)S(1)}, u32[]{:S(2)}, u32[]{:S(2)}) collective-permute-start(f32[8,16]{1,0:T(8,128)S(1)} %add.32), channel_id=1, source_target_pairs={{0,6},{1,7},{2,4},{3,5},{4,2},{5,3},{6,0},{7,1},{8,14},{9,15},{10,... | collective-permute-start | bytes 1544 | tf_op jit(solution)/shard_map/ppermute | solution.py:226
  130.7 11.1 %all-to-all-done.2.refs_0_ = bf16[32,3,64,128]{3,2,1,0:T(8,128)(2,1)} async-done(((bf16[32,3,64,128]{3,2,1,0:T(8,128)(2,1)}), bf16[32,3,64,128]{3,2,1,0:T(8,128)(2,1)}, u32[]{:S(2)}, u32[]{:S(2)}) %all-to-all-start.2) | async-done | bytes 1572896 | tf_op jit(solution)/shard_map/all_to_all | solution.py:248
  141.8 2.7 %unpack.3 = (bf16[2,64,4096]{2,1,0:T(8,128)(2,1)}, bf16[2,64,4096]{2,1,0:T(8,128)(2,1)}, bf16[2,64,4096]{2,1,0:T(8,128)(2,1)}) custom-call(bf16[32,3,64,128]{3,2,1,0:T(8,128)(2,1)} %all-to-all-done.2.refs_0_, bf16[2,64,4096]{2,1,0:T(8,128)(2,1)} %get-tuple-element.29.refs_1_, ...), custom_call_target="tpu_custom_call", output_to_operand_aliasing={{0}: (1, {}), {1}: (2, {}), {2}: (3, {})} | custom-call | bytes 3145728 | tf_op jit(solution)/shard_map/unpack/pallas_call | solution.py:97
  (21 shorter events, 2.0 us)
Async XLA Ops:
  1.4 1.2 collective-permute-start
  3.3 14.4 %copy-start = (bf16[16]{0:T(256)(128)(2,1)S(1)}, bf16[16]{0:T(256)(128)(2,1)}, u32[]{:S(2)}) copy-start(bf16[16]{0:T(256)(128)(2,1)} %param.9) | copy-start | bytes 100
  3.3 11.3 %collective-permute-start.1 = (bf16[8,16]{1,0:T(8,128)(2,1)S(1)}, bf16[8,16]{1,0:T(8,128)(2,1)S(1)}, u32[]{:S(2)}, u32[]{:S(2)}) collective-permute-start(bf16[8,16]{1,0:T(8,128)(2,1)S(1)} %fusion), channel_id=1, source_target_pairs={{0,2},{1,3},{2,0},{3,1},{4,6},{5,7},{6,4},{7,5},{8,10},{9,11},{10,... | collective-permute-start | bytes 776 | tf_op jit(solution)/shard_map/ppermute | solution.py:226
  6.5 8.1 %collective-permute-start.2 = (bf16[8,16]{1,0:T(8,128)(2,1)S(1)}, bf16[8,16]{1,0:T(8,128)(2,1)S(1)}, u32[]{:S(2)}, u32[]{:S(2)}) collective-permute-start(bf16[8,16]{1,0:T(8,128)(2,1)S(1)} %fusion), channel_id=1, source_target_pairs={{0,4},{1,5},{2,6},{3,7},{4,0},{5,1},{6,2},{7,3},{8,12},{9,13},{10,... | collective-permute-start | bytes 776 | tf_op jit(solution)/shard_map/ppermute | solution.py:226
  11.9 5.7 %collective-permute-start.3 = (bf16[8,16]{1,0:T(8,128)(2,1)S(1)}, bf16[8,16]{1,0:T(8,128)(2,1)S(1)}, u32[]{:S(2)}, u32[]{:S(2)}) collective-permute-start(bf16[8,16]{1,0:T(8,128)(2,1)S(1)} %fusion), channel_id=1, source_target_pairs={{0,6},{1,7},{2,4},{3,5},{4,2},{5,3},{6,0},{7,1},{8,14},{9,15},{10,... | collective-permute-start | bytes 776 | tf_op jit(solution)/shard_map/ppermute | solution.py:226
  18.3 37.8 %all-to-all-start.1 = ((bf16[32,4,64,128]{3,2,1,0:T(8,128)(2,1)}), bf16[32,4,64,128]{3,2,1,0:T(8,128)(2,1)}, u32[]{:S(2)}, u32[]{:S(2)}) async-start(bf16[32,4,64,128]{3,2,1,0:T(8,128)(2,1)} %pack.3), calls=%async_computation.1 | async-start | bytes 4194304 | tf_op jit(solution)/shard_map/all_to_all | solution.py:246
  56.1 33.5 %all-to-all-start = ((bf16[32,4,64,128]{3,2,1,0:T(8,128)(2,1)}), bf16[32,4,64,128]{3,2,1,0:T(8,128)(2,1)}, u32[]{:S(2)}, u32[]{:S(2)}) async-start(bf16[32,4,64,128]{3,2,1,0:T(8,128)(2,1)} %pack.2), calls=%async_computation | async-start | bytes 4194304 | tf_op jit(solution)/shard_map/all_to_all | solution.py:246
  89.6 26.0 %all-to-all-start.3 = ((bf16[32,3,64,128]{3,2,1,0:T(8,128)(2,1)}), bf16[32,3,64,128]{3,2,1,0:T(8,128)(2,1)S(1)}, u32[]{:S(2)}, u32[]{:S(2)}) async-start(bf16[32,3,64,128]{3,2,1,0:T(8,128)(2,1)} %get-tuple-element.24), calls=%async_computation.3 | async-start | bytes 3145728 | tf_op jit(solution)/shard_map/all_to_all | solution.py:248
  115.7 7.2 %copy-start.1 = (f32[8,128]{1,0:T(8,128)S(1)}, f32[8,128]{1,0:T(8,128)}, u32[]{:S(2)}) copy-start(f32[8,128]{1,0:T(8,128)} %get-tuple-element.35) | copy-start | bytes 12292
  115.7 26.1 %all-to-all-start.2 = ((bf16[32,3,64,128]{3,2,1,0:T(8,128)(2,1)}), bf16[32,3,64,128]{3,2,1,0:T(8,128)(2,1)}, u32[]{:S(2)}, u32[]{:S(2)}) async-start(bf16[32,3,64,128]{3,2,1,0:T(8,128)(2,1)} %get-tuple-element.23), calls=%async_computation.2 | async-start | bytes 3145728 | tf_op jit(solution)/shard_map/all_to_all | solution.py:248
  123.0 1.2 collective-permute-start.4
  124.2 20.3 %collective-permute-start.5 = (f32[8,16]{1,0:T(8,128)S(1)}, f32[8,16]{1,0:T(8,128)S(1)}, u32[]{:S(2)}, u32[]{:S(2)}) collective-permute-start(f32[8,16]{1,0:T(8,128)S(1)} %add.32), channel_id=1, source_target_pairs={{0,2},{1,3},{2,0},{3,1},{4,6},{5,7},{6,4},{7,5},{8,10},{9,11},{10,... | collective-permute-start | bytes 1544 | tf_op jit(solution)/shard_map/ppermute | solution.py:226
  125.6 18.8 %collective-permute-start.6 = (f32[8,16]{1,0:T(8,128)S(1)}, f32[8,16]{1,0:T(8,128)S(1)}, u32[]{:S(2)}, u32[]{:S(2)}) collective-permute-start(f32[8,16]{1,0:T(8,128)S(1)} %add.32), channel_id=1, source_target_pairs={{0,4},{1,5},{2,6},{3,7},{4,0},{5,1},{6,2},{7,3},{8,12},{9,13},{10,... | collective-permute-start | bytes 1544 | tf_op jit(solution)/shard_map/ppermute | solution.py:226
  128.3 16.2 %collective-permute-start.7 = (f32[8,16]{1,0:T(8,128)S(1)}, f32[8,16]{1,0:T(8,128)S(1)}, u32[]{:S(2)}, u32[]{:S(2)}) collective-permute-start(f32[8,16]{1,0:T(8,128)S(1)} %add.32), channel_id=1, source_target_pairs={{0,6},{1,7},{2,4},{3,5},{4,2},{5,3},{6,0},{7,1},{8,14},{9,15},{10,... | collective-permute-start | bytes 1544 | tf_op jit(solution)/shard_map/ppermute | solution.py:226

commit v5 on v2

--- a/solution.py
+++ b/solution.py
@@ -233,9 +233,11 @@
     share = query_bias.shape[0]
     me = lax.axis_index("dp")
 
-    own = lax.broadcasted_iota(jnp.int32, (dp_size, share), 0) == me
-    slots = jnp.where(own, query_bias[None, :], jnp.zeros((), query_bias.dtype))
-    bias = spread_sum(slots, dp_size).astype(jnp.float32).reshape(1, dp_size * share)
+    lanes = dp_size * share
+    wide = jnp.tile(query_bias.astype(jnp.float32), dp_size).reshape(1, lanes)
+    own = lax.broadcasted_iota(jnp.int32, (HDIM, lanes), 1) // share == me
+    slots = jnp.where(own, jnp.broadcast_to(wide, (HDIM, lanes)), 0.0)
+    bias = lax.psum(slots, "dp")[:1]
 
     sums = jnp.zeros((8, HDIM), jnp.float32)
     results = []

time: 134 us -> 205 us (1.53); the launches traced: 133 us -> 201 us
  waiting for transfers between devices: 59.2 us -> 115 us
  between operations: 0.82 us -> 14.2 us
  starting transfers between devices: 41.5 us -> 38.9 us
    psum x0 -> x1, waiting for transfers between devices: none -> 74.1 us  [body(): bias = lax.psum(slots, 'dp')[:1]]
    all_to_all x2, waiting for transfers between devices: 18.8 us -> 7.76 us  [body(): lax.all_to_all(grads, 'seq', split_axis=0, concat_axis=0, tiled=True)]
    ppermute x6 -> x3, waiting for transfers between devices: 19.4 us -> 12.1 us  [spread_sum(): parts.append(lax.ppermute(pair, 'dp', [(d, d ^ step) for d in range(size)]))]
    ppermute x6 -> x3, starting transfers between devices: 14.3 us -> 12.9 us  [spread_sum(): parts.append(lax.ppermute(pair, 'dp', [(d, d ^ step) for d in range(size)]))]
  transfers between devices with their start and end apart: 12 -> 9, of which waited for: 7 -> 6; matrix products, arithmetic and copies ran while one was open for 0% -> 1% of each run, Pallas kernels for 19% -> 12%
where the time goes in v5:
time: 205 us; the launch traced here: 201 us
  waiting for transfers between devices  115 us (56%)
  starting transfers between devices  38.9 us (19%)
  Pallas kernels  28.6 us (14%)
  between operations  14.2 us (7%)
  local copies, waits for them, and re-layouts  3.72 us (2%)
    psum x1, waiting for transfers between devices, body(): bias = lax.psum(slots, 'dp')[:1]  74.1 us
    pallas_call x2, Pallas kernels, attend(): pl.pallas_call(_attend_kernel, in_specs=[pl.BlockSpec(memory_space=pltpu....  20.8 us
    all_to_all x2, waiting for transfers between devices, body(): lax.all_to_all(packed, 'seq', split_axis=0, concat_axis=0, tiled=True)  20.2 us
    all_to_all x2, starting transfers between devices, body(): lax.all_to_all(packed, 'seq', split_axis=0, concat_axis=0, tiled=True)  16.4 us
    ppermute x3, starting transfers between devices, spread_sum(): parts.append(lax.ppermute(pair, 'dp', [(d, d ^ step) for d in range(size)]))  12.9 us
    ppermute x3, waiting for transfers between devices, spread_sum(): parts.append(lax.ppermute(pair, 'dp', [(d, d ^ step) for d in range(size)]))  12.1 us
    all_to_all x2, starting transfers between devices, body(): lax.all_to_all(grads, 'seq', split_axis=0, concat_axis=0, tiled=True)  9.45 us
    all_to_all x2, waiting for transfers between devices, body(): lax.all_to_all(grads, 'seq', split_axis=0, concat_axis=0, tiled=True)  7.76 us
  transfers between devices with their start and end apart: 9, of which 6 were waited for; matrix products, arithmetic and copies ran while one was open for 1% of the time, Pallas kernels for 12%

profile of v5, /device:TPU:8, one launch (start us, length us, event | category | flops | bytes accessed | tf_op | source)
XLA Modules:
  0.0 201.4 jit_solution(12650572828546024542)
XLA Ops:
  7.2 2.7 %pack.3 = bf16[32,4,64,128]{3,2,1,0:T(8,128)(2,1)} custom-call(bf16[2,64,4096]{2,1,0:T(8,128)(2,1)} %refs_0_.3, bf16[2,64,4096]{2,1,0:T(8,128)(2,1)} %refs_1_.3, bf16[2,64,4096]{2,1,0:T(8,128)(2,1)} %refs_2_.3, bf16[2,64,4096]{2,1,0:T(8,128)(2,1)} %refs_3_.3), custom_call_target="tpu_custom_call" | custom-call | bytes 4194304 | tf_op jit(solution)/shard_map/pack/pallas_call | solution.py:49
  9.8 8.9 %all-to-all-start.1 = ((bf16[32,4,64,128]{3,2,1,0:T(8,128)(2,1)}), bf16[32,4,64,128]{3,2,1,0:T(8,128)(2,1)S(1)}, u32[]{:S(2)}, u32[]{:S(2)}) async-start(bf16[32,4,64,128]{3,2,1,0:T(8,128)(2,1)} %pack.3), calls=%async_computation.1 | async-start | bytes 4194304 | tf_op jit(solution)/shard_map/all_to_all | solution.py:248
  18.9 0.6 fusion
  19.6 2.7 %pack.2 = bf16[32,4,64,128]{3,2,1,0:T(8,128)(2,1)} custom-call(bf16[2,64,4096]{2,1,0:T(8,128)(2,1)} %refs_0_.3, bf16[2,64,4096]{2,1,0:T(8,128)(2,1)} %refs_1_.3, bf16[2,64,4096]{2,1,0:T(8,128)(2,1)} %refs_2_.3, bf16[2,64,4096]{2,1,0:T(8,128)(2,1)} %refs_3_.3), custom_call_target="tpu_custom_call" | custom-call | bytes 4194304 | tf_op jit(solution)/shard_map/pack/pallas_call | solution.py:49
  22.3 74.1 %all-reduce.2.cloned.1.call-done = f32[128,128]{1,0:T(8,128)} async-done(((f32[128,128]{1,0:T(8,128)}), f32[128,128]{1,0:T(8,128)}) %all-reduce.2.cloned.1.call-update) | async-done | bytes 65552 | tf_op jit(solution)/shard_map/psum | solution.py:240
  96.4 0.7 slice.4.bias_ref
  97.1 7.5 %all-to-all-start = ((bf16[32,4,64,128]{3,2,1,0:T(8,128)(2,1)}), bf16[32,4,64,128]{3,2,1,0:T(8,128)(2,1)}, u32[]{:S(2)}, u32[]{:S(2)}) async-start(bf16[32,4,64,128]{3,2,1,0:T(8,128)(2,1)} %pack.2), calls=%async_computation | async-start | bytes 4194304 | tf_op jit(solution)/shard_map/all_to_all | solution.py:248
  104.6 9.6 %attend.2 = (bf16[32,3,64,128]{3,2,1,0:T(8,128)(2,1)S(1)}, f32[8,128]{1,0:T(8,128)S(1)}) custom-call(bf16[32,4,64,128]{3,2,1,0:T(8,128)(2,1)S(1)} %all-to-all-done.1.x_ref, f32[1,128]{1,0:T(1,128)S(1)} %slice.4.bias_ref, f32[8,128]{1,0:T(8,128)S(1)} %broadcast_in_dim.17.prior_ref), custom_call_target="tpu_custom_call" | custom-call | flops 6039797760 | bytes 3670016 | tf_op jit(solution)/shard_map/attend/pallas_call | solution.py:198
  114.2 1.2 copy-done.1
  115.4 20.2 %all-to-all-done.x_ref = bf16[32,4,64,128]{3,2,1,0:T(8,128)(2,1)} async-done(((bf16[32,4,64,128]{3,2,1,0:T(8,128)(2,1)}), bf16[32,4,64,128]{3,2,1,0:T(8,128)(2,1)}, u32[]{:S(2)}, u32[]{:S(2)}) %all-to-all-start) | async-done | bytes 2097184 | tf_op jit(solution)/shard_map/all_to_all | solution.py:248
  135.5 4.3 %all-to-all-start.3 = ((bf16[32,3,64,128]{3,2,1,0:T(8,128)(2,1)}), bf16[32,3,64,128]{3,2,1,0:T(8,128)(2,1)S(1)}, u32[]{:S(2)}, u32[]{:S(2)}) async-start(bf16[32,3,64,128]{3,2,1,0:T(8,128)(2,1)} %copy-done.1), calls=%async_computation.3 | async-start | bytes 3145728 | tf_op jit(solution)/shard_map/all_to_all | solution.py:250
  139.8 11.2 %attend.3 = (bf16[32,3,64,128]{3,2,1,0:T(8,128)(2,1)S(1)}, f32[8,128]{1,0:T(8,128)S(1)}) custom-call(bf16[32,4,64,128]{3,2,1,0:T(8,128)(2,1)} %all-to-all-done.x_ref, f32[1,128]{1,0:T(1,128)S(1)} %slice.4.bias_ref, f32[8,128]{1,0:T(8,128)S(1)} %get-tuple-element.22.prior_ref), custom_call_target="tpu_custom_call" | custom-call | flops 6039797760 | bytes 3670016 | tf_op jit(solution)/shard_map/attend/pallas_call | solution.py:198
  151.0 1.2 copy-done
  152.2 7.8 %all-to-all-done.3.refs_0_ = bf16[32,3,64,128]{3,2,1,0:T(8,128)(2,1)S(1)} async-done(((bf16[32,3,64,128]{3,2,1,0:T(8,128)(2,1)}), bf16[32,3,64,128]{3,2,1,0:T(8,128)(2,1)S(1)}, u32[]{:S(2)}, u32[]{:S(2)}) %all-to-all-start.3) | async-done | bytes 1572896 | tf_op jit(solution)/shard_map/all_to_all | solution.py:250
  159.9 5.2 %all-to-all-start.2 = ((bf16[32,3,64,128]{3,2,1,0:T(8,128)(2,1)}), bf16[32,3,64,128]{3,2,1,0:T(8,128)(2,1)S(1)}, u32[]{:S(2)}, u32[]{:S(2)}) async-start(bf16[32,3,64,128]{3,2,1,0:T(8,128)(2,1)} %copy-done), calls=%async_computation.2 | async-start | bytes 3145728 | tf_op jit(solution)/shard_map/all_to_all | solution.py:250
  165.1 1.3 unpack.2
  166.4 0.1 reshape.13
  166.5 1.2 collective-permute-done
  167.7 5.5 %collective-permute-start.1 = (f32[8,16]{1,0:T(8,128)S(1)}, f32[8,16]{1,0:T(8,128)S(1)}, u32[]{:S(2)}, u32[]{:S(2)}) collective-permute-start(f32[8,16]{1,0:T(8,128)S(1)} %add.20), channel_id=1, source_target_pairs={{0,2},{1,3},{2,0},{3,1},{4,6},{5,7},{6,4},{7,5},{8,10},{9,11},{10,... | collective-permute-start | bytes 1544 | tf_op jit(solution)/shard_map/ppermute | solution.py:226
  173.2 7.4 %collective-permute-start.2 = (f32[8,16]{1,0:T(8,128)S(1)}, f32[8,16]{1,0:T(8,128)S(1)}, u32[]{:S(2)}, u32[]{:S(2)}) collective-permute-start(f32[8,16]{1,0:T(8,128)S(1)} %add.20), channel_id=1, source_target_pairs={{0,4},{1,5},{2,6},{3,7},{4,0},{5,1},{6,2},{7,3},{8,12},{9,13},{10,... | collective-permute-start | bytes 1544 | tf_op jit(solution)/shard_map/ppermute | solution.py:226
  180.6 4.6 %collective-permute-done.2 = f32[8,16]{1,0:T(8,128)S(1)} collective-permute-done((f32[8,16]{1,0:T(8,128)S(1)}, f32[8,16]{1,0:T(8,128)S(1)}, u32[]{:S(2)}, u32[]{:S(2)}) %collective-permute-start.2) | collective-permute-done | bytes 544 | tf_op jit(solution)/shard_map/ppermute | solution.py:226
  185.2 7.5 %collective-permute-done.3 = f32[8,16]{1,0:T(8,128)S(1)} collective-permute-done((f32[8,16]{1,0:T(8,128)S(1)}, f32[8,16]{1,0:T(8,128)S(1)}, u32[]{:S(2)}, u32[]{:S(2)}) %collective-permute-start.3) | collective-permute-done | bytes 544 | tf_op jit(solution)/shard_map/ppermute | solution.py:226
  192.7 0.5 dynamic-slice_bitcast_fusion
  193.3 1.3 unpack.3
  (19 shorter events, 0.2 us)
Async XLA Ops:
  9.8 9.0 %copy-start.2 = (bf16[16]{0:T(256)(128)(2,1)S(1)}, bf16[16]{0:T(256)(128)(2,1)}, u32[]{:S(2)}) copy-start(bf16[16]{0:T(256)(128)(2,1)} %param.9) | copy-start | bytes 100
  9.8 87.2 %all-to-all-start.1 = ((bf16[32,4,64,128]{3,2,1,0:T(8,128)(2,1)}), bf16[32,4,64,128]{3,2,1,0:T(8,128)(2,1)S(1)}, u32[]{:S(2)}, u32[]{:S(2)}) async-start(bf16[32,4,64,128]{3,2,1,0:T(8,128)(2,1)} %pack.3), calls=%async_computation.1 | async-start | bytes 4194304 | tf_op jit(solution)/shard_map/all_to_all | solution.py:248
  18.7 77.6 %all-reduce.2.cloned.1.call-start = ((), (), s32[]{:S(2)}) async-start(), calls=%async_computation.4 | async-start | bytes 131072 | tf_op jit(solution)/shard_map/psum | solution.py:240
  97.1 38.5 %all-to-all-start = ((bf16[32,4,64,128]{3,2,1,0:T(8,128)(2,1)}), bf16[32,4,64,128]{3,2,1,0:T(8,128)(2,1)}, u32[]{:S(2)}, u32[]{:S(2)}) async-start(bf16[32,4,64,128]{3,2,1,0:T(8,128)(2,1)} %pack.2), calls=%async_computation | async-start | bytes 4194304 | tf_op jit(solution)/shard_map/all_to_all | solution.py:248
  114.2 1.2 copy-start.1
  135.5 24.4 %all-to-all-start.3 = ((bf16[32,3,64,128]{3,2,1,0:T(8,128)(2,1)}), bf16[32,3,64,128]{3,2,1,0:T(8,128)(2,1)S(1)}, u32[]{:S(2)}, u32[]{:S(2)}) async-start(bf16[32,3,64,128]{3,2,1,0:T(8,128)(2,1)} %copy-done.1), calls=%async_computation.3 | async-start | bytes 3145728 | tf_op jit(solution)/shard_map/all_to_all | solution.py:250
  151.0 1.2 copy-start
  159.9 33.3 %all-to-all-start.2 = ((bf16[32,3,64,128]{3,2,1,0:T(8,128)(2,1)}), bf16[32,3,64,128]{3,2,1,0:T(8,128)(2,1)S(1)}, u32[]{:S(2)}, u32[]{:S(2)}) async-start(bf16[32,3,64,128]{3,2,1,0:T(8,128)(2,1)} %copy-done), calls=%async_computation.2 | async-start | bytes 3145728 | tf_op jit(solution)/shard_map/all_to_all | solution.py:250
  166.5 1.2 collective-permute-start
  167.7 12.9 %collective-permute-start.1 = (f32[8,16]{1,0:T(8,128)S(1)}, f32[8,16]{1,0:T(8,128)S(1)}, u32[]{:S(2)}, u32[]{:S(2)}) collective-permute-start(f32[8,16]{1,0:T(8,128)S(1)} %add.20), channel_id=1, source_target_pairs={{0,2},{1,3},{2,0},{3,1},{4,6},{5,7},{6,4},{7,5},{8,10},{9,11},{10,... | collective-permute-start | bytes 1544 | tf_op jit(solution)/shard_map/ppermute | solution.py:226
  173.2 12.1 %collective-permute-start.2 = (f32[8,16]{1,0:T(8,128)S(1)}, f32[8,16]{1,0:T(8,128)S(1)}, u32[]{:S(2)}, u32[]{:S(2)}) collective-permute-start(f32[8,16]{1,0:T(8,128)S(1)} %add.20), channel_id=1, source_target_pairs={{0,4},{1,5},{2,6},{3,7},{4,0},{5,1},{6,2},{7,3},{8,12},{9,13},{10,... | collective-permute-start | bytes 1544 | tf_op jit(solution)/shard_map/ppermute | solution.py:226
  180.6 12.1 %collective-permute-start.3 = (f32[8,16]{1,0:T(8,128)S(1)}, f32[8,16]{1,0:T(8,128)S(1)}, u32[]{:S(2)}, u32[]{:S(2)}) collective-permute-start(f32[8,16]{1,0:T(8,128)S(1)} %add.20), channel_id=1, source_target_pairs={{0,6},{1,7},{2,4},{3,5},{4,2},{5,3},{6,0},{7,1},{8,14},{9,15},{10,... | collective-permute-start | bytes 1544 | tf_op jit(solution)/shard_map/ppermute | solution.py:226
Sparse Core Ops, SparseCore 0:
  22.8 73.5 all-reduce.1

commit v6 on v3

--- a/solution.py
+++ b/solution.py
@@ -11,9 +11,7 @@
 HDIM = 128
 TILE = 256
 MASKED = -1e30
-IN_CHUNKS = ((0, 1),)
-OUT_CHUNKS = ((0, 1),)
-GATE = -1
+OUT_CHUNKS = ((0,), (1,))
 
 
 def _pack_kernel(items, count, groups, *refs):
@@ -137,6 +135,7 @@
 
 def _attend_kernel(
     items,
+    first,
     x_hbm,
     bias_ref,
     prior_ref,
@@ -166,8 +165,12 @@
     total_sums = [prior_ref[...]]
 
     def load(n, i):
-        place = (pl.ds(i * per, per), pl.ds(4 * n, 4))
-        return pltpu.make_async_copy(x_hbm.at[place], x_ref.at[place], in_sem.at[n, i])
+        span = pl.ds(i * per, per)
+        return pltpu.make_async_copy(
+            x_hbm.at[span, pl.ds(4 * (first + n), 4)],
+            x_ref.at[span, pl.ds(4 * n, 4)],
+            in_sem.at[n, i],
+        )
 
     def store(n, i):
         place = (pl.ds(i * per, per), pl.ds(3 * n, 3))
@@ -254,13 +257,13 @@
         store(n, i).wait()
 
 
-def attend(x, bias, prior, items):
+def attend(x, bias, prior, first, items):
     peers, _, rows, _ = x.shape
     seq = peers * rows
     blocks = seq // TILE
     area = items * seq * (seq + TILE) // 2
     return pl.pallas_call(
-        functools.partial(_attend_kernel, items),
+        functools.partial(_attend_kernel, items, first),
         in_specs=[pl.BlockSpec(memory_space=pl.ANY)] + [pl.BlockSpec(memory_space=pltpu.VMEM)] * 2,
         out_specs=[pl.BlockSpec(memory_space=pl.ANY), pl.BlockSpec(memory_space=pltpu.VMEM)],
         out_shape=[
@@ -268,7 +271,7 @@
             jax.ShapeDtypeStruct((8, HDIM), jnp.float32),
         ],
         scratch_shapes=[
-            pltpu.VMEM(x.shape, x.dtype),
+            pltpu.VMEM((peers, 4 * items, rows, HDIM), x.dtype),
             pltpu.VMEM((peers, 3 * items, rows, HDIM), jnp.bfloat16),
             pltpu.VMEM((items, blocks, TILE, HDIM), jnp.bfloat16),
             pltpu.VMEM((items, blocks, HDIM, TILE), jnp.bfloat16),
@@ -289,12 +292,15 @@
     )(x, bias, prior)
 
 
-def spread_sum(x, size):
-    pair = x + lax.ppermute(x, "dp", [(d, d ^ 1) for d in range(size)])
-    parts = [pair]
-    for step in range(2, size, 2):
-        parts.append(lax.ppermute(pair, "dp", [(d, d ^ step) for d in range(size)]))
-    return sum(parts[1:], parts[0])
+def pair_sum(x, size):
+    return x + lax.ppermute(x, "dp", [(d, d ^ 1) for d in range(size)])
+
+
+def others(pair, size):
+    return [
+        lax.ppermute(pair, "dp", [(d, d ^ step) for d in range(size)])
+        for step in range(2, size, 2)
+    ]
 
 
 def body(queries, key_states, value_states, grad_output, query_bias, *, dp_size):
@@ -305,26 +311,26 @@
 
     own = lax.broadcasted_iota(jnp.int32, (dp_size, share), 0) == me
     slots = jnp.where(own, query_bias[None, :], jnp.zeros((), query_bias.dtype))
-    bias = spread_sum(slots, dp_size).astype(jnp.float32).reshape(1, dp_size * share)
+    pair = pair_sum(slots, dp_size)
+    parts = others(pair, dp_size)
+
+    packed = pack(inputs, tuple(range(items)), 4)
+    moved = lax.all_to_all(packed, "seq", split_axis=0, concat_axis=0, tiled=True)
+    moved, pair = lax.optimization_barrier((moved, pair))
+    bias = sum(parts, pair).astype(jnp.float32).reshape(1, dp_size * share)
 
     sums = jnp.zeros((8, HDIM), jnp.float32)
-    received = {}
-    for first, chunk in enumerate(IN_CHUNKS):
-        packed = pack(inputs, chunk, 4)
-        if GATE == first:
-            packed, bias = lax.optimization_barrier((packed, bias))
-        moved = lax.all_to_all(packed, "seq", split_axis=0, concat_axis=0, tiled=True)
-        for n, item in enumerate(chunk):
-            received[item] = moved[:, 4 * n : 4 * n + 4]
+    results = []
+    for chunk in OUT_CHUNKS:
+        grads, sums = attend(moved, bias, sums, chunk[0], len(chunk))
+        results.append(lax.all_to_all(grads, "seq", split_axis=0, concat_axis=0, tiled=True))
     outs = None
-    for chunk in OUT_CHUNKS:
-        x = jnp.concatenate([received[item] for item in chunk], axis=1)
-        grads, sums = attend(x, bias, sums, len(chunk))
-        packed = lax.all_to_all(grads, "seq", split_axis=0, concat_axis=0, tiled=True)
+    for chunk, packed in zip(OUT_CHUNKS, results):
         outs = unpack(packed, chunk, 3, items, 4, into=outs)
-        if chunk[0] == 0 and len(OUT_CHUNKS) > 1:
+        if chunk[-1] < items - 1:
             outs, sums = lax.optimization_barrier((outs, sums))
-    total = spread_sum(jnp.sum(sums, axis=0).reshape(dp_size, share), dp_size)
+    pair = pair_sum(jnp.sum(sums, axis=0).reshape(dp_size, share), dp_size)
+    total = sum(others(pair, dp_size), pair)
     grad_bias = lax.dynamic_index_in_dim(total, me, 0, keepdims=False)
     return (*outs, grad_bias)
 

time: 156 us -> 150 us (0.962)
  waiting for transfers between devices: 92.1 us -> 79.6 us
  starting transfers between devices: 34.1 us -> 38.2 us
  Pallas kernels: 25.3 us -> 28.9 us
    ppermute x8, waiting for transfers between devices: 81.8 us -> 2.31 us  [the longest x2 2.3 us: pair_sum(): return x + lax.ppermute(x, 'dp', [(d, d ^ 1) for d in range(size)])]
    all_to_all x1, waiting for transfers between devices: 5.83 us -> 55.3 us  [body(): lax.all_to_all(packed, 'seq', split_axis=0, concat_axis=0, tiled=True)]
    all_to_all x1 -> x2, waiting for transfers between devices: 4.47 us -> 21.9 us  [body(): lax.all_to_all(grads, 'seq', split_axis=0, concat_axis=0, tiled=True)]
    all_to_all x1 -> x2, starting transfers between devices: 10.8 us -> 14.9 us  [body(): lax.all_to_all(grads, 'seq', split_axis=0, concat_axis=0, tiled=True)]
    pallas_call x1 -> x2, Pallas kernels: 19.8 us -> 22.6 us  [attend(): pl.pallas_call(functools.partial(_attend_kernel, items, first), in_specs=...]
  transfers between devices with their start and end apart: 10 -> 11, of which waited for: 8 -> 5; matrix products, arithmetic and copies ran while one was open for 1% -> 0% of each run, Pallas kernels for 0% -> 9%
where the time goes in v6:
time: 150 us; the launch traced here: 149 us
  waiting for transfers between devices  79.6 us (53%)
  starting transfers between devices  38.2 us (25%)
  Pallas kernels  28.9 us (19%)
  local copies, waits for them, and re-layouts  1.8 us (1%)
    all_to_all x1, waiting for transfers between devices, body(): lax.all_to_all(packed, 'seq', split_axis=0, concat_axis=0, tiled=True)  55.3 us
    pallas_call x2, Pallas kernels, attend(): pl.pallas_call(functools.partial(_attend_kernel, items, first), in_specs=...  22.6 us
    all_to_all x2, waiting for transfers between devices, body(): lax.all_to_all(grads, 'seq', split_axis=0, concat_axis=0, tiled=True)  21.9 us
    all_to_all x2, starting transfers between devices, body(): lax.all_to_all(grads, 'seq', split_axis=0, concat_axis=0, tiled=True)  14.9 us
    ppermute x6, starting transfers between devices, others(): lax.ppermute(pair, 'dp', [(d, d ^ step) for d in range(size)])  14.3 us
    all_to_all x1, starting transfers between devices, body(): lax.all_to_all(packed, 'seq', split_axis=0, concat_axis=0, tiled=True)  8.95 us
    pallas_call x1, Pallas kernels, pack(): pl.pallas_call(functools.partial(_pack_kernel, items, count, groups), in_...  3.71 us
  transfers between devices with their start and end apart: 11, of which 5 were waited for; matrix products, arithmetic and copies ran while one was open for 0% of the time, Pallas kernels for 9%

profile of v6, /device:TPU:8, one launch (start us, length us, event | category | flops | bytes accessed | tf_op | source)
XLA Modules:
  0.0 149.4 jit_solution(14694060635311796984)
XLA Ops:
  0.6 3.7 %pack.1 = bf16[32,8,64,128]{3,2,1,0:T(8,128)(2,1)} custom-call(bf16[2,64,4096]{2,1,0:T(8,128)(2,1)} %refs_0_.1, bf16[2,64,4096]{2,1,0:T(8,128)(2,1)} %refs_1_.1, bf16[2,64,4096]{2,1,0:T(8,128)(2,1)} %refs_2_.1, bf16[2,64,4096]{2,1,0:T(8,128)(2,1)} %refs_3_.1), custom_call_target="tpu_custom_call" | custom-call | bytes 8388608 | tf_op jit(solution)/shard_map/pack/pallas_call | solution.py:52
  4.4 9.0 %all-to-all-start = ((bf16[32,8,64,128]{3,2,1,0:T(8,128)(2,1)}), bf16[32,8,64,128]{3,2,1,0:T(8,128)(2,1)}, u32[]{:S(2)}, u32[]{:S(2)}) async-start(bf16[32,8,64,128]{3,2,1,0:T(8,128)(2,1)} %pack.1), calls=%async_computation | async-start | bytes 8388608 | tf_op jit(solution)/shard_map/all_to_all | solution.py:318
  13.4 0.1 broadcast_select_fusion
  13.5 1.1 collective-permute-done
  14.7 5.4 %collective-permute-start.3 = (bf16[8,16]{1,0:T(8,128)(2,1)S(1)}, bf16[8,16]{1,0:T(8,128)(2,1)S(1)}, u32[]{:S(2)}, u32[]{:S(2)}) collective-permute-start(bf16[8,16]{1,0:T(8,128)(2,1)S(1)} %fusion), channel_id=1, source_target_pairs={{0,6},{1,7},{2,4},{3,5},{4,2},{5,3},{6,0},{7,1},{8,14},{9,15},{10,... | collective-permute-start | bytes 776 | tf_op jit(solution)/shard_map/ppermute | solution.py:301
  20.1 1.4 collective-permute-start.2
  21.5 0.9 collective-permute-start.1
  22.5 55.3 %all-to-all-done.x_hbm = bf16[32,8,64,128]{3,2,1,0:T(8,128)(2,1)} async-done(((bf16[32,8,64,128]{3,2,1,0:T(8,128)(2,1)}), bf16[32,8,64,128]{3,2,1,0:T(8,128)(2,1)}, u32[]{:S(2)}, u32[]{:S(2)}) %all-to-all-start) | async-done | bytes 4194336 | tf_op jit(solution)/shard_map/all_to_all | solution.py:318
  77.8 0.6 reshape.21.bias_ref
  78.4 0.6 broadcast_in_dim.18.prior_ref
  79.0 11.3 %attend.2 = (bf16[32,3,64,128]{3,2,1,0:T(8,128)(2,1)}, f32[8,128]{1,0:T(8,128)}) custom-call(bf16[32,8,64,128]{3,2,1,0:T(8,128)(2,1)} %all-to-all-done.x_hbm, f32[1,128]{1,0:T(1,128)} %reshape.21.bias_ref, f32[8,128]{1,0:T(8,128)} %broadcast_in_dim.18.prior_ref), custom_call_target="tpu_custom_call" | custom-call | flops 3019898880 | bytes 3670016 | tf_op jit(solution)/shard_map/attend/pallas_call | solution.py:265
  90.3 10.1 %all-to-all-start.2 = ((bf16[32,3,64,128]{3,2,1,0:T(8,128)(2,1)}), bf16[32,3,64,128]{3,2,1,0:T(8,128)(2,1)S(1)}, u32[]{:S(2)}, u32[]{:S(2)}) async-start(bf16[32,3,64,128]{3,2,1,0:T(8,128)(2,1)} %get-tuple-element.24), calls=%async_computation.2 | async-start | bytes 3145728 | tf_op jit(solution)/shard_map/all_to_all | solution.py:326
  100.4 11.3 %attend.3 = (bf16[32,3,64,128]{3,2,1,0:T(8,128)(2,1)}, f32[8,128]{1,0:T(8,128)}) custom-call(bf16[32,8,64,128]{3,2,1,0:T(8,128)(2,1)} %all-to-all-done.x_hbm, f32[1,128]{1,0:T(1,128)} %reshape.21.bias_ref, f32[8,128]{1,0:T(8,128)} %get-tuple-element.22.prior_ref), custom_call_target="tpu_custom_call" | custom-call | flops 3019898880 | bytes 3670016 | tf_op jit(solution)/shard_map/attend/pallas_call | solution.py:265
  111.7 10.6 %all-to-all-done.2.refs_0_ = bf16[32,3,64,128]{3,2,1,0:T(8,128)(2,1)S(1)} async-done(((bf16[32,3,64,128]{3,2,1,0:T(8,128)(2,1)}), bf16[32,3,64,128]{3,2,1,0:T(8,128)(2,1)S(1)}, u32[]{:S(2)}, u32[]{:S(2)}) %all-to-all-start.2) | async-done | bytes 1572896 | tf_op jit(solution)/shard_map/all_to_all | solution.py:326
  122.4 4.8 %all-to-all-start.1 = ((bf16[32,3,64,128]{3,2,1,0:T(8,128)(2,1)}), bf16[32,3,64,128]{3,2,1,0:T(8,128)(2,1)S(1)}, u32[]{:S(2)}, u32[]{:S(2)}) async-start(bf16[32,3,64,128]{3,2,1,0:T(8,128)(2,1)} %get-tuple-element.23), calls=%async_computation.1 | async-start | bytes 3145728 | tf_op jit(solution)/shard_map/all_to_all | solution.py:326
  127.2 1.3 unpack.2
  128.5 0.1 reshape.19
  128.6 1.2 collective-permute-done.4
  129.8 3.2 %collective-permute-start.7 = (f32[8,16]{1,0:T(8,128)S(1)}, f32[8,16]{1,0:T(8,128)S(1)}, u32[]{:S(2)}, u32[]{:S(2)}) collective-permute-start(f32[8,16]{1,0:T(8,128)S(1)} %add.32), channel_id=1, source_target_pairs={{0,6},{1,7},{2,4},{3,5},{4,2},{5,3},{6,0},{7,1},{8,14},{9,15},{10,... | collective-permute-start | bytes 1544 | tf_op jit(solution)/shard_map/ppermute | solution.py:301
  133.0 1.8 %collective-permute-start.6 = (f32[8,16]{1,0:T(8,128)S(1)}, f32[8,16]{1,0:T(8,128)S(1)}, u32[]{:S(2)}, u32[]{:S(2)}) collective-permute-start(f32[8,16]{1,0:T(8,128)S(1)} %add.32), channel_id=1, source_target_pairs={{0,4},{1,5},{2,6},{3,7},{4,0},{5,1},{6,2},{7,3},{8,12},{9,13},{10,... | collective-permute-start | bytes 1544 | tf_op jit(solution)/shard_map/ppermute | solution.py:301
  134.8 1.5 collective-permute-start.5
  136.2 11.3 %all-to-all-done.1.refs_0_ = bf16[32,3,64,128]{3,2,1,0:T(8,128)(2,1)S(1)} async-done(((bf16[32,3,64,128]{3,2,1,0:T(8,128)(2,1)}), bf16[32,3,64,128]{3,2,1,0:T(8,128)(2,1)S(1)}, u32[]{:S(2)}, u32[]{:S(2)}) %all-to-all-start.1) | async-done | bytes 1572896 | tf_op jit(solution)/shard_map/all_to_all | solution.py:326
  147.6 1.3 unpack.3
  148.9 0.5 dynamic-slice_bitcast_fusion
  (18 shorter events, 0.2 us)
Async XLA Ops:
  4.4 9.0 %copy-start.1 = (bf16[16]{0:T(256)(128)(2,1)S(1)}, bf16[16]{0:T(256)(128)(2,1)}, u32[]{:S(2)}) copy-start(bf16[16]{0:T(256)(128)(2,1)} %param.9) | copy-start | bytes 100
  4.4 73.4 %all-to-all-start = ((bf16[32,8,64,128]{3,2,1,0:T(8,128)(2,1)}), bf16[32,8,64,128]{3,2,1,0:T(8,128)(2,1)}, u32[]{:S(2)}, u32[]{:S(2)}) async-start(bf16[32,8,64,128]{3,2,1,0:T(8,128)(2,1)} %pack.1), calls=%async_computation | async-start | bytes 8388608 | tf_op jit(solution)/shard_map/all_to_all | solution.py:318
  13.4 1.2 collective-permute-start
  14.7 63.1 %collective-permute-start.3 = (bf16[8,16]{1,0:T(8,128)(2,1)S(1)}, bf16[8,16]{1,0:T(8,128)(2,1)S(1)}, u32[]{:S(2)}, u32[]{:S(2)}) collective-permute-start(bf16[8,16]{1,0:T(8,128)(2,1)S(1)} %fusion), channel_id=1, source_target_pairs={{0,6},{1,7},{2,4},{3,5},{4,2},{5,3},{6,0},{7,1},{8,14},{9,15},{10,... | collective-permute-start | bytes 776 | tf_op jit(solution)/shard_map/ppermute | solution.py:301
  20.1 57.7 %collective-permute-start.2 = (bf16[8,16]{1,0:T(8,128)(2,1)S(1)}, bf16[8,16]{1,0:T(8,128)(2,1)S(1)}, u32[]{:S(2)}, u32[]{:S(2)}) collective-permute-start(bf16[8,16]{1,0:T(8,128)(2,1)S(1)} %fusion), channel_id=1, source_target_pairs={{0,4},{1,5},{2,6},{3,7},{4,0},{5,1},{6,2},{7,3},{8,12},{9,13},{10,... | collective-permute-start | bytes 776 | tf_op jit(solution)/shard_map/ppermute | solution.py:301
  21.5 56.3 %collective-permute-start.1 = (bf16[8,16]{1,0:T(8,128)(2,1)S(1)}, bf16[8,16]{1,0:T(8,128)(2,1)S(1)}, u32[]{:S(2)}, u32[]{:S(2)}) collective-permute-start(bf16[8,16]{1,0:T(8,128)(2,1)S(1)} %fusion), channel_id=1, source_target_pairs={{0,2},{1,3},{2,0},{3,1},{4,6},{5,7},{6,4},{7,5},{8,10},{9,11},{10,... | collective-permute-start | bytes 776 | tf_op jit(solution)/shard_map/ppermute | solution.py:301
  90.3 32.0 %all-to-all-start.2 = ((bf16[32,3,64,128]{3,2,1,0:T(8,128)(2,1)}), bf16[32,3,64,128]{3,2,1,0:T(8,128)(2,1)S(1)}, u32[]{:S(2)}, u32[]{:S(2)}) async-start(bf16[32,3,64,128]{3,2,1,0:T(8,128)(2,1)} %get-tuple-element.24), calls=%async_computation.2 | async-start | bytes 3145728 | tf_op jit(solution)/shard_map/all_to_all | solution.py:326
  122.4 25.2 %all-to-all-start.1 = ((bf16[32,3,64,128]{3,2,1,0:T(8,128)(2,1)}), bf16[32,3,64,128]{3,2,1,0:T(8,128)(2,1)S(1)}, u32[]{:S(2)}, u32[]{:S(2)}) async-start(bf16[32,3,64,128]{3,2,1,0:T(8,128)(2,1)} %get-tuple-element.23), calls=%async_computation.1 | async-start | bytes 3145728 | tf_op jit(solution)/shard_map/all_to_all | solution.py:326
  127.2 1.3 copy-start
  128.6 1.2 collective-permute-start.4
  129.8 19.1 %collective-permute-start.7 = (f32[8,16]{1,0:T(8,128)S(1)}, f32[8,16]{1,0:T(8,128)S(1)}, u32[]{:S(2)}, u32[]{:S(2)}) collective-permute-start(f32[8,16]{1,0:T(8,128)S(1)} %add.32), channel_id=1, source_target_pairs={{0,6},{1,7},{2,4},{3,5},{4,2},{5,3},{6,0},{7,1},{8,14},{9,15},{10,... | collective-permute-start | bytes 1544 | tf_op jit(solution)/shard_map/ppermute | solution.py:301
  133.0 15.9 %collective-permute-start.6 = (f32[8,16]{1,0:T(8,128)S(1)}, f32[8,16]{1,0:T(8,128)S(1)}, u32[]{:S(2)}, u32[]{:S(2)}) collective-permute-start(f32[8,16]{1,0:T(8,128)S(1)} %add.32), channel_id=1, source_target_pairs={{0,4},{1,5},{2,6},{3,7},{4,0},{5,1},{6,2},{7,3},{8,12},{9,13},{10,... | collective-permute-start | bytes 1544 | tf_op jit(solution)/shard_map/ppermute | solution.py:301
  134.8 14.1 %collective-permute-start.5 = (f32[8,16]{1,0:T(8,128)S(1)}, f32[8,16]{1,0:T(8,128)S(1)}, u32[]{:S(2)}, u32[]{:S(2)}) collective-permute-start(f32[8,16]{1,0:T(8,128)S(1)} %add.32), channel_id=1, source_target_pairs={{0,2},{1,3},{2,0},{3,1},{4,6},{5,7},{6,4},{7,5},{8,10},{9,11},{10,... | collective-permute-start | bytes 1544 | tf_op jit(solution)/shard_map/ppermute | solution.py:301

commit v7 on v2

--- a/solution.py
+++ b/solution.py
@@ -219,8 +219,11 @@
     )(x, bias, prior)
 
 
-def spread_sum(x, size):
-    pair = x + lax.ppermute(x, "dp", [(d, d ^ 1) for d in range(size)])
+def pair_sum(x, size):
+    return x + lax.ppermute(x, "dp", [(d, d ^ 1) for d in range(size)])
+
+
+def spread_sum(pair, size):
     parts = [pair]
     for step in range(2, size, 2):
         parts.append(lax.ppermute(pair, "dp", [(d, d ^ step) for d in range(size)]))
@@ -235,12 +238,13 @@
 
     own = lax.broadcasted_iota(jnp.int32, (dp_size, share), 0) == me
     slots = jnp.where(own, query_bias[None, :], jnp.zeros((), query_bias.dtype))
-    bias = spread_sum(slots, dp_size).astype(jnp.float32).reshape(1, dp_size * share)
+    first, pair = lax.optimization_barrier((pack(inputs, 0, 4), pair_sum(slots, dp_size)))
+    bias = spread_sum(pair, dp_size).astype(jnp.float32).reshape(1, dp_size * share)
 
     sums = jnp.zeros((8, HDIM), jnp.float32)
     results = []
     for item in range(items):
-        packed = pack(inputs, item, 4)
+        packed = first if item == 0 else pack(inputs, item, 4)
         if item == 1:
             packed, bias = lax.optimization_barrier((packed, bias))
         moved = lax.all_to_all(packed, "seq", split_axis=0, concat_axis=0, tiled=True)
@@ -251,7 +255,7 @@
         outs = unpack(packed, item, items, 4, into=outs)
         if item == 0:
             outs, sums = lax.optimization_barrier((outs, sums))
-    total = spread_sum(jnp.sum(sums, axis=0).reshape(dp_size, share), dp_size)
+    total = spread_sum(pair_sum(jnp.sum(sums, axis=0).reshape(dp_size, share), dp_size), dp_size)
     grad_bias = lax.dynamic_index_in_dim(total, me, 0, keepdims=False)
     return (*outs, grad_bias)
 

time: 134 us -> 140 us (1.045)
  waiting for transfers between devices: 59.2 us -> 64.6 us
    ppermute x6, waiting for transfers between devices: 19.4 us -> 22.7 us  [spread_sum(): parts.append(lax.ppermute(pair, 'dp', [(d, d ^ step) for d in range(size)]))]
    all_to_all x2, waiting for transfers between devices: 18.8 us -> 20.5 us  [body(): lax.all_to_all(grads, 'seq', split_axis=0, concat_axis=0, tiled=True)]
    all_to_all x2, waiting for transfers between devices: 18.7 us -> 20.2 us  [body(): lax.all_to_all(packed, 'seq', split_axis=0, concat_axis=0, tiled=True)]
  transfers between devices with their start and end apart: 12 -> 12, of which waited for: 7 -> 7; matrix products, arithmetic and copies ran while one was open for 0% -> 0% of each run, Pallas kernels for 19% -> 20%
where the time goes in v7:
time: 140 us
  waiting for transfers between devices  64.6 us (46%)
  starting transfers between devices  42.1 us (30%)
  Pallas kernels  28.6 us (20%)
  local copies, waits for them, and re-layouts  3.05 us (2%)
    ppermute x6, waiting for transfers between devices, spread_sum(): parts.append(lax.ppermute(pair, 'dp', [(d, d ^ step) for d in range(size)]))  22.7 us
    pallas_call x2, Pallas kernels, attend(): pl.pallas_call(_attend_kernel, in_specs=[pl.BlockSpec(memory_space=pltpu....  20.8 us
    all_to_all x2, waiting for transfers between devices, body(): lax.all_to_all(grads, 'seq', split_axis=0, concat_axis=0, tiled=True)  20.5 us
    all_to_all x2, waiting for transfers between devices, body(): lax.all_to_all(packed, 'seq', split_axis=0, concat_axis=0, tiled=True)  20.2 us
    all_to_all x2, starting transfers between devices, body(): lax.all_to_all(packed, 'seq', split_axis=0, concat_axis=0, tiled=True)  18 us
    ppermute x6, starting transfers between devices, spread_sum(): parts.append(lax.ppermute(pair, 'dp', [(d, d ^ step) for d in range(size)]))  14.3 us
    all_to_all x2, starting transfers between devices, body(): lax.all_to_all(grads, 'seq', split_axis=0, concat_axis=0, tiled=True)  9.74 us
    pallas_call x2, Pallas kernels, pack(): pl.pallas_call(functools.partial(_pack_kernel, item, count, groups), in_s...  5.3 us
  transfers between devices with their start and end apart: 12, of which 7 were waited for; matrix products, arithmetic and copies ran while one was open for 0% of the time, Pallas kernels for 20%

profile of v7, /device:TPU:8, one launch (start us, length us, event | category | flops | bytes accessed | tf_op | source)
XLA Modules:
  0.0 139.9 jit_solution(2937994855704037121)
XLA Ops:
  0.6 0.7 broadcast_select_fusion
  1.4 2.6 %pack.3 = bf16[32,4,64,128]{3,2,1,0:T(8,128)(2,1)} custom-call(bf16[2,64,4096]{2,1,0:T(8,128)(2,1)} %refs_0_.3, bf16[2,64,4096]{2,1,0:T(8,128)(2,1)} %refs_1_.3, bf16[2,64,4096]{2,1,0:T(8,128)(2,1)} %refs_2_.3, bf16[2,64,4096]{2,1,0:T(8,128)(2,1)} %refs_3_.3), custom_call_target="tpu_custom_call" | custom-call | bytes 4194304 | tf_op jit(solution)/shard_map/pack/pallas_call | solution.py:49
  4.1 8.9 %all-to-all-start.1 = ((bf16[32,4,64,128]{3,2,1,0:T(8,128)(2,1)}), bf16[32,4,64,128]{3,2,1,0:T(8,128)(2,1)S(1)}, u32[]{:S(2)}, u32[]{:S(2)}) async-start(bf16[32,4,64,128]{3,2,1,0:T(8,128)(2,1)} %pack.3), calls=%async_computation.1 | async-start | bytes 4194304 | tf_op jit(solution)/shard_map/all_to_all | solution.py:250
  13.0 3.4 %collective-permute-start.1 = (bf16[8,16]{1,0:T(8,128)(2,1)S(1)}, bf16[8,16]{1,0:T(8,128)(2,1)S(1)}, u32[]{:S(2)}, u32[]{:S(2)}) collective-permute-start(bf16[8,16]{1,0:T(8,128)(2,1)S(1)} %fusion), channel_id=1, source_target_pairs={{0,2},{1,3},{2,0},{3,1},{4,6},{5,7},{6,4},{7,5},{8,10},{9,11},{10,... | collective-permute-start | bytes 776 | tf_op jit(solution)/shard_map/ppermute | solution.py:229
  16.4 4.5 %collective-permute-start.2 = (bf16[8,16]{1,0:T(8,128)(2,1)S(1)}, bf16[8,16]{1,0:T(8,128)(2,1)S(1)}, u32[]{:S(2)}, u32[]{:S(2)}) collective-permute-start(bf16[8,16]{1,0:T(8,128)(2,1)S(1)} %fusion), channel_id=1, source_target_pairs={{0,4},{1,5},{2,6},{3,7},{4,0},{5,1},{6,2},{7,3},{8,12},{9,13},{10,... | collective-permute-start | bytes 776 | tf_op jit(solution)/shard_map/ppermute | solution.py:229
  20.9 2.7 %pack.2 = bf16[32,4,64,128]{3,2,1,0:T(8,128)(2,1)} custom-call(bf16[2,64,4096]{2,1,0:T(8,128)(2,1)} %refs_0_.3, bf16[2,64,4096]{2,1,0:T(8,128)(2,1)} %refs_1_.3, bf16[2,64,4096]{2,1,0:T(8,128)(2,1)} %refs_2_.3, bf16[2,64,4096]{2,1,0:T(8,128)(2,1)} %refs_3_.3), custom_call_target="tpu_custom_call" | custom-call | bytes 4194304 | tf_op jit(solution)/shard_map/pack/pallas_call | solution.py:49
  23.5 16.0 %collective-permute-done.1 = bf16[8,16]{1,0:T(8,128)(2,1)S(1)} collective-permute-done((bf16[8,16]{1,0:T(8,128)(2,1)S(1)}, bf16[8,16]{1,0:T(8,128)(2,1)S(1)}, u32[]{:S(2)}, u32[]{:S(2)}) %collective-permute-start.1) | collective-permute-done | bytes 288 | tf_op jit(solution)/shard_map/ppermute | solution.py:229
  39.6 6.7 %collective-permute-done.2 = bf16[8,16]{1,0:T(8,128)(2,1)S(1)} collective-permute-done((bf16[8,16]{1,0:T(8,128)(2,1)S(1)}, bf16[8,16]{1,0:T(8,128)(2,1)S(1)}, u32[]{:S(2)}, u32[]{:S(2)}) %collective-permute-start.2) | collective-permute-done | bytes 288 | tf_op jit(solution)/shard_map/ppermute | solution.py:229
  46.8 9.1 %all-to-all-start = ((bf16[32,4,64,128]{3,2,1,0:T(8,128)(2,1)}), bf16[32,4,64,128]{3,2,1,0:T(8,128)(2,1)}, u32[]{:S(2)}, u32[]{:S(2)}) async-start(bf16[32,4,64,128]{3,2,1,0:T(8,128)(2,1)} %pack.2), calls=%async_computation | async-start | bytes 4194304 | tf_op jit(solution)/shard_map/all_to_all | solution.py:250
  55.9 9.6 %attend.2 = (bf16[32,3,64,128]{3,2,1,0:T(8,128)(2,1)S(1)}, f32[8,128]{1,0:T(8,128)S(1)}) custom-call(bf16[32,4,64,128]{3,2,1,0:T(8,128)(2,1)S(1)} %all-to-all-done.1.x_ref, f32[1,128]{1,0:T(1,128)S(1)} %reshape.21.bias_ref, f32[8,128]{1,0:T(8,128)S(1)} %broadcast_in_dim.18.prior_ref), custom_call_target="tpu_custom_call" | custom-call | flops 6039797760 | bytes 3670016 | tf_op jit(solution)/shard_map/attend/pallas_call | solution.py:198
  65.5 1.2 copy-done.1
  66.7 19.8 %all-to-all-done.x_ref = bf16[32,4,64,128]{3,2,1,0:T(8,128)(2,1)} async-done(((bf16[32,4,64,128]{3,2,1,0:T(8,128)(2,1)}), bf16[32,4,64,128]{3,2,1,0:T(8,128)(2,1)}, u32[]{:S(2)}, u32[]{:S(2)}) %all-to-all-start) | async-done | bytes 2097184 | tf_op jit(solution)/shard_map/all_to_all | solution.py:250
  86.4 4.7 %all-to-all-start.3 = ((bf16[32,3,64,128]{3,2,1,0:T(8,128)(2,1)}), bf16[32,3,64,128]{3,2,1,0:T(8,128)(2,1)S(1)}, u32[]{:S(2)}, u32[]{:S(2)}) async-start(bf16[32,3,64,128]{3,2,1,0:T(8,128)(2,1)} %copy-done.1), calls=%async_computation.3 | async-start | bytes 3145728 | tf_op jit(solution)/shard_map/all_to_all | solution.py:252
  91.2 11.2 %attend.3 = (bf16[32,3,64,128]{3,2,1,0:T(8,128)(2,1)S(1)}, f32[8,128]{1,0:T(8,128)S(1)}) custom-call(bf16[32,4,64,128]{3,2,1,0:T(8,128)(2,1)} %all-to-all-done.x_ref, f32[1,128]{1,0:T(1,128)S(1)} %reshape.21.bias_ref, f32[8,128]{1,0:T(8,128)S(1)} %get-tuple-element.26.prior_ref), custom_call_target="tpu_custom_call" | custom-call | flops 6039797760 | bytes 3670016 | tf_op jit(solution)/shard_map/attend/pallas_call | solution.py:198
  102.4 1.2 copy-done
  103.6 9.0 %all-to-all-done.3.refs_0_ = bf16[32,3,64,128]{3,2,1,0:T(8,128)(2,1)S(1)} async-done(((bf16[32,3,64,128]{3,2,1,0:T(8,128)(2,1)}), bf16[32,3,64,128]{3,2,1,0:T(8,128)(2,1)S(1)}, u32[]{:S(2)}, u32[]{:S(2)}) %all-to-all-start.3) | async-done | bytes 1572896 | tf_op jit(solution)/shard_map/all_to_all | solution.py:252
  112.6 5.0 %all-to-all-start.2 = ((bf16[32,3,64,128]{3,2,1,0:T(8,128)(2,1)}), bf16[32,3,64,128]{3,2,1,0:T(8,128)(2,1)S(1)}, u32[]{:S(2)}, u32[]{:S(2)}) async-start(bf16[32,3,64,128]{3,2,1,0:T(8,128)(2,1)} %copy-done), calls=%async_computation.2 | async-start | bytes 3145728 | tf_op jit(solution)/shard_map/all_to_all | solution.py:252
  117.6 1.3 unpack.2
  119.0 1.2 collective-permute-done.4
  120.2 1.7 %collective-permute-start.5 = (f32[8,16]{1,0:T(8,128)S(1)}, f32[8,16]{1,0:T(8,128)S(1)}, u32[]{:S(2)}, u32[]{:S(2)}) collective-permute-start(f32[8,16]{1,0:T(8,128)S(1)} %add.32), channel_id=1, source_target_pairs={{0,2},{1,3},{2,0},{3,1},{4,6},{5,7},{6,4},{7,5},{8,10},{9,11},{10,... | collective-permute-start | bytes 1544 | tf_op jit(solution)/shard_map/ppermute | solution.py:229
  121.8 2.4 %collective-permute-start.6 = (f32[8,16]{1,0:T(8,128)S(1)}, f32[8,16]{1,0:T(8,128)S(1)}, u32[]{:S(2)}, u32[]{:S(2)}) collective-permute-start(f32[8,16]{1,0:T(8,128)S(1)} %add.32), channel_id=1, source_target_pairs={{0,4},{1,5},{2,6},{3,7},{4,0},{5,1},{6,2},{7,3},{8,12},{9,13},{10,... | collective-permute-start | bytes 1544 | tf_op jit(solution)/shard_map/ppermute | solution.py:229
  124.2 2.4 %collective-permute-start.7 = (f32[8,16]{1,0:T(8,128)S(1)}, f32[8,16]{1,0:T(8,128)S(1)}, u32[]{:S(2)}, u32[]{:S(2)}) collective-permute-start(f32[8,16]{1,0:T(8,128)S(1)} %add.32), channel_id=1, source_target_pairs={{0,6},{1,7},{2,4},{3,5},{4,2},{5,3},{6,0},{7,1},{8,14},{9,15},{10,... | collective-permute-start | bytes 1544 | tf_op jit(solution)/shard_map/ppermute | solution.py:229
  126.7 11.4 %all-to-all-done.2.refs_0_ = bf16[32,3,64,128]{3,2,1,0:T(8,128)(2,1)S(1)} async-done(((bf16[32,3,64,128]{3,2,1,0:T(8,128)(2,1)}), bf16[32,3,64,128]{3,2,1,0:T(8,128)(2,1)S(1)}, u32[]{:S(2)}, u32[]{:S(2)}) %all-to-all-start.2) | async-done | bytes 1572896 | tf_op jit(solution)/shard_map/all_to_all | solution.py:252
  138.1 1.3 unpack.3
  (23 shorter events, 1.3 us)
Async XLA Ops:
  1.4 2.7 %copy-start.2 = (bf16[16]{0:T(256)(128)(2,1)S(1)}, bf16[16]{0:T(256)(128)(2,1)}, u32[]{:S(2)}) copy-start(bf16[16]{0:T(256)(128)(2,1)} %param.9) | copy-start | bytes 100
  1.4 2.7 %collective-permute-start = (bf16[8,16]{1,0:T(8,128)(2,1)S(1)}, bf16[8,16]{1,0:T(8,128)(2,1)S(1)}, u32[]{:S(2)}, u32[]{:S(2)}) collective-permute-start(bf16[8,16]{1,0:T(8,128)(2,1)S(1)} %broadcast_select_fusion), channel_id=1, source_target_pairs={{0,1},{1,0},{2,3},{3,2},{4,5},{5,4},{6,7},{7,6},{8,9},{9,8},{10,11... | collective-permute-start | bytes 776 | tf_op jit(solution)/shard_map/ppermute | solution.py:223
  4.1 42.7 %all-to-all-start.1 = ((bf16[32,4,64,128]{3,2,1,0:T(8,128)(2,1)}), bf16[32,4,64,128]{3,2,1,0:T(8,128)(2,1)S(1)}, u32[]{:S(2)}, u32[]{:S(2)}) async-start(bf16[32,4,64,128]{3,2,1,0:T(8,128)(2,1)} %pack.3), calls=%async_computation.1 | async-start | bytes 4194304 | tf_op jit(solution)/shard_map/all_to_all | solution.py:250
  13.0 26.5 %collective-permute-start.1 = (bf16[8,16]{1,0:T(8,128)(2,1)S(1)}, bf16[8,16]{1,0:T(8,128)(2,1)S(1)}, u32[]{:S(2)}, u32[]{:S(2)}) collective-permute-start(bf16[8,16]{1,0:T(8,128)(2,1)S(1)} %fusion), channel_id=1, source_target_pairs={{0,2},{1,3},{2,0},{3,1},{4,6},{5,7},{6,4},{7,5},{8,10},{9,11},{10,... | collective-permute-start | bytes 776 | tf_op jit(solution)/shard_map/ppermute | solution.py:229
  16.4 29.9 %collective-permute-start.2 = (bf16[8,16]{1,0:T(8,128)(2,1)S(1)}, bf16[8,16]{1,0:T(8,128)(2,1)S(1)}, u32[]{:S(2)}, u32[]{:S(2)}) collective-permute-start(bf16[8,16]{1,0:T(8,128)(2,1)S(1)} %fusion), channel_id=1, source_target_pairs={{0,4},{1,5},{2,6},{3,7},{4,0},{5,1},{6,2},{7,3},{8,12},{9,13},{10,... | collective-permute-start | bytes 776 | tf_op jit(solution)/shard_map/ppermute | solution.py:229
  20.9 25.4 %collective-permute-start.3 = (bf16[8,16]{1,0:T(8,128)(2,1)S(1)}, bf16[8,16]{1,0:T(8,128)(2,1)S(1)}, u32[]{:S(2)}, u32[]{:S(2)}) collective-permute-start(bf16[8,16]{1,0:T(8,128)(2,1)S(1)} %fusion), channel_id=1, source_target_pairs={{0,6},{1,7},{2,4},{3,5},{4,2},{5,3},{6,0},{7,1},{8,14},{9,15},{10,... | collective-permute-start | bytes 776 | tf_op jit(solution)/shard_map/ppermute | solution.py:229
  46.8 39.6 %all-to-all-start = ((bf16[32,4,64,128]{3,2,1,0:T(8,128)(2,1)}), bf16[32,4,64,128]{3,2,1,0:T(8,128)(2,1)}, u32[]{:S(2)}, u32[]{:S(2)}) async-start(bf16[32,4,64,128]{3,2,1,0:T(8,128)(2,1)} %pack.2), calls=%async_computation | async-start | bytes 4194304 | tf_op jit(solution)/shard_map/all_to_all | solution.py:250
  65.5 1.2 copy-start.1
  86.4 26.2 %all-to-all-start.3 = ((bf16[32,3,64,128]{3,2,1,0:T(8,128)(2,1)}), bf16[32,3,64,128]{3,2,1,0:T(8,128)(2,1)S(1)}, u32[]{:S(2)}, u32[]{:S(2)}) async-start(bf16[32,3,64,128]{3,2,1,0:T(8,128)(2,1)} %copy-done.1), calls=%async_computation.3 | async-start | bytes 3145728 | tf_op jit(solution)/shard_map/all_to_all | solution.py:252
  102.4 1.2 copy-start
  112.6 25.5 %all-to-all-start.2 = ((bf16[32,3,64,128]{3,2,1,0:T(8,128)(2,1)}), bf16[32,3,64,128]{3,2,1,0:T(8,128)(2,1)S(1)}, u32[]{:S(2)}, u32[]{:S(2)}) async-start(bf16[32,3,64,128]{3,2,1,0:T(8,128)(2,1)} %copy-done), calls=%async_computation.2 | async-start | bytes 3145728 | tf_op jit(solution)/shard_map/all_to_all | solution.py:252
  119.0 1.2 collective-permute-start.4
  120.2 19.2 %collective-permute-start.5 = (f32[8,16]{1,0:T(8,128)S(1)}, f32[8,16]{1,0:T(8,128)S(1)}, u32[]{:S(2)}, u32[]{:S(2)}) collective-permute-start(f32[8,16]{1,0:T(8,128)S(1)} %add.32), channel_id=1, source_target_pairs={{0,2},{1,3},{2,0},{3,1},{4,6},{5,7},{6,4},{7,5},{8,10},{9,11},{10,... | collective-permute-start | bytes 1544 | tf_op jit(solution)/shard_map/ppermute | solution.py:229
  121.8 17.6 %collective-permute-start.6 = (f32[8,16]{1,0:T(8,128)S(1)}, f32[8,16]{1,0:T(8,128)S(1)}, u32[]{:S(2)}, u32[]{:S(2)}) collective-permute-start(f32[8,16]{1,0:T(8,128)S(1)} %add.32), channel_id=1, source_target_pairs={{0,4},{1,5},{2,6},{3,7},{4,0},{5,1},{6,2},{7,3},{8,12},{9,13},{10,... | collective-permute-start | bytes 1544 | tf_op jit(solution)/shard_map/ppermute | solution.py:229
  124.2 15.2 %collective-permute-start.7 = (f32[8,16]{1,0:T(8,128)S(1)}, f32[8,16]{1,0:T(8,128)S(1)}, u32[]{:S(2)}, u32[]{:S(2)}) collective-permute-start(f32[8,16]{1,0:T(8,128)S(1)} %add.32), channel_id=1, source_target_pairs={{0,6},{1,7},{2,4},{3,5},{4,2},{5,3},{6,0},{7,1},{8,14},{9,15},{10,... | collective-permute-start | bytes 1544 | tf_op jit(solution)/shard_map/ppermute | solution.py:229

commit v8 on v2

--- a/solution.py
+++ b/solution.py
@@ -227,6 +227,20 @@
     return sum(parts[1:], parts[0])
 
 
+def shared_sum(x, size, ahead):
+    swap = [(d, d ^ 1) for d in range(size)]
+    pair = x + lax.ppermute(x, "dp", swap)
+    pair, ahead = lax.optimization_barrier((pair, ahead))
+    got = None
+    for even, odd in ((2, 4), (6, None)):
+        moves = [(d, d ^ even) for d in range(0, size, 2)]
+        if odd is not None:
+            moves += [(d, d ^ odd) for d in range(1, size, 2)]
+        part = lax.ppermute(pair, "dp", moves)
+        got = part if got is None else got + part
+    return pair + got + lax.ppermute(got, "dp", swap), ahead
+
+
 def body(queries, key_states, value_states, grad_output, query_bias, *, dp_size):
     items, rows, width = queries.shape
     inputs = (queries, key_states, value_states, grad_output)
@@ -235,12 +249,13 @@
 
     own = lax.broadcasted_iota(jnp.int32, (dp_size, share), 0) == me
     slots = jnp.where(own, query_bias[None, :], jnp.zeros((), query_bias.dtype))
-    bias = spread_sum(slots, dp_size).astype(jnp.float32).reshape(1, dp_size * share)
+    bias, second = shared_sum(slots, dp_size, pack(inputs, 1, 4))
+    bias = bias.astype(jnp.float32).reshape(1, dp_size * share)
 
     sums = jnp.zeros((8, HDIM), jnp.float32)
     results = []
     for item in range(items):
-        packed = pack(inputs, item, 4)
+        packed = second if item == 1 else pack(inputs, item, 4)
         if item == 1:
             packed, bias = lax.optimization_barrier((packed, bias))
         moved = lax.all_to_all(packed, "seq", split_axis=0, concat_axis=0, tiled=True)

time: 134 us -> 140 us (1.045)
  waiting for transfers between devices: 59.2 us -> 64.8 us
    ppermute x0 -> x4, waiting for transfers between devices: none -> 19.7 us  [the longest x2 18.6 us: shared_sum(): part = lax.ppermute(pair, 'dp', moves)]
    ppermute x6 -> x3, waiting for transfers between devices: 19.4 us -> 0.01 us  [spread_sum(): parts.append(lax.ppermute(pair, 'dp', [(d, d ^ step) for d in range(size)]))]
    ppermute x0 -> x4, starting transfers between devices: none -> 8.81 us  [the longest x2 8.78 us: shared_sum(): part = lax.ppermute(pair, 'dp', moves)]
    ppermute x6 -> x3, starting transfers between devices: 14.3 us -> 6.5 us  [spread_sum(): parts.append(lax.ppermute(pair, 'dp', [(d, d ^ step) for d in range(size)]))]
    all_to_all x2, waiting for transfers between devices: 18.8 us -> 22.8 us  [body(): lax.all_to_all(grads, 'seq', split_axis=0, concat_axis=0, tiled=True)]
    all_to_all x2, waiting for transfers between devices: 18.7 us -> 21.2 us  [body(): lax.all_to_all(packed, 'seq', split_axis=0, concat_axis=0, tiled=True)]
where the time goes in v8:
time: 140 us; the launch traced here: 139 us
  waiting for transfers between devices  64.8 us (46%)
  starting transfers between devices  41.8 us (30%)
  Pallas kernels  28.6 us (20%)
  local copies, waits for them, and re-layouts  3.05 us (2%)
    all_to_all x2, waiting for transfers between devices, body(): lax.all_to_all(grads, 'seq', split_axis=0, concat_axis=0, tiled=True)  22.8 us
    all_to_all x2, waiting for transfers between devices, body(): lax.all_to_all(packed, 'seq', split_axis=0, concat_axis=0, tiled=True)  21.2 us
    pallas_call x2, Pallas kernels, attend(): pl.pallas_call(_attend_kernel, in_specs=[pl.BlockSpec(memory_space=pltpu....  20.8 us
    ppermute x2, waiting for transfers between devices, shared_sum(): part = lax.ppermute(pair, 'dp', moves)  18.6 us
    all_to_all x2, starting transfers between devices, body(): lax.all_to_all(packed, 'seq', split_axis=0, concat_axis=0, tiled=True)  16.4 us
    all_to_all x2, starting transfers between devices, body(): lax.all_to_all(grads, 'seq', split_axis=0, concat_axis=0, tiled=True)  10.1 us
    ppermute x2, starting transfers between devices, shared_sum(): part = lax.ppermute(pair, 'dp', moves)  8.78 us
    ppermute x3, starting transfers between devices, spread_sum(): parts.append(lax.ppermute(pair, 'dp', [(d, d ^ step) for d in range(size)]))  6.5 us
  transfers between devices with their start and end apart: 12, of which 7 were waited for; matrix products, arithmetic and copies ran while one was open for 0% of the time, Pallas kernels for 19%

profile of v8, /device:TPU:8, one launch (start us, length us, event | category | flops | bytes accessed | tf_op | source)
XLA Modules:
  0.0 139.3 jit_solution(2858982076694866944)
XLA Ops:
  0.6 2.6 %pack.3 = bf16[32,4,64,128]{3,2,1,0:T(8,128)(2,1)} custom-call(bf16[2,64,4096]{2,1,0:T(8,128)(2,1)} %refs_0_.3, bf16[2,64,4096]{2,1,0:T(8,128)(2,1)} %refs_1_.3, bf16[2,64,4096]{2,1,0:T(8,128)(2,1)} %refs_2_.3, bf16[2,64,4096]{2,1,0:T(8,128)(2,1)} %refs_3_.3), custom_call_target="tpu_custom_call" | custom-call | bytes 4194304 | tf_op jit(solution)/shard_map/pack/pallas_call | solution.py:49
  3.3 8.9 %all-to-all-start.1 = ((bf16[32,4,64,128]{3,2,1,0:T(8,128)(2,1)}), bf16[32,4,64,128]{3,2,1,0:T(8,128)(2,1)S(1)}, u32[]{:S(2)}, u32[]{:S(2)}) async-start(bf16[32,4,64,128]{3,2,1,0:T(8,128)(2,1)} %pack.3), calls=%async_computation.1 | async-start | bytes 4194304 | tf_op jit(solution)/shard_map/all_to_all | solution.py:261
  12.3 2.7 %pack.2 = bf16[32,4,64,128]{3,2,1,0:T(8,128)(2,1)} custom-call(bf16[2,64,4096]{2,1,0:T(8,128)(2,1)} %refs_0_.3, bf16[2,64,4096]{2,1,0:T(8,128)(2,1)} %refs_1_.3, bf16[2,64,4096]{2,1,0:T(8,128)(2,1)} %refs_2_.3, bf16[2,64,4096]{2,1,0:T(8,128)(2,1)} %refs_3_.3), custom_call_target="tpu_custom_call" | custom-call | bytes 4194304 | tf_op jit(solution)/shard_map/pack/pallas_call | solution.py:49
  15.1 3.3 %collective-permute-start.1 = (bf16[8,16]{1,0:T(8,128)(2,1)S(1)}, bf16[8,16]{1,0:T(8,128)(2,1)S(1)}, u32[]{:S(2)}, u32[]{:S(2)}) collective-permute-start(bf16[8,16]{1,0:T(8,128)(2,1)S(1)} %fusion), channel_id=1, source_target_pairs={{0,2},{2,0},{4,6},{6,4},{1,5},{3,7},{5,1},{7,3},{8,10},{10,8},{12,... | collective-permute-start | bytes 776 | tf_op jit(solution)/shard_map/ppermute | solution.py:239
  18.4 5.5 %collective-permute-start.2 = (bf16[8,16]{1,0:T(8,128)(2,1)S(1)}, bf16[8,16]{1,0:T(8,128)(2,1)S(1)}, u32[]{:S(2)}, u32[]{:S(2)}) collective-permute-start(bf16[8,16]{1,0:T(8,128)(2,1)S(1)} %fusion), channel_id=1, source_target_pairs={{0,6},{2,4},{4,2},{6,0},{8,14},{10,12},{12,10},{14,8},{16,22},{18,... | collective-permute-start | bytes 776 | tf_op jit(solution)/shard_map/ppermute | solution.py:239
  23.9 12.8 %collective-permute-done.1 = bf16[8,16]{1,0:T(8,128)(2,1)S(1)} collective-permute-done((bf16[8,16]{1,0:T(8,128)(2,1)S(1)}, bf16[8,16]{1,0:T(8,128)(2,1)S(1)}, u32[]{:S(2)}, u32[]{:S(2)}) %collective-permute-start.1) | collective-permute-done | bytes 288 | tf_op jit(solution)/shard_map/ppermute | solution.py:239
  36.6 5.8 %collective-permute-done.2 = bf16[8,16]{1,0:T(8,128)(2,1)S(1)} collective-permute-done((bf16[8,16]{1,0:T(8,128)(2,1)S(1)}, bf16[8,16]{1,0:T(8,128)(2,1)S(1)}, u32[]{:S(2)}, u32[]{:S(2)}) %collective-permute-start.2) | collective-permute-done | bytes 288 | tf_op jit(solution)/shard_map/ppermute | solution.py:239
  42.4 1.2 collective-permute-done.3
  43.7 7.5 %all-to-all-start = ((bf16[32,4,64,128]{3,2,1,0:T(8,128)(2,1)}), bf16[32,4,64,128]{3,2,1,0:T(8,128)(2,1)}, u32[]{:S(2)}, u32[]{:S(2)}) async-start(bf16[32,4,64,128]{3,2,1,0:T(8,128)(2,1)} %pack.2), calls=%async_computation | async-start | bytes 4194304 | tf_op jit(solution)/shard_map/all_to_all | solution.py:261
  51.2 9.6 %attend.2 = (bf16[32,3,64,128]{3,2,1,0:T(8,128)(2,1)S(1)}, f32[8,128]{1,0:T(8,128)S(1)}) custom-call(bf16[32,4,64,128]{3,2,1,0:T(8,128)(2,1)S(1)} %all-to-all-done.1.x_ref, f32[1,128]{1,0:T(1,128)S(1)} %reshape.21.bias_ref, f32[8,128]{1,0:T(8,128)S(1)} %broadcast_in_dim.18.prior_ref), custom_call_target="tpu_custom_call" | custom-call | flops 6039797760 | bytes 3670016 | tf_op jit(solution)/shard_map/attend/pallas_call | solution.py:198
  60.8 1.2 copy-done.1
  62.0 21.2 %all-to-all-done.x_ref = bf16[32,4,64,128]{3,2,1,0:T(8,128)(2,1)} async-done(((bf16[32,4,64,128]{3,2,1,0:T(8,128)(2,1)}), bf16[32,4,64,128]{3,2,1,0:T(8,128)(2,1)}, u32[]{:S(2)}, u32[]{:S(2)}) %all-to-all-start) | async-done | bytes 2097184 | tf_op jit(solution)/shard_map/all_to_all | solution.py:261
  83.1 5.7 %all-to-all-start.3 = ((bf16[32,3,64,128]{3,2,1,0:T(8,128)(2,1)}), bf16[32,3,64,128]{3,2,1,0:T(8,128)(2,1)S(1)}, u32[]{:S(2)}, u32[]{:S(2)}) async-start(bf16[32,3,64,128]{3,2,1,0:T(8,128)(2,1)} %copy-done.1), calls=%async_computation.3 | async-start | bytes 3145728 | tf_op jit(solution)/shard_map/all_to_all | solution.py:263
  88.8 11.2 %attend.3 = (bf16[32,3,64,128]{3,2,1,0:T(8,128)(2,1)S(1)}, f32[8,128]{1,0:T(8,128)S(1)}) custom-call(bf16[32,4,64,128]{3,2,1,0:T(8,128)(2,1)} %all-to-all-done.x_ref, f32[1,128]{1,0:T(1,128)S(1)} %reshape.21.bias_ref, f32[8,128]{1,0:T(8,128)S(1)} %get-tuple-element.26.prior_ref), custom_call_target="tpu_custom_call" | custom-call | flops 6039797760 | bytes 3670016 | tf_op jit(solution)/shard_map/attend/pallas_call | solution.py:198
  100.0 1.2 copy-done
  101.2 11.7 %all-to-all-done.3.refs_0_ = bf16[32,3,64,128]{3,2,1,0:T(8,128)(2,1)S(1)} async-done(((bf16[32,3,64,128]{3,2,1,0:T(8,128)(2,1)}), bf16[32,3,64,128]{3,2,1,0:T(8,128)(2,1)S(1)}, u32[]{:S(2)}, u32[]{:S(2)}) %all-to-all-start.3) | async-done | bytes 1572896 | tf_op jit(solution)/shard_map/all_to_all | solution.py:263
  112.8 4.4 %all-to-all-start.2 = ((bf16[32,3,64,128]{3,2,1,0:T(8,128)(2,1)}), bf16[32,3,64,128]{3,2,1,0:T(8,128)(2,1)S(1)}, u32[]{:S(2)}, u32[]{:S(2)}) async-start(bf16[32,3,64,128]{3,2,1,0:T(8,128)(2,1)} %copy-done), calls=%async_computation.2 | async-start | bytes 3145728 | tf_op jit(solution)/shard_map/all_to_all | solution.py:263
  117.3 1.3 unpack.2
  118.7 1.2 collective-permute-done.4
  119.8 0.2 collective-permute-start.5
  120.1 6.3 %collective-permute-start.7 = (f32[8,16]{1,0:T(8,128)S(1)}, f32[8,16]{1,0:T(8,128)S(1)}, u32[]{:S(2)}, u32[]{:S(2)}) collective-permute-start(f32[8,16]{1,0:T(8,128)S(1)} %add.32), channel_id=1, source_target_pairs={{0,6},{1,7},{2,4},{3,5},{4,2},{5,3},{6,0},{7,1},{8,14},{9,15},{10,... | collective-permute-start | bytes 1544 | tf_op jit(solution)/shard_map/ppermute | solution.py:226
  126.3 11.1 %all-to-all-done.2.refs_0_ = bf16[32,3,64,128]{3,2,1,0:T(8,128)(2,1)S(1)} async-done(((bf16[32,3,64,128]{3,2,1,0:T(8,128)(2,1)}), bf16[32,3,64,128]{3,2,1,0:T(8,128)(2,1)S(1)}, u32[]{:S(2)}, u32[]{:S(2)}) %all-to-all-start.2) | async-done | bytes 1572896 | tf_op jit(solution)/shard_map/all_to_all | solution.py:263
  137.4 1.3 unpack.3
  138.8 0.5 dynamic-slice_bitcast_fusion
  (24 shorter events, 0.5 us)
Async XLA Ops:
  3.3 8.9 %copy-start.2 = (bf16[16]{0:T(256)(128)(2,1)S(1)}, bf16[16]{0:T(256)(128)(2,1)}, u32[]{:S(2)}) copy-start(bf16[16]{0:T(256)(128)(2,1)} %param.9) | copy-start | bytes 100
  3.3 40.4 %all-to-all-start.1 = ((bf16[32,4,64,128]{3,2,1,0:T(8,128)(2,1)}), bf16[32,4,64,128]{3,2,1,0:T(8,128)(2,1)S(1)}, u32[]{:S(2)}, u32[]{:S(2)}) async-start(bf16[32,4,64,128]{3,2,1,0:T(8,128)(2,1)} %pack.3), calls=%async_computation.1 | async-start | bytes 4194304 | tf_op jit(solution)/shard_map/all_to_all | solution.py:261
  12.3 2.7 %collective-permute-start = (bf16[8,16]{1,0:T(8,128)(2,1)S(1)}, bf16[8,16]{1,0:T(8,128)(2,1)S(1)}, u32[]{:S(2)}, u32[]{:S(2)}) collective-permute-start(bf16[8,16]{1,0:T(8,128)(2,1)S(1)} %broadcast_select_fusion), channel_id=1, source_target_pairs={{0,1},{1,0},{2,3},{3,2},{4,5},{5,4},{6,7},{7,6},{8,9},{9,8},{10,11... | collective-permute-start | bytes 776 | tf_op jit(solution)/shard_map/ppermute | solution.py:232
  15.1 21.5 %collective-permute-start.1 = (bf16[8,16]{1,0:T(8,128)(2,1)S(1)}, bf16[8,16]{1,0:T(8,128)(2,1)S(1)}, u32[]{:S(2)}, u32[]{:S(2)}) collective-permute-start(bf16[8,16]{1,0:T(8,128)(2,1)S(1)} %fusion), channel_id=1, source_target_pairs={{0,2},{2,0},{4,6},{6,4},{1,5},{3,7},{5,1},{7,3},{8,10},{10,8},{12,... | collective-permute-start | bytes 776 | tf_op jit(solution)/shard_map/ppermute | solution.py:239
  18.4 24.0 %collective-permute-start.2 = (bf16[8,16]{1,0:T(8,128)(2,1)S(1)}, bf16[8,16]{1,0:T(8,128)(2,1)S(1)}, u32[]{:S(2)}, u32[]{:S(2)}) collective-permute-start(bf16[8,16]{1,0:T(8,128)(2,1)S(1)} %fusion), channel_id=1, source_target_pairs={{0,6},{2,4},{4,2},{6,0},{8,14},{10,12},{12,10},{14,8},{16,22},{18,... | collective-permute-start | bytes 776 | tf_op jit(solution)/shard_map/ppermute | solution.py:239
  42.4 1.2 collective-permute-start.3
  43.7 39.4 %all-to-all-start = ((bf16[32,4,64,128]{3,2,1,0:T(8,128)(2,1)}), bf16[32,4,64,128]{3,2,1,0:T(8,128)(2,1)}, u32[]{:S(2)}, u32[]{:S(2)}) async-start(bf16[32,4,64,128]{3,2,1,0:T(8,128)(2,1)} %pack.2), calls=%async_computation | async-start | bytes 4194304 | tf_op jit(solution)/shard_map/all_to_all | solution.py:261
  60.8 1.2 copy-start.1
  83.1 29.7 %all-to-all-start.3 = ((bf16[32,3,64,128]{3,2,1,0:T(8,128)(2,1)}), bf16[32,3,64,128]{3,2,1,0:T(8,128)(2,1)S(1)}, u32[]{:S(2)}, u32[]{:S(2)}) async-start(bf16[32,3,64,128]{3,2,1,0:T(8,128)(2,1)} %copy-done.1), calls=%async_computation.3 | async-start | bytes 3145728 | tf_op jit(solution)/shard_map/all_to_all | solution.py:263
  100.0 1.2 copy-start
  112.8 24.6 %all-to-all-start.2 = ((bf16[32,3,64,128]{3,2,1,0:T(8,128)(2,1)}), bf16[32,3,64,128]{3,2,1,0:T(8,128)(2,1)S(1)}, u32[]{:S(2)}, u32[]{:S(2)}) async-start(bf16[32,3,64,128]{3,2,1,0:T(8,128)(2,1)} %copy-done), calls=%async_computation.2 | async-start | bytes 3145728 | tf_op jit(solution)/shard_map/all_to_all | solution.py:263
  118.7 1.2 collective-permute-start.4
  119.8 18.9 %collective-permute-start.5 = (f32[8,16]{1,0:T(8,128)S(1)}, f32[8,16]{1,0:T(8,128)S(1)}, u32[]{:S(2)}, u32[]{:S(2)}) collective-permute-start(f32[8,16]{1,0:T(8,128)S(1)} %add.32), channel_id=1, source_target_pairs={{0,2},{1,3},{2,0},{3,1},{4,6},{5,7},{6,4},{7,5},{8,10},{9,11},{10,... | collective-permute-start | bytes 1544 | tf_op jit(solution)/shard_map/ppermute | solution.py:226
  120.0 18.7 %collective-permute-start.6 = (f32[8,16]{1,0:T(8,128)S(1)}, f32[8,16]{1,0:T(8,128)S(1)}, u32[]{:S(2)}, u32[]{:S(2)}) collective-permute-start(f32[8,16]{1,0:T(8,128)S(1)} %add.32), channel_id=1, source_target_pairs={{0,4},{1,5},{2,6},{3,7},{4,0},{5,1},{6,2},{7,3},{8,12},{9,13},{10,... | collective-permute-start | bytes 1544 | tf_op jit(solution)/shard_map/ppermute | solution.py:226
  120.1 18.7 %collective-permute-start.7 = (f32[8,16]{1,0:T(8,128)S(1)}, f32[8,16]{1,0:T(8,128)S(1)}, u32[]{:S(2)}, u32[]{:S(2)}) collective-permute-start(f32[8,16]{1,0:T(8,128)S(1)} %add.32), channel_id=1, source_target_pairs={{0,6},{1,7},{2,4},{3,5},{4,2},{5,3},{6,0},{7,1},{8,14},{9,15},{10,... | collective-permute-start | bytes 1544 | tf_op jit(solution)/shard_map/ppermute | solution.py:226
